TPU v7x, 32 devices: a whole 2x2x4 slice. The times are simulated.
32 devices in a mesh: wide: 8 (over z, x), tensor: 4 (over y, core).
Axes of the slice: x: 2, y: 2, z: 4, core: 2. Of those that a mesh axis runs over, the one named last changes fastest.
Arguments:
- tokens: bfloat16 [2, 12544, 768], P(None, ('wide', 'tensor')), may hold values from -6 to 6
- cotangent: bfloat16 [2, 12544, 768], P(None, ('wide', 'tensor')), may hold values from -6 to 6
- ln_gain: bfloat16 [3, 768], P(None, 'wide'), may hold values from 0.25 to 1.75
- biases: bfloat16 [10, 768], P(None, 'wide'), may hold values from -1.1953125 to 1.1953125
- fc1_bias: bfloat16 [3072], P('wide'), may hold values from -1.1953125 to 1.1953125
- w_qkv_s: bfloat16 [3, 768, 768], P(None, 'wide', 'tensor'), may hold values from -0.21875 to 0.21875
- w_out_s: bfloat16 [768, 768], P('tensor', 'wide'), may hold values from -2.5 to 2.5
- w_qkv_t: bfloat16 [3, 768, 768], P(None, 'wide', 'tensor'), may hold values from -0.21875 to 0.21875
- w_out_t: bfloat16 [768, 768], P('tensor', 'wide'), may hold values from -0.625 to 0.625
- w_up: bfloat16 [768, 3072], P('wide', 'tensor'), may hold values from -0.21875 to 0.21875
- w_down: bfloat16 [3072, 768], P('tensor', 'wide'), may hold values from -0.109375 to 0.109375
Outputs:
- mixed: bfloat16 [2, 12544, 768], P(None, ('wide', 'tensor'))
- grad_tokens: float32 [2, 12544, 768], P(None, ('wide', 'tensor'))
- grad_ln_gain: float32 [3, 768], P(None, 'wide')
- grad_biases: float32 [10, 768], P(None, 'wide')
- grad_fc1_bias: float32 [3072], P('wide')
- grad_w_qkv_s: float32 [3, 768, 768], P(None, 'wide', 'tensor')
- grad_w_out_s: float32 [768, 768], P('tensor', 'wide')
- grad_w_qkv_t: float32 [3, 768, 768], P(None, 'wide', 'tensor')
- grad_w_out_t: float32 [768, 768], P('tensor', 'wide')
- grad_w_up: float32 [768, 3072], P('wide', 'tensor')
- grad_w_down: float32 [3072, 768], P('tensor', 'wide')
All inputs are finite; a program needn't handle non-finite values.
Results may differ from a plain program's by a relative error of at most 0.014.
Values may be sent and summed in bfloat16 or wider, within the bound.
No kernel may reach another device: no remote copies, remote signals or barrier semaphores. Data moves between devices by JAX's collectives and lax.ppermute only.
A program may use at most 256 MiB of HBM per device.

v0:
```python
import jax
import jax.numpy as jnp
from jax import lax
from jax.sharding import PartitionSpec as P

HEAD_DIM = 64
PATCHES = 196
FRAMES = 16
FRAME_RUN = 2


EPSILON = 1e-06


def layer_norm(rows, gain, shift):
    center = rows - jnp.mean(rows, axis=-1, keepdims=True)
    spread = jnp.mean(center * center, axis=-1, keepdims=True)
    return center * lax.rsqrt(spread + EPSILON) * gain + shift


def exact_gelu(values):
    return jax.nn.gelu(values, approximate=False)


def norm_back(rows_in, gain, shift, grad_rows):
    _, pullback = jax.vjp(layer_norm, rows_in, gain, shift)
    return pullback(grad_rows)


def into_time(block, clip_count):
    rest = block.shape[1:]
    grouped = block.reshape((FRAMES // FRAME_RUN, clip_count, FRAME_RUN) + rest)
    return jnp.swapaxes(grouped, 1, 2).reshape((FRAMES, clip_count) + rest)


def out_of_time(block):
    clip_count = block.shape[1]
    rest = block.shape[2:]
    grouped = block.reshape((FRAMES // FRAME_RUN, FRAME_RUN, clip_count) + rest)
    return jnp.swapaxes(grouped, 1, 2).reshape((FRAMES * clip_count,) + rest)


def attend(queries, key_rows, value_rows, einsum_forms):
    score_form, out_form, key_form = einsum_forms
    score_scale = queries.shape[-1] ** (-0.5)
    scores = (
        jnp.einsum(score_form, queries, key_rows, preferred_element_type=jnp.float32) * score_scale
    )
    log_total = jax.nn.logsumexp(scores, axis=-1, keepdims=True)
    weights = jnp.exp(scores - log_total).astype(jnp.bfloat16)
    result = jnp.einsum(out_form, weights, value_rows, preferred_element_type=jnp.float32)
    return (result.astype(jnp.bfloat16), log_total)


def attend_back(queries, key_rows, value_rows, log_total, grad_out, einsum_forms):
    score_form, out_form, key_form = einsum_forms
    score_scale = queries.shape[-1] ** (-0.5)
    scores = (
        jnp.einsum(score_form, queries, key_rows, preferred_element_type=jnp.float32) * score_scale
    )
    probabilities = jnp.exp(scores - log_total)
    grad_probs = jnp.einsum(score_form, grad_out, value_rows, preferred_element_type=jnp.float32)
    row_inner = jnp.sum(probabilities * grad_probs, axis=-1, keepdims=True)
    grad_scores = (probabilities * (grad_probs - row_inner)).astype(jnp.bfloat16)
    grad_q = (
        jnp.einsum(out_form, grad_scores, key_rows, preferred_element_type=jnp.float32)
        * score_scale
    ).astype(jnp.bfloat16)
    grad_k = (
        jnp.einsum(key_form, grad_scores, queries, preferred_element_type=jnp.float32) * score_scale
    ).astype(jnp.bfloat16)
    grad_v = jnp.einsum(
        key_form, probabilities.astype(jnp.bfloat16), grad_out, preferred_element_type=jnp.float32
    ).astype(jnp.bfloat16)
    return (grad_q, grad_k, grad_v)


def product_term(einsum_form, left, right):

    def term(first_row, row_span):
        return jnp.einsum(einsum_form, left, right, preferred_element_type=jnp.float32)

    return term


def gather_rows(block):
    return lax.all_gather(block, "tensor", axis=0, tiled=True)


def sum_rows(term, row_count):
    return lax.psum_scatter(
        term(jnp.int32(0), row_count * lax.axis_size("tensor")),
        "tensor",
        scatter_dimension=0,
        tiled=True,
    )


def out_project(attn_rows, w_out_piece, row_count):
    return sum_rows(product_term("gc,cd->gd", attn_rows, w_out_piece), row_count)


def to_patches(block, patch_pad):
    padded = jnp.pad(block, ((0, 0), (0, patch_pad - block.shape[1]), (0, 0)))
    return lax.all_to_all(padded, "wide", split_axis=1, concat_axis=0, tiled=True)


def to_frames(block, patch_count):
    returned = lax.all_to_all(block, "wide", split_axis=0, concat_axis=1, tiled=True)
    return returned[:, :patch_count]


def reduce_wide(packed):
    return (
        lax.psum_scatter(packed[0], "wide", scatter_dimension=1, tiled=True),
        lax.psum_scatter(packed[1], "wide", scatter_dimension=1, tiled=True),
        lax.psum_scatter(packed[2], "wide", scatter_dimension=1, tiled=True),
        lax.psum_scatter(packed[3], "wide", scatter_dimension=1, tiled=True),
        lax.psum_scatter(packed[4], "wide", scatter_dimension=0, tiled=True),
        lax.psum_scatter(packed[5], "wide", scatter_dimension=1, tiled=True),
        lax.psum_scatter(packed[6], "wide", scatter_dimension=1, tiled=True),
        lax.psum_scatter(packed[7], "wide", scatter_dimension=1, tiled=True),
        lax.psum_scatter(packed[8], "wide", scatter_dimension=0, tiled=True),
    )


def per_device(
    tokens, cotangent, ln_gain, biases, fc1_bias, w_qkv_s, w_out_s, w_qkv_t, w_out_t, w_up, w_down
):
    wide_count = lax.axis_size("wide")
    tensor_count = lax.axis_size("tensor")
    tensor_rank = lax.axis_index("tensor")
    micro_total = tokens.shape[0]
    row_count = tokens.shape[1]
    model_width = tokens.shape[2]
    head_cols = w_qkv_s.shape[2]
    hidden = w_up.shape[1]
    local_heads = head_cols // HEAD_DIM
    frames = row_count * tensor_count // PATCHES
    patch_slot = (PATCHES + wide_count - 1) // wide_count
    patch_pad = patch_slot * wide_count
    clip_count = frames * wide_count // FRAMES
    spatial_forms = ("fphe,fqhe->fhpq", "fhpq,fqhe->fphe", "fhpq,fphe->fqhe")
    temporal_forms = ("tcphe,ucphe->cphtu", "cphtu,ucphe->tcphe", "cphtu,tcphe->ucphe")

    def fetch_all():
        return (
            lax.all_gather(w_qkv_s, "wide", axis=1, tiled=True),
            lax.all_gather(w_out_s, "wide", axis=1, tiled=True),
            lax.all_gather(w_qkv_t, "wide", axis=1, tiled=True),
            lax.all_gather(w_out_t, "wide", axis=1, tiled=True),
            lax.all_gather(w_up, "wide", axis=0, tiled=True),
            lax.all_gather(w_down, "wide", axis=1, tiled=True),
            lax.all_gather(ln_gain, "wide", axis=1, tiled=True),
            lax.all_gather(biases, "wide", axis=1, tiled=True),
            lax.all_gather(fc1_bias, "wide", axis=0, tiled=True),
        )

    shares = None
    sums = [
        jnp.zeros((3, model_width, head_cols), jnp.float32),
        jnp.zeros((head_cols, model_width), jnp.float32),
        jnp.zeros((3, model_width, head_cols), jnp.float32),
        jnp.zeros((head_cols, model_width), jnp.float32),
        jnp.zeros((model_width, hidden), jnp.float32),
        jnp.zeros((hidden, model_width), jnp.float32),
        jnp.zeros((3, model_width), jnp.float32),
        jnp.zeros((10, model_width), jnp.float32),
        jnp.zeros((3, head_cols), jnp.float32),
        jnp.zeros((3, head_cols), jnp.float32),
        jnp.zeros((hidden,), jnp.float32),
    ]
    outputs = []
    input_grads = []
    for micro_index in range(micro_total):
        fetched = fetch_all()
        gains = fetched[6].astype(jnp.float32)
        shifts = fetched[7].astype(jnp.float32)
        offset = tensor_rank * head_cols
        empty_cols = jnp.zeros((head_cols,), jnp.float32)
        bias_s = jnp.stack(
            [
                lax.dynamic_slice_in_dim(shifts[3], offset, head_cols),
                empty_cols,
                lax.dynamic_slice_in_dim(shifts[4], offset, head_cols),
            ]
        )
        bias_t = jnp.stack(
            [
                lax.dynamic_slice_in_dim(shifts[6], offset, head_cols),
                empty_cols,
                lax.dynamic_slice_in_dim(shifts[7], offset, head_cols),
            ]
        )
        up_bias = lax.dynamic_slice_in_dim(
            fetched[8].astype(jnp.float32), tensor_rank * hidden, hidden
        )
        gains, shifts, bias_s, bias_t, up_bias = (gains, shifts, bias_s, bias_t, up_bias)
        source = tokens[micro_index].astype(jnp.float32)
        norm_s = layer_norm(source, gains[0], shifts[0]).astype(jnp.bfloat16)
        full_s = gather_rows(norm_s)
        qkv_s = (
            jnp.einsum("gd,kdc->gkc", full_s, fetched[0], preferred_element_type=jnp.float32)
            + bias_s
        ).astype(jnp.bfloat16)
        split_s = qkv_s.reshape(frames, PATCHES, 3, local_heads, HEAD_DIM)
        attn_s, total_s = attend(
            split_s[:, :, 0], split_s[:, :, 1], split_s[:, :, 2], spatial_forms
        )
        attn_s = attn_s.reshape(-1, head_cols)
        resid_s = source + out_project(attn_s, fetched[1], row_count) + shifts[5]
        norm_t = layer_norm(resid_s, gains[1], shifts[1]).astype(jnp.bfloat16)
        full_t = gather_rows(norm_t)
        qkv_t = (
            jnp.einsum("gd,kdc->gkc", full_t, fetched[2], preferred_element_type=jnp.float32)
            + bias_t
        ).astype(jnp.bfloat16)
        moved = to_patches(qkv_t.reshape(frames, PATCHES, 3 * head_cols), patch_pad)
        split_t = into_time(moved, clip_count).reshape(
            FRAMES, clip_count, patch_slot, 3, local_heads, HEAD_DIM
        )
        attn_t, total_t = attend(
            split_t[:, :, :, 0], split_t[:, :, :, 1], split_t[:, :, :, 2], temporal_forms
        )
        attn_t = out_of_time(attn_t).reshape(wide_count * frames, patch_slot, head_cols)
        attn_t = to_frames(attn_t, PATCHES).reshape(-1, head_cols)
        resid_t = resid_s + out_project(attn_t, fetched[3], row_count) + shifts[8]
        norm_m = layer_norm(resid_t, gains[2], shifts[2]).astype(jnp.bfloat16)
        full_m = gather_rows(norm_m)
        pre_act = jnp.dot(full_m, fetched[4], preferred_element_type=jnp.float32) + up_bias
        activ = exact_gelu(pre_act).astype(jnp.bfloat16)
        mixed_rows = (
            resid_t + sum_rows(product_term("gf,fd->gd", activ, fetched[5]), row_count) + shifts[9]
        )
        outputs.append(mixed_rows.astype(jnp.bfloat16))
        fetched = fetch_all()
        grad_out = cotangent[micro_index].astype(jnp.float32)
        sums[7] = sums[7].at[9].add(jnp.sum(grad_out, axis=0))
        grad_branch = gather_rows(grad_out.astype(jnp.bfloat16))
        sums[5] = sums[5] + jnp.einsum(
            "gf,gd->fd", activ, grad_branch, preferred_element_type=jnp.float32
        )
        grad_act = jnp.einsum(
            "gd,fd->gf", grad_branch, fetched[5], preferred_element_type=jnp.float32
        )
        _, gelu_pull = jax.vjp(exact_gelu, pre_act)
        grad_pre = gelu_pull(grad_act)[0].astype(jnp.bfloat16)
        sums[4] = sums[4] + jnp.einsum(
            "gd,gf->df", full_m, grad_pre, preferred_element_type=jnp.float32
        )
        sums[10] = sums[10] + jnp.sum(grad_pre, axis=0, dtype=jnp.float32)
        grad_norm = sum_rows(product_term("gf,df->gd", grad_pre, fetched[4]), row_count)
        back_in, back_gain, back_shift = norm_back(resid_t, gains[2], shifts[2], grad_norm)
        sums[6] = sums[6].at[2].add(back_gain)
        sums[7] = sums[7].at[2].add(back_shift)
        grad_resid = grad_out + back_in
        sums[7] = sums[7].at[8].add(jnp.sum(grad_resid, axis=0))
        grad_branch = gather_rows(grad_resid.astype(jnp.bfloat16))
        sums[3] = sums[3] + jnp.einsum(
            "gc,gd->cd", attn_t, grad_branch, preferred_element_type=jnp.float32
        )
        grad_attn = jnp.einsum(
            "gd,cd->gc", grad_branch, fetched[3], preferred_element_type=jnp.float32
        ).astype(jnp.bfloat16)
        grad_moved = to_patches(grad_attn.reshape(frames, PATCHES, head_cols), patch_pad)
        grad_moved = into_time(grad_moved, clip_count).reshape(
            FRAMES, clip_count, patch_slot, local_heads, HEAD_DIM
        )
        grad_q, grad_k, grad_v = attend_back(
            split_t[:, :, :, 0],
            split_t[:, :, :, 1],
            split_t[:, :, :, 2],
            total_t,
            grad_moved,
            temporal_forms,
        )
        grad_qkv = out_of_time(jnp.stack([grad_q, grad_k, grad_v], axis=3)).reshape(
            wide_count * frames, patch_slot, 3 * head_cols
        )
        grad_qkv = to_frames(grad_qkv, PATCHES).reshape(-1, 3, head_cols)
        sums[2] = sums[2] + jnp.einsum(
            "gd,gkc->kdc", full_t, grad_qkv, preferred_element_type=jnp.float32
        )
        sums[9] = sums[9] + jnp.sum(grad_qkv, axis=0, dtype=jnp.float32)
        grad_norm = sum_rows(product_term("gkc,kdc->gd", grad_qkv, fetched[2]), row_count)
        back_in, back_gain, back_shift = norm_back(resid_s, gains[1], shifts[1], grad_norm)
        sums[6] = sums[6].at[1].add(back_gain)
        sums[7] = sums[7].at[1].add(back_shift)
        grad_resid = grad_resid + back_in
        sums[7] = sums[7].at[5].add(jnp.sum(grad_resid, axis=0))
        grad_branch = gather_rows(grad_resid.astype(jnp.bfloat16))
        sums[1] = sums[1] + jnp.einsum(
            "gc,gd->cd", attn_s, grad_branch, preferred_element_type=jnp.float32
        )
        grad_attn = jnp.einsum(
            "gd,cd->gc", grad_branch, fetched[1], preferred_element_type=jnp.float32
        ).astype(jnp.bfloat16)
        grad_heads = grad_attn.reshape(frames, PATCHES, local_heads, HEAD_DIM)
        grad_q, grad_k, grad_v = attend_back(
            split_s[:, :, 0], split_s[:, :, 1], split_s[:, :, 2], total_s, grad_heads, spatial_forms
        )
        grad_qkv = jnp.stack([grad_q, grad_k, grad_v], axis=2).reshape(-1, 3, head_cols)
        sums[0] = sums[0] + jnp.einsum(
            "gd,gkc->kdc", full_s, grad_qkv, preferred_element_type=jnp.float32
        )
        sums[8] = sums[8] + jnp.sum(grad_qkv, axis=0, dtype=jnp.float32)
        grad_norm = sum_rows(product_term("gkc,kdc->gd", grad_qkv, fetched[0]), row_count)
        back_in, back_gain, back_shift = norm_back(source, gains[0], shifts[0], grad_norm)
        sums[6] = sums[6].at[0].add(back_gain)
        sums[7] = sums[7].at[0].add(back_shift)
        input_grads.append(grad_resid + back_in)
    columns = jnp.stack([sums[8][0], sums[8][2], sums[9][0], sums[9][2]])
    placed = lax.dynamic_update_slice(
        jnp.zeros((4, model_width), jnp.float32), columns, (0, tensor_rank * head_cols)
    )
    blank = jnp.zeros((1, model_width), jnp.float32)
    shift_full = sums[7] + jnp.concatenate(
        [blank, blank, blank, placed[0:2], blank, placed[2:4], blank, blank], axis=0
    )
    up_full = lax.dynamic_update_slice(
        jnp.zeros((hidden * tensor_count,), jnp.float32), sums[10], (tensor_rank * hidden,)
    )
    shares = reduce_wide(
        (sums[0], sums[1], sums[2], sums[3], sums[4], sums[5], sums[6], shift_full, up_full)
    )
    gain_grad, shift_grad, up_grad = lax.psum((shares[6], shares[7], shares[8]), "tensor")
    return (
        jnp.stack(outputs),
        jnp.stack(input_grads),
        gain_grad,
        shift_grad,
        up_grad,
        shares[0],
        shares[1],
        shares[2],
        shares[3],
        shares[4],
        shares[5],
    )


def solution(mesh):
    return jax.shard_map(
        per_device,
        mesh=mesh,
        in_specs=(
            P(None, ("wide", "tensor"), None),
            P(None, ("wide", "tensor"), None),
            P(None, "wide"),
            P(None, "wide"),
            P("wide"),
            P(None, "wide", "tensor"),
            P("tensor", "wide"),
            P(None, "wide", "tensor"),
            P("tensor", "wide"),
            P("wide", "tensor"),
            P("tensor", "wide"),
        ),
        out_specs=(
            P(None, ("wide", "tensor"), None),
            P(None, ("wide", "tensor"), None),
            P(None, "wide"),
            P(None, "wide"),
            P("wide"),
            P(None, "wide", "tensor"),
            P("tensor", "wide"),
            P(None, "wide", "tensor"),
            P("tensor", "wide"),
            P("wide", "tensor"),
            P("tensor", "wide"),
        ),
        check_vma=False,
    )
```

profile of v0, /device:TPU:0, one launch (start us, length us, event | category | flops | bytes accessed | tf_op | source)
XLA Modules:
  0.0 2080.9 jit_solution(17069805705926739419)
XLA Ops:
  8.1 32.7 %all-gather.3 = bf16[8,96,10]{1,2,0:T(8,128)(2,1)S(1)} all-gather(bf16[1,96,10]{1,2,0:T(8,128)(2,1)} %bitcast.574), channel_id=1, replica_groups=mesh['wide'=8,'tensor'=4] {'wide'}, dimensions={0}, use_global_device_ids=true | all-gather | bytes 17280 | tf_op jit(solution)/shard_map/all_gather | solution.py:155
  45.4 20.5 all-gather.2
  68.6 35.7 %all_gather.87 = bf16[3,768,192]{2,0,1:T(4,128)(2,1)} all-gather(bf16[3,96,192]{2,0,1:T(4,128)(2,1)S(1)} %copy.214), channel_id=1, replica_groups=mesh['wide'=8,'tensor'=4] {'wide'}, dimensions={1}, use_global_device_ids=true | all-gather | bytes 995328 | tf_op jit(solution)/shard_map/all_gather | solution.py:148
  107.2 31.2 %all_gather.88 = bf16[192,768]{0,1:T(8,128)(2,1)S(1)} all-gather(bf16[192,96]{0,1:T(8,128)(2,1)S(1)} %copy.221), channel_id=1, replica_groups=mesh['wide'=8,'tensor'=4] {'wide'}, dimensions={1}, use_global_device_ids=true | all-gather | bytes 331776 | tf_op jit(solution)/shard_map/all_gather | solution.py:149
  138.5 5.5 fusion.154
  150.6 5.8 reshape.812
  167.7 5.9 reshape.806
  185.0 29.6 %reduce-scatter.39.cloned.1.call-done = f32[392,768]{1,0:T(8,128)} async-done(((f32[1568,768]{1,0:T(8,128)}), f32[392,768]{1,0:T(8,128)}) %reduce-scatter.39.cloned.1.call-update) | async-done | bytes 1204240 | tf_op jit(solution)/shard_map/reduce_scatter | solution.py:91
  214.5 51.0 %reduce-scatter.33.cloned.1.call-done = f32[392,768]{1,0:T(8,128)} async-done(((f32[1568,768]{1,0:T(8,128)}), f32[392,768]{1,0:T(8,128)}) %reduce-scatter.33.cloned.1.call-update) | async-done | bytes 1204240 | tf_op jit(solution)/shard_map/reduce_scatter | solution.py:91
  271.9 37.6 %all_gather.90 = bf16[3,768,192]{2,0,1:T(4,128)(2,1)S(1)} all-gather(bf16[3,96,192]{2,0,1:T(4,128)(2,1)S(1)} %copy.222), channel_id=1, replica_groups=mesh['wide'=8,'tensor'=4] {'wide'}, dimensions={1}, use_global_device_ids=true | all-gather | bytes 995328 | tf_op jit(solution)/shard_map/all_gather | solution.py:150
  311.5 5.7 fusion.151
  331.7 6.5 copy.339
  338.4 53.1 %all_to_all.132 = bf16[8,200,576]{2,0,1:T(8,128)(2,1)S(1)} all-to-all(bf16[8,200,576]{2,0,1:T(8,128)(2,1)S(1)} %pad.53.clone), channel_id=1, replica_groups=mesh['wide'=8,'tensor'=4] {'wide'}, dimensions={1} | all-to-all | bytes 3686400 | tf_op jit(solution)/shard_map/all_to_all | solution.py:105
  395.7 6.0 reshape_reshape.26
  417.5 46.3 %all_gather.91 = bf16[192,768]{0,1:T(8,128)(2,1)S(1)} all-gather(bf16[192,96]{0,1:T(8,128)(2,1)S(1)} %copy.234), channel_id=1, replica_groups=mesh['wide'=8,'tensor'=4] {'wide'}, dimensions={1}, use_global_device_ids=true | all-gather | bytes 331776 | tf_op jit(solution)/shard_map/all_gather | solution.py:151
  471.9 5.9 reshape.808
  477.8 5.4 copy.338
  485.0 46.4 %all_to_all.133 = bf16[8,200,576]{2,0,1:T(8,128)(2,1)} all-to-all(bf16[8,200,576]{2,0,1:T(8,128)(2,1)S(1)} %pad.52.clone), channel_id=1, replica_groups=mesh['wide'=8,'tensor'=4] {'wide'}, dimensions={1} | all-to-all | bytes 3686400 | tf_op jit(solution)/shard_map/all_to_all | solution.py:105
  531.4 5.2 reshape.809
  540.2 10.0 reshape_reshape.24
  564.9 27.2 %all_to_all.134 = bf16[64,25,192]{2,1,0:T(8,128)(2,1)S(1)} all-to-all(bf16[64,25,192]{2,1,0:T(8,128)(2,1)S(1)} %copy.231), channel_id=1, replica_groups=mesh['wide'=8,'tensor'=4] {'wide'}, dimensions={0} | all-to-all | bytes 1228800 | tf_op jit(solution)/shard_map/all_to_all | solution.py:109
  602.2 46.2 %reduce-scatter.35.cloned.1.call-done = f32[392,768]{1,0:T(8,128)} async-done(((f32[1568,768]{1,0:T(8,128)}), f32[392,768]{1,0:T(8,128)}) %reduce-scatter.35.cloned.1.call-update) | async-done | bytes 1204240 | tf_op jit(solution)/shard_map/reduce_scatter | solution.py:91
  655.8 26.3 %all-gather.4 = bf16[8,1,384]{2,1,0:T(2,128)(2,1)S(1)} all-gather(bf16[1,1,384]{2,1,0:T(2,128)(2,1)S(1)} %reshape.852), channel_id=1, replica_groups=mesh['wide'=8,'tensor'=4] {'wide'}, dimensions={0}, use_global_device_ids=true | all-gather | bytes 6912 | tf_op jit(solution)/shard_map/all_gather | solution.py:156
  682.2 6.3 fusion.158
  688.5 14.5 all-gather.24.cloned.1.call-done
  703.0 24.7 %multiply_convert_fusion.3 = (bf16[1568,768]{1,0:T(8,128)(2,1)}, f32[1568,768]{1,0:T(8,128)}, bf16[1568,768]{1,0:T(8,128)(2,1)}, f32[1568,768]{1,0:T(8,128)}, f32[1568,768]{1,0:T(8,128)}) fusion(f32[768]{0:T(1024)S(1)} %dynamic_slice.24, f32[1568,768]{1,0:T(8,128)} %fusion.158, bf16[1568,768]{1,0:T(8,128)(2,1)} %all-gather.24.cloned.1.call-done, ...), kind=kOutput, calls=%fused_computation.31 | convolution fusion | flops 2008645632 | bytes 27675648 | tf_op jit(solution)/shard_map/dot_general | solution.py:230
  727.8 18.9 all-gather.28.cloned.1.call-done
  746.7 24.2 %all-gather.46.cloned.1.call-done = bf16[1,1568,768]{2,1,0:T(8,128)(2,1)} async-done(((bf16[1,392,768]{2,1,0:T(8,128)(2,1)}), bf16[1,1568,768]{2,1,0:T(8,128)(2,1)}) %all-gather.46.cloned.1.call-update) | async-done | bytes 2408464 | tf_op jit(solution)/shard_map/all_gather | solution.py:87
  770.9 8.9 convert_reduce_fusion
  785.7 10.9 all-gather.44.cloned.1.call-done
  796.7 8.1 convert_reduce_fusion.1
  810.6 5.9 fusion.153
  816.6 6.0 fusion.159
  822.7 24.8 %reduce-scatter.51.cloned.1.call-done = f32[392,768]{1,0:T(8,128)} async-done(((f32[1568,768]{1,0:T(8,128)}), f32[392,768]{1,0:T(8,128)}) %reduce-scatter.51.cloned.1.call-update) | async-done | bytes 1204240 | tf_op jit(solution)/shard_map/reduce_scatter | solution.py:91
  847.6 50.9 %reduce-scatter.45.cloned.1.call-done = f32[392,768]{1,0:T(8,128)} async-done(((f32[1568,768]{1,0:T(8,128)}), f32[392,768]{1,0:T(8,128)}) %reduce-scatter.45.cloned.1.call-update) | async-done | bytes 1204240 | tf_op jit(solution)/shard_map/reduce_scatter | solution.py:91
  901.1 48.3 %reduce-scatter.37.cloned.1.call-done = f32[392,768]{1,0:T(8,128)} async-done(((f32[1568,768]{1,0:T(8,128)}), f32[392,768]{1,0:T(8,128)}) %reduce-scatter.37.cloned.1.call-update) | async-done | bytes 1204240 | tf_op jit(solution)/shard_map/reduce_scatter | solution.py:91
  949.4 51.1 %reduce-scatter.43.cloned.1.call-done = f32[392,768]{1,0:T(8,128)} async-done(((f32[1568,768]{1,0:T(8,128)}), f32[392,768]{1,0:T(8,128)}) %reduce-scatter.43.cloned.1.call-update) | async-done | bytes 1204240 | tf_op jit(solution)/shard_map/reduce_scatter | solution.py:91
  1007.0 24.5 %all-gather.40.cloned.1.call-done = bf16[1568,768]{1,0:T(8,128)(2,1)} async-done(((bf16[392,768]{1,0:T(8,128)(2,1)}), bf16[1568,768]{1,0:T(8,128)(2,1)}) %all-gather.40.cloned.1.call-update) | async-done | bytes 2408464 | tf_op jit(solution)/shard_map/all_gather | solution.py:87
  1036.7 27.7 %all_to_all.135 = bf16[8,200,192]{2,0,1:T(8,128)(2,1)S(1)} all-to-all(bf16[8,200,192]{2,0,1:T(8,128)(2,1)S(1)} %pad.55), channel_id=1, replica_groups=mesh['wide'=8,'tensor'=4] {'wide'}, dimensions={1} | all-to-all | bytes 1228800 | tf_op jit(solution)/shard_map/all_to_all | solution.py:105
  1083.1 5.6 maximum_bitcast_fusion.1
  1088.7 8.1 reshape_reshape.31
  1103.9 57.9 %all-to-all-done.7 = bf16[64,25,576]{2,1,0:T(8,128)(2,1)S(1)} async-done(((bf16[64,25,576]{2,1,0:T(8,128)(2,1)}), bf16[64,25,576]{2,1,0:T(8,128)(2,1)S(1)}, u32[]{:S(2)}, u32[]{:S(2)}) %all-to-all-start.7) | async-done | bytes 1843232 | tf_op jit(solution)/shard_map/all_to_all | solution.py:109
  1173.2 6.0 convolution_bitcast_fusion.1
  1184.6 25.4 %all_to_all.136 = bf16[8,200,192]{2,0,1:T(8,128)(2,1)S(1)} all-to-all(bf16[8,200,192]{2,0,1:T(8,128)(2,1)S(1)} %pad.54), channel_id=1, replica_groups=mesh['wide'=8,'tensor'=4] {'wide'}, dimensions={1} | all-to-all | bytes 1228800 | tf_op jit(solution)/shard_map/all_to_all | solution.py:105
  1225.2 5.6 maximum_bitcast_fusion
  1230.7 8.1 reshape_reshape.29
  1240.0 62.3 %all_to_all.137 = bf16[64,25,576]{2,1,0:T(8,128)(2,1)S(1)} all-to-all(bf16[64,25,576]{2,1,0:T(8,128)(2,1)S(1)} %copy.260), channel_id=1, replica_groups=mesh['wide'=8,'tensor'=4] {'wide'}, dimensions={0} | all-to-all | bytes 3686400 | tf_op jit(solution)/shard_map/all_to_all | solution.py:109
  1313.7 5.9 convolution_bitcast_fusion.3
  1319.7 46.6 %reduce-scatter.47.cloned.1.call-done = f32[392,768]{1,0:T(8,128)} async-done(((f32[1568,768]{1,0:T(8,128)}), f32[392,768]{1,0:T(8,128)}) %reduce-scatter.47.cloned.1.call-update) | async-done | bytes 1204240 | tf_op jit(solution)/shard_map/reduce_scatter | solution.py:91
  1375.3 23.0 %all-gather.42.cloned.1.call-done = bf16[1568,768]{1,0:T(8,128)(2,1)} async-done(((bf16[392,768]{1,0:T(8,128)(2,1)}), bf16[1568,768]{1,0:T(8,128)(2,1)}) %all-gather.42.cloned.1.call-update) | async-done | bytes 2408464 | tf_op jit(solution)/shard_map/all_gather | solution.py:87
  1475.7 4.8 reshape.881
  1481.2 6.6 fusion.164
  1513.9 13.1 reduce-scatter.49.cloned.1.call-done
  1535.2 7.0 convolution_add_fusion
  1542.4 5.0 fusion.22
  1553.4 37.1 %all-reduce.6 = f32[3072]{0:T(1024)S(1)} all-reduce(f32[3072]{0:T(1024)S(1)} %add_dynamic-update-slice_fusion), channel_id=18, replica_groups=mesh['wide'=8,'tensor'=4] {'wide'}, use_global_device_ids=true, to_apply=%region_76.77.clone | all-reduce | flops 3072 | bytes 24576
  1595.2 68.3 %reduce-scatter.69.cloned.1.call-done = f32[96,576]{1,0:T(8,128)} async-done(((f32[768,576]{1,0:T(8,128)}), f32[96,576]{1,0:T(8,128)}) %reduce-scatter.69.cloned.1.call-update) | async-done | bytes 221200
  1665.4 63.4 %reduce-scatter.67.cloned.1.call-done = f32[96,192]{1,0:T(8,128)} async-done(((f32[768,192]{1,0:T(8,128)}), f32[96,192]{1,0:T(8,128)}) %reduce-scatter.67.cloned.1.call-update) | async-done | bytes 73744
  1730.4 68.4 %reduce-scatter.65.cloned.1.call-done = f32[96,576]{1,0:T(8,128)} async-done(((f32[768,576]{1,0:T(8,128)}), f32[96,576]{1,0:T(8,128)}) %reduce-scatter.65.cloned.1.call-update) | async-done | bytes 221200
  1804.9 58.3 %reduce-scatter.61.cloned.1.call-done = f32[96,3]{1,0:T(8,128)} async-done(((f32[768,3]{1,0:T(8,128)}), f32[96,3]{1,0:T(8,128)}) %reduce-scatter.61.cloned.1.call-update) | async-done | bytes 1168
  1864.0 63.5 %reduce-scatter.63.cloned.1.call-done = f32[96,10]{1,0:T(8,128)} async-done(((f32[768,10]{1,0:T(8,128)}), f32[96,10]{1,0:T(8,128)}) %reduce-scatter.63.cloned.1.call-update) | async-done | bytes 3856
  1928.4 10.7 all-reduce.7
  1939.1 61.1 %reduce-scatter.57.cloned.1.call-done = f32[96,768]{1,0:T(8,128)} async-done(((f32[768,768]{1,0:T(8,128)}), f32[96,768]{1,0:T(8,128)}) %reduce-scatter.57.cloned.1.call-update) | async-done | bytes 294928 | tf_op jit(solution)/shard_map/reduce_scatter | solution.py:119
  2000.2 73.1 %reduce-scatter.59.cloned.1.call-done = f32[768,96]{0,1:T(8,128)} async-done(((f32[768,768]{0,1:T(8,128)}), f32[768,96]{0,1:T(8,128)}) %reduce-scatter.59.cloned.1.call-update) | async-done | bytes 294928 | tf_op jit(solution)/shard_map/reduce_scatter | solution.py:120
  (650 shorter events, 365.3 us)
Async XLA Ops:
  8.0 58.0 %copy-start.6 = (bf16[2,392,768]{2,1,0:T(8,128)(2,1)S(1)}, bf16[2,392,768]{2,1,0:T(8,128)(2,1)}, u32[]{:S(2)}) copy-start(bf16[2,392,768]{2,1,0:T(8,128)(2,1)} %param.47) | copy-start | bytes 3612676
  8.0 37.4 %copy-start.128 = (bf16[3,96]{1,0:T(4,128)(2,1)S(1)}, bf16[3,96]{1,0:T(4,128)(2,1)}, u32[]{:S(2)}) copy-start(bf16[3,96]{1,0:T(4,128)(2,1)} %param.49) | copy-start | bytes 1732
  8.0 130.5 %all-gather.30.cloned.1.call-start = ((), (), s32[]{:S(2)}) async-start(), calls=%async_computation.36 | async-start | bytes 3010560 | tf_op jit(solution)/shard_map/all_gather | solution.py:87
  43.0 25.3 %copy-start.97 = (f32[392]{0:T(512)}, f32[392]{0:T(512)S(1)}, u32[]{:S(2)}) copy-start(f32[392]{0:T(512)S(1)} %get-tuple-element.423) | copy-start | bytes 4708
  43.0 25.3 %copy-start.99 = (f32[392]{0:T(512)}, f32[392]{0:T(512)S(1)}, u32[]{:S(2)}) copy-start(f32[392]{0:T(512)S(1)} %get-tuple-element.424) | copy-start | bytes 4708
  43.0 25.4 %copy-start.93 = (bf16[3,96,192]{2,1,0:T(8,128)(2,1)S(1)}, bf16[3,96,192]{2,1,0:T(8,128)(2,1)}, u32[]{:S(2)}) copy-start(bf16[3,96,192]{2,1,0:T(8,128)(2,1)} %param.52) | copy-start | bytes 331780
  66.0 38.3 %copy-start.95 = (f32[768]{0:T(1024)}, f32[768]{0:T(1024)S(1)}, u32[]{:S(2)}) copy-start(f32[768]{0:T(1024)S(1)} %get-tuple-element.309) | copy-start | bytes 9220
  66.0 203.7 %copy-start.101 = (f32[768]{0:T(1024)}, f32[768]{0:T(1024)S(1)}, u32[]{:S(2)}) copy-start(f32[768]{0:T(1024)S(1)} %get-tuple-element.308) | copy-start | bytes 9220
  67.6 76.5 %all-gather.20.cloned.1.call-start = ((), (), s32[]{:S(2)}) async-start(), calls=%async_computation.28 | async-start | bytes 3010560 | tf_op jit(solution)/shard_map/all_gather | solution.py:87
  68.3 38.5 %copy-start.107 = (bf16[192,96]{1,0:T(8,128)(2,1)S(1)}, bf16[192,96]{1,0:T(8,128)(2,1)}, u32[]{:S(2)}) copy-start(bf16[192,96]{1,0:T(8,128)(2,1)} %param.53) | copy-start | bytes 110596
  68.3 146.2 %reduce-scatter.39.cloned.1.call-start = ((), (), s32[]{:S(2)}) async-start(), calls=%async_computation.37 | async-start | bytes 6021120 | tf_op jit(solution)/shard_map/reduce_scatter | solution.py:91
  106.9 37.2 %copy-start.84 = (bf16[3,768,192]{1,2,0:T(8,128)(2,1)}, bf16[3,768,192]{1,2,0:T(8,128)(2,1)S(1)}, u32[]{:S(2)}) copy-start(bf16[3,768,192]{1,2,0:T(8,128)(2,1)S(1)} %copy.215) | copy-start | bytes 2654212
  138.5 43.3 %copy-start.44 = (bf16[192,768]{0,1:T(8,128)(2,1)}, bf16[192,768]{0,1:T(8,128)(2,1)S(1)}, u32[]{:S(2)}) copy-start(bf16[192,768]{0,1:T(8,128)(2,1)S(1)} %all_gather.88) | copy-start | bytes 884740
  167.1 98.5 %reduce-scatter.33.cloned.1.call-start = ((), (), s32[]{:S(2)}) async-start(), calls=%async_computation.29 | async-start | bytes 6021120 | tf_op jit(solution)/shard_map/reduce_scatter | solution.py:91
  184.9 126.6 %all-gather.22.cloned.1.call-start = ((), (), s32[]{:S(2)}) async-start(), calls=%async_computation.30 | async-start | bytes 3010560 | tf_op jit(solution)/shard_map/all_gather | solution.py:87
  267.7 380.7 %copy-start.8 = (f32[392,768]{1,0:T(8,128)}, f32[392,768]{1,0:T(8,128)S(1)}, u32[]{:S(2)}) copy-start(f32[392,768]{1,0:T(8,128)S(1)} %get-tuple-element.330) | copy-start | bytes 3612676
  271.2 50.3 %all-gather.32.cloned.1.call-start = ((), (), s32[]{:S(2)}) async-start(), calls=%async_computation.38 | async-start | bytes 3010560 | tf_op jit(solution)/shard_map/all_gather | solution.py:87
  413.8 50.1 %all-to-all-start.3 = ((bf16[64,25,192]{2,1,0:T(8,128)(2,1)}), bf16[64,25,192]{2,1,0:T(8,128)(2,1)S(1)}, u32[]{:S(2)}, u32[]{:S(2)}) async-start(bf16[64,25,192]{2,1,0:T(8,128)(2,1)} %copy.249), calls=%async_computation.7 | async-start | bytes 2097152 | tf_op jit(solution)/shard_map/all_to_all | solution.py:109
  417.4 184.8 %reduce-scatter.41.cloned.1.call-start = ((), (), s32[]{:S(2)}) async-start(), calls=%async_computation.39 | async-start | bytes 6021120 | tf_op jit(solution)/shard_map/reduce_scatter | solution.py:91
  471.5 176.8 %reduce-scatter.35.cloned.1.call-start = ((), (), s32[]{:S(2)}) async-start(), calls=%async_computation.31 | async-start | bytes 6021120 | tf_op jit(solution)/shard_map/reduce_scatter | solution.py:91
  601.5 46.8 %copy-start.11 = (f32[392,768]{1,0:T(8,128)S(1)}, f32[392,768]{1,0:T(8,128)}, u32[]{:S(2)}) copy-start(f32[392,768]{1,0:T(8,128)} %copy-done.10) | copy-start | bytes 3612676
  601.5 80.7 %all-gather.26.cloned.1.call-start = ((), (), s32[]{:S(2)}) async-start(), calls=%async_computation.33 | async-start | bytes 1327104 | tf_op jit(solution)/shard_map/all_gather | solution.py:152
  602.1 80.1 %all-gather.34.cloned.1.call-start = ((), (), s32[]{:S(2)}) async-start(), calls=%async_computation.40 | async-start | bytes 3010560 | tf_op jit(solution)/shard_map/all_gather | solution.py:87
  652.5 50.5 %all-gather.24.cloned.1.call-start = ((), (), s32[]{:S(2)}) async-start(), calls=%async_computation.32 | async-start | bytes 3010560 | tf_op jit(solution)/shard_map/all_gather | solution.py:87
  653.1 93.6 %all-gather.28.cloned.1.call-start = ((), (), s32[]{:S(2)}) async-start(), calls=%async_computation.34 | async-start | bytes 1327104 | tf_op jit(solution)/shard_map/all_gather | solution.py:153
  653.8 117.0 %all-gather.46.cloned.1.call-start = ((), (), s32[]{:S(2)}) async-start(), calls=%async_computation.55 | async-start | bytes 3010560 | tf_op jit(solution)/shard_map/all_gather | solution.py:87
  655.0 141.6 %all-gather.44.cloned.1.call-start = ((), (), s32[]{:S(2)}) async-start(), calls=%async_computation.54 | async-start | bytes 3010560 | tf_op jit(solution)/shard_map/all_gather | solution.py:87
  655.7 191.8 %reduce-scatter.51.cloned.1.call-start = ((), (), s32[]{:S(2)}) async-start(), calls=%async_computation.47 | async-start | bytes 6021120 | tf_op jit(solution)/shard_map/reduce_scatter | solution.py:91
  785.5 113.0 %reduce-scatter.45.cloned.1.call-start = ((), (), s32[]{:S(2)}) async-start(), calls=%async_computation.42 | async-start | bytes 6021120 | tf_op jit(solution)/shard_map/reduce_scatter | solution.py:91
  810.6 138.8 %reduce-scatter.37.cloned.1.call-start = ((), (), s32[]{:S(2)}) async-start(), calls=%async_computation.35 | async-start | bytes 6021120 | tf_op jit(solution)/shard_map/reduce_scatter | solution.py:91
  816.6 183.9 %reduce-scatter.43.cloned.1.call-start = ((), (), s32[]{:S(2)}) async-start(), calls=%async_computation.41 | async-start | bytes 6021120 | tf_op jit(solution)/shard_map/reduce_scatter | solution.py:91
  822.7 75.8 %copy-start.14 = (f32[392,768]{1,0:T(8,128)S(1)}, f32[392,768]{1,0:T(8,128)}, u32[]{:S(2)}) copy-start(f32[392,768]{1,0:T(8,128)} %copy-done.13) | copy-start | bytes 3612676
  822.7 75.8 %copy-start.16 = (f32[392,768]{1,0:T(8,128)S(1)}, f32[392,768]{1,0:T(8,128)}, u32[]{:S(2)}) copy-start(f32[392,768]{1,0:T(8,128)} %copy-done.15) | copy-start | bytes 3612676
  822.7 177.8 %copy-start.125 = (f32[768]{0:T(1024)S(1)}, f32[768]{0:T(1024)}, u32[]{:S(2)}) copy-start(f32[768]{0:T(1024)} %get-tuple-element.301) | copy-start | bytes 9220
  822.7 208.8 %all-gather.40.cloned.1.call-start = ((), (), s32[]{:S(2)}) async-start(), calls=%async_computation.48 | async-start | bytes 3010560 | tf_op jit(solution)/shard_map/all_gather | solution.py:87
  1099.5 62.3 %all-to-all-start.7 = ((bf16[64,25,576]{2,1,0:T(8,128)(2,1)}), bf16[64,25,576]{2,1,0:T(8,128)(2,1)S(1)}, u32[]{:S(2)}, u32[]{:S(2)}) async-start(bf16[64,25,576]{2,1,0:T(8,128)(2,1)} %copy.282), calls=%async_computation.17 | async-start | bytes 5242880 | tf_op jit(solution)/shard_map/all_to_all | solution.py:109
  1103.1 76.3 %all-gather.36.cloned.1.call-start = ((), (), s32[]{:S(2)}) async-start(), calls=%async_computation.43 | async-start | bytes 3010560 | tf_op jit(solution)/shard_map/all_gather | solution.py:87
  1103.7 216.0 %reduce-scatter.53.cloned.1.call-start = ((), (), s32[]{:S(2)}) async-start(), calls=%async_computation.49 | async-start | bytes 6021120 | tf_op jit(solution)/shard_map/reduce_scatter | solution.py:91
  1179.3 187.0 %reduce-scatter.47.cloned.1.call-start = ((), (), s32[]{:S(2)}) async-start(), calls=%async_computation.44 | async-start | bytes 6021120 | tf_op jit(solution)/shard_map/reduce_scatter | solution.py:91
  1319.6 46.8 %copy-start.9 = (f32[392,768]{1,0:T(8,128)S(1)}, f32[392,768]{1,0:T(8,128)}, u32[]{:S(2)}) copy-start(f32[392,768]{1,0:T(8,128)} %copy-done.8) | copy-start | bytes 3612676
  1319.6 46.8 %copy-start.12 = (f32[392,768]{1,0:T(8,128)S(1)}, f32[392,768]{1,0:T(8,128)}, u32[]{:S(2)}) copy-start(f32[392,768]{1,0:T(8,128)} %copy-done.10) | copy-start | bytes 3612676
  1319.6 46.8 %copy-start.102 = (f32[768]{0:T(1024)S(1)}, f32[768]{0:T(1024)}, u32[]{:S(2)}) copy-start(f32[768]{0:T(1024)} %copy-done.101) | copy-start | bytes 9220
  1319.6 46.8 %copy-start.104 = (f32[392]{0:T(512)S(1)}, f32[392]{0:T(512)}, u32[]{:S(2)}) copy-start(f32[392]{0:T(512)} %copy-done.103) | copy-start | bytes 4708
  1319.6 46.8 %copy-start.106 = (f32[392]{0:T(512)S(1)}, f32[392]{0:T(512)}, u32[]{:S(2)}) copy-start(f32[392]{0:T(512)} %copy-done.105) | copy-start | bytes 4708
  1319.6 46.8 %copy-start.110 = (f32[392]{0:T(512)S(1)}, f32[392]{0:T(512)}, u32[]{:S(2)}) copy-start(f32[392]{0:T(512)} %copy-done.109) | copy-start | bytes 4708
  1319.6 46.8 %copy-start.112 = (f32[392]{0:T(512)S(1)}, f32[392]{0:T(512)}, u32[]{:S(2)}) copy-start(f32[392]{0:T(512)} %copy-done.111) | copy-start | bytes 4708
  1319.6 49.5 %copy-start.122 = (f32[392]{0:T(512)S(1)}, f32[392]{0:T(512)}, u32[]{:S(2)}) copy-start(f32[392]{0:T(512)} %copy-done.121) | copy-start | bytes 4708
  1319.6 49.5 %copy-start.124 = (f32[392]{0:T(512)S(1)}, f32[392]{0:T(512)}, u32[]{:S(2)}) copy-start(f32[392]{0:T(512)} %copy-done.123) | copy-start | bytes 4708
  1319.7 78.6 %all-gather.42.cloned.1.call-start = ((), (), s32[]{:S(2)}) async-start(), calls=%async_computation.50 | async-start | bytes 3010560 | tf_op jit(solution)/shard_map/all_gather | solution.py:87
  1372.8 25.4 %copy-start.45 = (bf16[192,768]{0,1:T(8,128)(2,1)S(1)}, bf16[192,768]{0,1:T(8,128)(2,1)}, u32[]{:S(2)}) copy-start(bf16[192,768]{0,1:T(8,128)(2,1)} %copy-done.44) | copy-start | bytes 884740
  1373.8 53.4 %all-gather.38.cloned.1.call-start = ((), (), s32[]{:S(2)}) async-start(), calls=%async_computation.45 | async-start | bytes 3010560 | tf_op jit(solution)/shard_map/all_gather | solution.py:87
  1374.8 27.3 %copy-start.92 = (f32[8,3,196]{2,1,0:T(4,128)S(1)}, f32[8,3,196]{2,1,0:T(4,128)}, u32[]{:S(2)}) copy-start(f32[8,3,196]{2,1,0:T(4,128)} %copy-done.91) | copy-start | bytes 56452
  1374.8 139.1 %reduce-scatter.55.cloned.1.call-start = ((), (), s32[]{:S(2)}) async-start(), calls=%async_computation.51 | async-start | bytes 6021120 | tf_op jit(solution)/shard_map/reduce_scatter | solution.py:91
  1426.8 100.2 %reduce-scatter.49.cloned.1.call-start = ((), (), s32[]{:S(2)}) async-start(), calls=%async_computation.46 | async-start | bytes 6021120 | tf_op jit(solution)/shard_map/reduce_scatter | solution.py:91
  1457.6 135.9 %reduce-scatter.71.cloned.1.call-start = ((), (), s32[]{:S(2)}) async-start(), calls=%async_computation.61 | async-start | bytes 884736
  1464.2 199.3 %reduce-scatter.69.cloned.1.call-start = ((), (), s32[]{:S(2)}) async-start(), calls=%async_computation.60 | async-start | bytes 2211840
  1480.5 248.3 %reduce-scatter.67.cloned.1.call-start = ((), (), s32[]{:S(2)}) async-start(), calls=%async_computation.59 | async-start | bytes 884736
  1497.4 301.4 %reduce-scatter.65.cloned.1.call-start = ((), (), s32[]{:S(2)}) async-start(), calls=%async_computation.58 | async-start | bytes 2211840
  1513.5 349.7 %reduce-scatter.61.cloned.1.call-start = ((), (), s32[]{:S(2)}) async-start(), calls=%async_computation.56 | async-start | bytes 442368
  1533.9 393.7 %reduce-scatter.63.cloned.1.call-start = ((), (), s32[]{:S(2)}) async-start(), calls=%async_computation.57 | async-start | bytes 442368
  1535.2 465.0 %reduce-scatter.57.cloned.1.call-start = ((), (), s32[]{:S(2)}) async-start(), calls=%async_computation.52 | async-start | bytes 2654208 | tf_op jit(solution)/shard_map/reduce_scatter | solution.py:119
  1542.3 531.0 %reduce-scatter.59.cloned.1.call-start = ((), (), s32[]{:S(2)}) async-start(), calls=%async_computation.53 | async-start | bytes 2654208 | tf_op jit(solution)/shard_map/reduce_scatter | solution.py:120
  1551.4 39.2 %copy-start.82 = (bf16[1,392,768]{2,1,0:T(8,128)(2,1)S(1)}, bf16[1,392,768]{2,1,0:T(8,128)(2,1)}, u32[]{:S(2)}) copy-start(bf16[1,392,768]{2,1,0:T(8,128)(2,1)} %get-tuple-element.362) | copy-start | bytes 1806340
  1590.6 210.1 %copy-start.25 = (f32[392,768]{1,0:T(8,128)S(1)}, f32[392,768]{1,0:T(8,128)}, u32[]{:S(2)}) copy-start(f32[392,768]{1,0:T(8,128)} %copy-done.24) | copy-start | bytes 3612676
  (114 other events, 503.6 us)
Sparse Core Ops, SparseCore 0:
  67.7 21.6 all-gather.29
  91.5 24.3 all-gather.19
  167.2 47.2 reduce-scatter.38
  217.0 48.5 reduce-scatter.32
  271.3 24.3 all-gather.21
  297.1 24.3 all-gather.31
  471.6 46.6 reduce-scatter.40
  601.6 46.6 reduce-scatter.34
  1007.1 24.3 all-gather.39
  1105.2 24.7 all-gather.35
  1373.9 24.3 all-gather.41
  1399.7 24.3 all-gather.37
  1426.9 48.9 reduce-scatter.54
  1478.4 48.5 reduce-scatter.48
  1530.1 63.3 reduce-scatter.70
  1596.9 66.5 reduce-scatter.68
  1666.6 62.1 reduce-scatter.66
  1732.1 66.6 reduce-scatter.64
  1802.1 61.0 reduce-scatter.60
  1866.3 61.2 reduce-scatter.62
  1931.6 68.5 reduce-scatter.56
  2004.3 68.9 reduce-scatter.58
Sparse Core Ops, SparseCore 1:
  604.2 39.5 all-gather.25
  652.6 24.2 all-gather.33
  678.8 24.2 all-gather.23
  705.2 41.4 all-gather.27
  748.3 22.5 all-gather.45
  772.4 24.2 all-gather.43
  799.1 48.4 reduce-scatter.50
  850.0 48.4 reduce-scatter.44
  900.9 48.4 reduce-scatter.36
  952.0 48.4 reduce-scatter.42
  1179.4 46.6 reduce-scatter.52
  1319.7 46.5 reduce-scatter.46
where the time goes:
time: 2090 us; the launch traced here: 2080 us
  waiting for transfers between devices  1000 us (48%)
  blocking collectives  520 us (25%)
  local copies, waits for them, and re-layouts  244 us (12%)
  matrix products  216 us (10%)
  other arithmetic  68.4 us (3%)
    reduce_scatter x12, waiting for transfers between devices, sum_rows(): lax.psum_scatter(term(jnp.int32(0), row_count * lax.axis_size('tensor')),...  362 us
    unnamed x40, waiting for transfers between devices  327 us
    all_to_all x4, blocking collectives, to_patches(): lax.all_to_all(padded, 'wide', split_axis=1, concat_axis=0, tiled=True)  153 us
    all_gather x12, waiting for transfers between devices, gather_rows(): return lax.all_gather(block, 'tensor', axis=0, tiled=True)  101 us
    all_to_all x2, blocking collectives, to_frames(): lax.all_to_all(block, 'wide', split_axis=0, concat_axis=1, tiled=True)  89.5 us
    reduce_scatter x1, waiting for transfers between devices, reduce_wide(): lax.psum_scatter(packed[5], 'wide', scatter_dimension=1, tiled=True)  73.1 us
    unnamed x313, local copies, waits for them, and re-layouts  63.9 us
    reduce_scatter x1, waiting for transfers between devices, reduce_wide(): lax.psum_scatter(packed[4], 'wide', scatter_dimension=0, tiled=True)  61.1 us
  transfers between devices with their start and end apart: 36, of which 25 were waited for; matrix products, arithmetic and copies ran while one was open for 18% of the time, Pallas kernels for 0%

commit v1 on v0

v1 whole, which is shorter than its diff:
```python
import jax
import jax.numpy as jnp
from jax import lax
from jax.sharding import PartitionSpec as P

HEAD_DIM = 64
PATCHES = 196
FRAMES = 16
FRAME_RUN = 2
EPSILON = 1e-06
RUNS = FRAMES // FRAME_RUN

BF = jnp.bfloat16
F32 = jnp.float32


def swap(block, axis, bits):
    size = lax.axis_size(axis)
    return lax.ppermute(block, axis, [(i, i ^ bits) for i in range(size)])


def dot(left, right, dims):
    return lax.dot_general(left, right, (dims, ((), ())), preferred_element_type=F32)


def gather_wide(shard):
    count = lax.axis_size("wide")
    if count != 8:
        return lax.all_gather(shard, "wide", axis=0, tiled=True)
    pieces = {0: shard, 1: swap(shard, "wide", 1)}
    for bits in (2, 4, 6):
        pieces[bits] = swap(shard, "wide", bits)
    for bits in (2, 4, 6):
        pieces[bits ^ 1] = swap(pieces[bits], "wide", 1)
    rows = shard.shape[0]
    me = lax.axis_index("wide")
    whole = jnp.zeros((count * rows, shard.shape[1]), shard.dtype)
    for bits in range(count):
        whole = lax.dynamic_update_slice(whole, pieces[bits], ((me ^ bits) * rows, 0))
    return whole


def gather_tensor(block):
    far = swap(block, "tensor", 2)
    return [block, swap(block, "tensor", 1), far, swap(far, "tensor", 1)]


def reduce_all(parts):
    near = parts[0].astype(F32) + swap(parts[1].astype(BF), "tensor", 1).astype(F32)
    far = parts[2].astype(F32) + swap(parts[3].astype(BF), "tensor", 1).astype(F32)
    total = near + swap(far.astype(BF), "tensor", 2).astype(F32)
    return reduce_wide(total, BF)


def reduce_wide(total, link):
    count = lax.axis_size("wide")
    if count != 8:
        return lax.psum_scatter(total, "wide", scatter_dimension=0, tiled=True)
    me = lax.axis_index("wide")
    grid = total.reshape(4, 2, total.shape[0] // 8, total.shape[1])
    mine = lax.dynamic_index_in_dim(grid, me & 1, 1, keepdims=False)
    other = lax.dynamic_index_in_dim(grid, 1 - (me & 1), 1, keepdims=False)
    half = mine + swap(other.astype(link), "wide", 1).astype(F32)
    place = me >> 1
    result = lax.dynamic_index_in_dim(half, place, 0, keepdims=False)
    for bits in (1, 2, 3):
        piece = lax.dynamic_index_in_dim(half, place ^ bits, 0, keepdims=False)
        result = result + swap(piece.astype(link), "wide", bits * 2).astype(F32)
    return result


def exchange(block):
    count = lax.axis_size("wide")
    stride = count // RUNS
    groups = [[run * stride + clip for run in range(RUNS)] for clip in range(stride)]
    return lax.all_to_all(
        block, "wide", split_axis=0, concat_axis=0, tiled=True, axis_index_groups=groups
    )


def to_patches(rows, micro):
    width = rows.shape[-1]
    share = micro * PATCHES // RUNS
    cut = PATCHES // share
    block = rows.reshape(micro, FRAME_RUN, cut, share, width).swapaxes(1, 2)
    return exchange(block.reshape(RUNS, FRAME_RUN * share, width)).reshape(-1, width)


def to_frames(rows, micro):
    width = rows.shape[-1]
    share = micro * PATCHES // RUNS
    cut = PATCHES // share
    block = exchange(rows.reshape(RUNS, FRAME_RUN * share, width))
    block = block.reshape(micro, cut, FRAME_RUN, share, width).swapaxes(1, 2)
    return block.reshape(-1, width)


def norm_parts(rows):
    center = rows - jnp.mean(rows, axis=-1, keepdims=True)
    scale = lax.rsqrt(jnp.mean(center * center, axis=-1, keepdims=True) + EPSILON)
    return center * scale, scale


def norm(rows, gain, shift):
    hat, _ = norm_parts(rows)
    return (hat * gain + shift).astype(BF)


def norm_back(rows, gain, grad):
    hat, scale = norm_parts(rows)
    back = grad * gain
    inner = jnp.mean(back * hat, axis=-1, keepdims=True)
    result = scale * (back - jnp.mean(back, axis=-1, keepdims=True) - hat * inner)
    return result, jnp.sum(grad * hat, axis=0), jnp.sum(grad, axis=0)


SPATIAL = ("fphe,fqhe->fhpq", "fhpq,fqhe->fphe", "fhpq,fphe->fqhe")
TEMPORAL = ("tphe,uphe->phtu", "phtu,uphe->tphe", "phtu,tphe->uphe")


def heads_of(joined, shape):
    return joined.reshape(shape + (joined.shape[-1] // HEAD_DIM, HEAD_DIM))


def attend(queries, key_rows, value_rows, forms):
    scores = jnp.einsum(forms[0], queries, key_rows, preferred_element_type=F32)
    weights = jax.nn.softmax(scores * HEAD_DIM**-0.5, axis=-1)
    result = jnp.einsum(forms[1], weights.astype(BF), value_rows, preferred_element_type=F32)
    return weights, result.astype(BF)


def attend_back(queries, key_rows, value_rows, weights, grad_out, forms):
    grad_w = jnp.einsum(forms[0], grad_out, value_rows, preferred_element_type=F32)
    inner = jnp.sum(weights * grad_w, axis=-1, keepdims=True)
    grad_s = (weights * (grad_w - inner)).astype(BF)
    scale = HEAD_DIM**-0.5
    grad_q = jnp.einsum(forms[1], grad_s, key_rows, preferred_element_type=F32) * scale
    grad_k = jnp.einsum(forms[2], grad_s, queries, preferred_element_type=F32) * scale
    grad_v = jnp.einsum(forms[2], weights.astype(BF), grad_out, preferred_element_type=F32)
    return grad_q.astype(BF), grad_k.astype(BF), grad_v.astype(BF)


def branch(rows, packs, biases, cols, shape, forms):
    parts = [dot(rows, pack[:, : 3 * cols], ((1,), (0,))) for pack in packs]
    joined = []
    for which in range(3):
        sides = [part[:, which * cols : (which + 1) * cols] for part in parts]
        whole = jnp.concatenate(sides, axis=1)
        if which != 1:
            whole = whole + biases[which // 2]
        joined.append(heads_of(whole.astype(BF), shape))
    weights, mixed = attend(*joined, forms)
    mixed = mixed.reshape(rows.shape)
    out = sum(
        dot(mixed[:, r * cols : (r + 1) * cols], packs[r][:, 3 * cols :], ((1,), (1,)))
        for r in range(4)
    )
    return joined, weights, mixed, out


def branch_back(rows, packs, kept, grad, cols, shape, forms):
    joined, weights, mixed = kept
    grad_mixed = jnp.concatenate(
        [dot(grad, pack[:, 3 * cols :], ((1,), (0,))) for pack in packs], axis=1
    ).astype(BF)
    grads = attend_back(*joined, weights, heads_of(grad_mixed, shape), forms)
    grads = [item.reshape(rows.shape) for item in grads]
    sums, grad_rows = [], 0.0
    for r in range(4):
        span = slice(r * cols, (r + 1) * cols)
        side = jnp.concatenate([item[:, span] for item in grads], axis=1)
        grad_rows = grad_rows + dot(side, packs[r][:, : 3 * cols], ((1,), (1,)))
        first = dot(rows, side, ((0,), (0,)))
        second = dot(grad, mixed[:, span], ((0,), (0,)))
        sums.append(jnp.concatenate([first, second], axis=1).astype(BF))
    bias_sums = [jnp.sum(grads[i].astype(F32), axis=0) for i in (0, 2)]
    return grad_rows, sums, bias_sums


def per_device(
    tokens, cotangent, ln_gain, biases, fc1_bias, w_qkv_s, w_out_s, w_qkv_t, w_out_t, w_up, w_down
):
    micro, row_count, width = tokens.shape
    wide_count = lax.axis_size("wide")
    tensor_count = lax.axis_size("tensor")
    me_t = lax.axis_index("tensor")
    cols = w_qkv_s.shape[2]
    hidden = w_up.shape[1]
    slim = ln_gain.shape[1]
    assert row_count == FRAME_RUN * PATCHES and tensor_count == 4
    assert wide_count % RUNS == 0 and (micro * PATCHES) % RUNS == 0

    def pack(w_qkv, w_out):
        return jnp.concatenate([w_qkv[0], w_qkv[1], w_qkv[2], w_out.T], axis=1)

    shards = [pack(w_qkv_s, w_out_s), pack(w_qkv_t, w_out_t), w_up, w_down.T]
    small = jnp.concatenate([ln_gain, biases, fc1_bias.reshape(-1, slim)], axis=0)
    extra = small.shape[0]
    small = lax.all_gather(small, "wide", axis=0).astype(F32)
    vectors = small[:, :13].swapaxes(0, 1).reshape(13, width)
    gains, shifts = vectors[:3], vectors[3:]
    fc1 = small[:, 13:].reshape(-1)
    order = [me_t ^ r for r in range(4)]

    def turned(vector, size):
        return jnp.concatenate(
            [lax.dynamic_slice_in_dim(vector, index * size, size) for index in order]
        )

    pack_s, pack_t, pack_u, pack_d = [gather_tensor(gather_wide(shard)) for shard in shards]

    source = tokens.reshape(micro * row_count, width).astype(F32)
    frame_shape = (micro * FRAME_RUN, PATCHES)
    clip_shape = (FRAMES, micro * PATCHES // RUNS)
    grad_out = to_patches(cotangent.reshape(-1, width), micro)

    a_s = norm(source, gains[0], shifts[0])
    bias_s = (turned(shifts[3], cols), turned(shifts[4], cols))
    joined_s, weights_s, mixed_s, out_s = branch(
        a_s, pack_s, bias_s, cols, frame_shape, SPATIAL
    )
    h1 = (source + out_s + shifts[5]).astype(BF)
    h1 = to_patches(h1, micro).astype(F32)

    a_t = norm(h1, gains[1], shifts[1])
    bias_t = (turned(shifts[6], cols), turned(shifts[7], cols))
    joined_t, weights_t, mixed_t, out_t = branch(
        a_t, pack_t, bias_t, cols, clip_shape, TEMPORAL
    )
    h2 = h1 + out_t + shifts[8]
    a_m = norm(h2, gains[2], shifts[2])
    up_bias = turned(fc1, hidden)
    dyb = grad_out
    dy = grad_out.astype(F32)
    mixed = h2 + shifts[9]
    grad_am, sums_u, sums_d, sum_fc1 = 0.0, [], [], []
    for r in range(4):
        pre = dot(a_m, pack_u[r], ((1,), (0,))) + up_bias[r * hidden : (r + 1) * hidden]
        half = 0.5 * (1.0 + lax.erf(pre * 0.5**0.5))
        act = (pre * half).astype(BF)
        slope = half + pre * jnp.exp(-0.5 * pre * pre) * 0.3989422804014327
        mixed = mixed + dot(act, pack_d[r], ((1,), (1,)))
        grad_act = dot(dyb, pack_d[r], ((1,), (0,)))
        grad_pre = (grad_act * slope).astype(BF)
        sums_d.append(dot(dyb, act, ((0,), (0,))).astype(BF))
        sums_u.append(dot(a_m, grad_pre, ((0,), (0,))).astype(BF))
        sum_fc1.append(jnp.sum(grad_pre.astype(F32), axis=0))
        grad_am = grad_am + dot(grad_pre, pack_u[r], ((1,), (1,)))
    mixed = to_frames(mixed.astype(BF), micro)
    grad_d = reduce_all(sums_d)
    grad_u = reduce_all(sums_u)

    back, gain_m, shift_m = norm_back(h2, gains[2], grad_am)
    dh2 = dy + back
    grad_at, sums_t, bias_sums_t = branch_back(
        a_t, pack_t, (joined_t, weights_t, mixed_t), dh2.astype(BF), cols, clip_shape, TEMPORAL
    )
    grad_t = reduce_all(sums_t)
    back, gain_t, shift_t = norm_back(h1, gains[1], grad_at)
    dh1 = dh2 + back
    sum_dh1 = jnp.sum(dh1, axis=0)
    dh1 = to_frames(dh1.astype(BF), micro)
    grad_as, sums_s, bias_sums_s = branch_back(
        a_s, pack_s, (joined_s, weights_s, mixed_s), dh1, cols, frame_shape, SPATIAL
    )
    grad_s = reduce_all(sums_s)
    back, gain_s, shift_s = norm_back(source, gains[0], grad_as)
    grad_tokens = dh1.astype(F32) + back

    def placed(items, size):
        whole = jnp.zeros((4 * size,), F32)
        for r in range(4):
            whole = lax.dynamic_update_slice(whole, items[r], (order[r] * size,))
        return whole

    def split(vector, size):
        return [vector[r * size : (r + 1) * size] for r in range(4)]

    rows = [gain_s, gain_t, gain_m, shift_s, shift_t, shift_m]
    rows += [placed(split(item, cols), cols) for item in bias_sums_s]
    rows += [sum_dh1]
    rows += [placed(split(item, cols), cols) for item in bias_sums_t]
    rows += [jnp.sum(dh2, axis=0), jnp.sum(dy, axis=0)]
    table = jnp.stack(rows).reshape(13, wide_count, slim).swapaxes(0, 1)
    table = jnp.concatenate(
        [table, placed(sum_fc1, hidden).reshape(wide_count, extra - 13, slim)], axis=1
    )
    table = jnp.pad(table, ((0, 0), (0, -extra % 8), (0, 0)))
    height = table.shape[1]
    table = table.reshape(wide_count * height, slim)
    table = table + swap(table, "tensor", 1)
    table = table + swap(table, "tensor", 2)
    table = reduce_wide(table, F32)

    def unpack(total):
        w_qkv = jnp.stack([total[:, i * cols : (i + 1) * cols] for i in range(3)])
        return w_qkv, total[:, 3 * cols :].T

    qkv_s, out_s = unpack(grad_s)
    qkv_t, out_t = unpack(grad_t)
    return (
        mixed.reshape(tokens.shape),
        grad_tokens.reshape(tokens.shape),
        table[:3],
        table[3:13],
        table[13:extra].reshape(-1),
        qkv_s,
        out_s,
        qkv_t,
        out_t,
        grad_u,
        grad_d.T,
    )


def solution(mesh):
    specs = (
        P(None, ("wide", "tensor"), None),
        P(None, ("wide", "tensor"), None),
        P(None, "wide"),
        P(None, "wide"),
        P("wide"),
        P(None, "wide", "tensor"),
        P("tensor", "wide"),
        P(None, "wide", "tensor"),
        P("tensor", "wide"),
        P("wide", "tensor"),
        P("tensor", "wide"),
    )
    return jax.shard_map(
        per_device, mesh=mesh, in_specs=specs, out_specs=specs, check_vma=False
    )
```

time: 2090 us -> 826 us (0.40)
  waiting for transfers between devices: 1000 us -> 150 us
  blocking collectives: 520 us -> 52.3 us
  starting transfers between devices: 11.1 us -> 103 us
  local copies, waits for them, and re-layouts: 244 us -> 206 us
  other arithmetic: 68.4 us -> 90.2 us
    reduce_scatter x14 -> x0, waiting for transfers between devices: 496 us -> none  [the longest x12 362 us: sum_rows(): lax.psum_scatter(term(jnp.int32(0), row_count * lax.axis_size('tensor')),...]
    unnamed x40 -> x0, waiting for transfers between devices: 327 us -> none
    all_to_all x6 -> x0, blocking collectives: 242 us -> none  [the longest x4 153 us: to_patches(): lax.all_to_all(padded, 'wide', split_axis=1, concat_axis=0, tiled=True)]
    all_gather x7 -> x1, blocking collectives: 230 us -> 52.3 us  [per_device(): small = lax.all_gather(small, 'wide', axis=0).astype(F32)]
    ppermute x0 -> x74, waiting for transfers between devices: none -> 150 us  [swap(): return lax.ppermute(block, axis, [(i, i ^ bits) for i in range(size)])]
    all_gather x14 -> x0, waiting for transfers between devices: 120 us -> none  [the longest x12 101 us: gather_rows(): return lax.all_gather(block, 'tensor', axis=0, tiled=True)]
    ppermute x0 -> x74, starting transfers between devices: none -> 81.9 us  [swap(): return lax.ppermute(block, axis, [(i, i ^ bits) for i in range(size)])]
    another operation x30 -> x38, local copies, waits for them, and re-layouts: 70.2 us -> 6.42 us  [the longest x4 20 us: per_device(): out_of_time(jnp.stack([grad_q, grad_k, grad_v], axis=3))]
  transfers between devices with their start and end apart: 36 -> 78, of which waited for: 25 -> 17; matrix products, arithmetic and copies ran while one was open for 18% -> 47% of each run, Pallas kernels for 0% -> 0%
where the time goes in v1:
time: 826 us; the launch traced here: 819 us
  matrix products  214 us (26%)
  local copies, waits for them, and re-layouts  206 us (25%)
  waiting for transfers between devices  150 us (18%)
  starting transfers between devices  103 us (12%)
  other arithmetic  90.2 us (11%)
  blocking collectives  52.3 us (6%)
    dot_general x72, matrix products, dot(): lax.dot_general(left, right, (dims, ((), ())), preferred_element_type=F32)  166 us
    ppermute x74, waiting for transfers between devices, swap(): return lax.ppermute(block, axis, [(i, i ^ bits) for i in range(size)])  150 us
    ppermute x74, starting transfers between devices, swap(): return lax.ppermute(block, axis, [(i, i ^ bits) for i in range(size)])  81.9 us
    all_gather x1, blocking collectives, per_device(): small = lax.all_gather(small, 'wide', axis=0).astype(F32)  52.3 us
    concatenate x6, local copies, waits for them, and re-layouts, branch(): whole = jnp.concatenate(sides, axis=1)  24.3 us
    reshape x6, local copies, waits for them, and re-layouts, branch_back(): grads = [item.reshape(rows.shape) for item in grads]  21.7 us
    all_to_all x4, starting transfers between devices, exchange(): lax.all_to_all(block, 'wide', split_axis=0, concat_axis=0, tiled=True, ax...  21 us
    dynamic_update_slice x32, local copies, waits for them, and re-layouts, gather_wide(): lax.dynamic_update_slice(whole, pieces[bits], ((me ^ bits) * rows, 0))  20.7 us
  transfers between devices with their start and end apart: 78, of which 17 were waited for; matrix products, arithmetic and copies ran while one was open for 47% of the time, Pallas kernels for 0%

profile of v1, /device:TPU:0, one launch (start us, length us, event | category | flops | bytes accessed | tf_op | source)
XLA Modules:
  0.0 819.4 jit_solution(14651008353032056921)
XLA Ops:
  15.0 6.2 all-to-all-start.2
  22.5 52.3 %all-gather.1 = bf16[8,17,96]{2,1,0:T(8,128)(2,1)S(1)} all-gather(bf16[1,17,96]{2,1,0:T(8,128)(2,1)S(1)} %maximum_bitcast_fusion), channel_id=2, replica_groups=mesh['wide'=8,'tensor'=4] {'wide'}, dimensions={0}, use_global_device_ids=true | all-gather | bytes 29376 | tf_op jit(solution)/shard_map/all_gather | solution.py:199
  91.4 3.1 collective-permute-start.13
  99.0 4.4 collective-permute-done.4
  105.1 4.1 collective-permute-done.6
  125.3 4.0 collective-permute-done.8
  140.0 3.5 reshape.458
  143.5 3.9 copy.321
  147.4 6.6 pad_maximum_fusion
  154.1 3.2 copy.318
  157.3 5.5 concatenate.163
  166.7 5.3 fusion.227
  172.0 3.3 copy.317
  175.3 5.5 concatenate.156
  183.2 5.4 fusion.64
  202.9 4.7 all-to-all-start
  209.1 3.8 collective-permute-start.25
  219.4 6.4 collective-permute-done.14
  225.9 7.0 collective-permute-start.32
  238.3 17.1 %collective-permute-done.30 = bf16[96,768]{1,0:T(8,128)(2,1)S(1)} collective-permute-done((bf16[96,768]{1,0:T(8,128)(2,1)S(1)}, bf16[96,768]{1,0:T(8,128)(2,1)S(1)}, u32[]{:S(2)}, u32[]{:S(2)}) %collective-permute-start.30) | collective-permute-done | bytes 147488 | tf_op jit(solution)/shard_map/ppermute | solution.py:19
  280.6 10.4 %collective-permute-done.18 = bf16[768,768]{1,0:T(8,128)(2,1)} collective-permute-done((bf16[768,768]{1,0:T(8,128)(2,1)}, bf16[768,768]{1,0:T(8,128)(2,1)}, u32[]{:S(2)}, u32[]{:S(2)}) %collective-permute-start.18) | collective-permute-done | bytes 1179680 | tf_op jit(solution)/shard_map/ppermute | solution.py:19
  291.0 25.3 %collective-permute-done.36 = bf16[768,768]{1,0:T(8,128)(2,1)} collective-permute-done((bf16[768,768]{1,0:T(8,128)(2,1)}, bf16[768,768]{1,0:T(8,128)(2,1)}, u32[]{:S(2)}, u32[]{:S(2)}) %collective-permute-start.36) | collective-permute-done | bytes 1179680 | tf_op jit(solution)/shard_map/ppermute | solution.py:19
  316.3 24.8 %collective-permute-done.37 = bf16[768,768]{1,0:T(8,128)(2,1)} collective-permute-done((bf16[768,768]{1,0:T(8,128)(2,1)}, bf16[768,768]{1,0:T(8,128)(2,1)}, u32[]{:S(2)}, u32[]{:S(2)}) %collective-permute-start.37) | collective-permute-done | bytes 1179680 | tf_op jit(solution)/shard_map/ppermute | solution.py:19
  353.6 3.4 concatenate.179
  359.6 4.0 convert_element_type.485
  363.6 4.5 add_convert_fusion
  369.8 3.9 fusion.228
  374.3 3.4 concatenate.172
  377.8 3.5 add_convert_fusion.1
  398.0 3.9 convert_reduce_fusion.6
  404.4 3.6 multiply_convert_fusion.9
  408.0 3.6 multiply_convert_fusion.8
  414.2 3.8 convert_reduce_fusion.8
  420.4 3.6 convert_reduce_fusion.9
  430.0 3.6 multiply_convert_fusion.7
  433.6 3.6 convert_reduce_fusion.7
  440.0 3.5 multiply_reduce_fusion.5
  452.4 7.5 reshape.459
  459.9 6.3 copy.353
  466.2 5.7 multiply_reduce_fusion.2
  471.9 4.1 multiply_convert_fusion.3
  481.0 3.4 convert_reduce_fusion
  491.5 5.1 reshape.428
  502.0 5.1 reshape.429
  512.4 5.2 reshape.430
  527.1 4.0 fusion.230
  551.9 4.3 all-to-all-start.3
  561.9 4.0 add_convert_fusion.4
  574.4 3.9 convolution_convert_fusion.7
  578.3 3.9 fusion.45
  583.6 3.8 add_convert_fusion.8
  590.6 5.9 all-to-all-start.1
  608.7 10.4 %multiply_reduce_fusion = (f32[4,12,196]{2,1,0:T(8,128)S(1)}, f32[4,12,196,196]{2,3,1,0:T(8,128)}) fusion(f32[4,12,196,196]{2,3,1,0:T(8,128)} %get-tuple-element.205, f32[4,12,196]{2,1,0:T(8,128)S(1)} %copy-done.101, bf16[4,196,12,64]{1,0,3,2:T(4,128)(2,1)} %copy-done.60, bf16[4,196,12,64]{1,0,3,2:T(4,128)(2,1)} %convert_element_type.511), kind=kOutput, calls=%fused_computation.3 | convolution fusion | flops 241550400 | bytes 17235456 | tf_op jit(solution)/shard_map/fphe,fqhe->fhpq/dot_general | solution.py:133
  619.1 11.4 %multiply_convert_fusion = bf16[4,12,196,196]{2,3,1,0:T(8,128)(2,1)} fusion(f32[4,12,196,196]{2,3,1,0:T(8,128)} %get-tuple-element.221, f32[4,12,196]{2,1,0:T(8,128)S(1)} %get-tuple-element.220, f32[4,12,196,196]{2,3,1,0:T(8,128)} %get-tuple-element.205, f32[4,12,196]{2,1,0:T(8,128)S(1)} %copy-done.101), kind=kLoop, calls=%fused_computation.2 | loop fusion | flops 7375872 | bytes 18514944 | tf_op jit(solution)/shard_map/convert_element_type | solution.py:135
  630.5 3.7 convert_reduce_fusion.3
  637.7 6.8 convert_reduce_fusion.2
  671.1 3.3 convolution_convert_fusion.10
  681.1 3.7 fusion.199
  684.9 3.3 multiply_add_fusion
  726.5 16.0 %collective-permute-done.55 = bf16[768,768]{0,1:T(8,128)(2,1)} collective-permute-done((bf16[768,768]{0,1:T(8,128)(2,1)S(1)}, bf16[768,768]{0,1:T(8,128)(2,1)}, u32[]{:S(2)}, u32[]{:S(2)}) %collective-permute-start.55) | collective-permute-done | bytes 1179680 | tf_op jit(solution)/shard_map/ppermute | solution.py:19
  758.1 6.5 collective-permute-done.56
  767.3 8.6 %collective-permute-done.48 = bf16[768,768]{0,1:T(8,128)(2,1)S(1)} collective-permute-done((bf16[768,768]{0,1:T(8,128)(2,1)S(1)}, bf16[768,768]{0,1:T(8,128)(2,1)S(1)}, u32[]{:S(2)}, u32[]{:S(2)}) %collective-permute-start.48) | collective-permute-done | bytes 1179680 | tf_op jit(solution)/shard_map/ppermute | solution.py:19
  792.9 8.0 collective-permute-done.58
  808.7 8.6 %collective-permute-done.51 = bf16[96,768]{1,0:T(8,128)(2,1)S(1)} collective-permute-done((bf16[96,768]{1,0:T(8,128)(2,1)S(1)}, bf16[96,768]{1,0:T(8,128)(2,1)S(1)}, u32[]{:S(2)}, u32[]{:S(2)}) %collective-permute-start.51) | collective-permute-done | bytes 147488 | tf_op jit(solution)/shard_map/ppermute | solution.py:19
  (795 shorter events, 385.3 us)
Async XLA Ops:
  2.8 86.0 %collective-permute-start = (bf16[96,768]{0,1:T(8,128)(2,1)S(1)}, bf16[96,768]{0,1:T(8,128)(2,1)}, u32[]{:S(2)}, u32[]{:S(2)}) collective-permute-start(bf16[96,768]{0,1:T(8,128)(2,1)S(1)} %pad_maximum_fusion.38), channel_id=1, source_target_pairs={{0,4},{4,0},{8,12},{12,8},{16,20},{20,16},{24,28},{28,24},{1,5},{5... | collective-permute-start | bytes 442376 | tf_op jit(solution)/shard_map/ppermute | solution.py:19
  5.8 84.1 %collective-permute-start.1 = (bf16[96,768]{0,1:T(8,128)(2,1)S(1)}, bf16[96,768]{0,1:T(8,128)(2,1)}, u32[]{:S(2)}, u32[]{:S(2)}) collective-permute-start(bf16[96,768]{0,1:T(8,128)(2,1)S(1)} %pad_maximum_fusion.38), channel_id=1, source_target_pairs={{0,8},{4,12},{8,0},{12,4},{16,24},{20,28},{24,16},{28,20},{1,9},{5... | collective-permute-start | bytes 442376 | tf_op jit(solution)/shard_map/ppermute | solution.py:19
  7.4 84.0 %collective-permute-start.3 = (bf16[96,768]{0,1:T(8,128)(2,1)S(1)}, bf16[96,768]{0,1:T(8,128)(2,1)}, u32[]{:S(2)}, u32[]{:S(2)}) collective-permute-start(bf16[96,768]{0,1:T(8,128)(2,1)S(1)} %pad_maximum_fusion.38), channel_id=1, source_target_pairs={{0,16},{4,20},{8,24},{12,28},{16,0},{20,4},{24,8},{28,12},{1,17},{... | collective-permute-start | bytes 442376 | tf_op jit(solution)/shard_map/ppermute | solution.py:19
  10.0 85.6 %collective-permute-start.5 = (bf16[96,768]{0,1:T(8,128)(2,1)S(1)}, bf16[96,768]{0,1:T(8,128)(2,1)S(1)}, u32[]{:S(2)}, u32[]{:S(2)}) collective-permute-start(bf16[96,768]{0,1:T(8,128)(2,1)S(1)} %pad_maximum_fusion.38), channel_id=1, source_target_pairs={{0,24},{4,28},{8,16},{12,20},{16,8},{20,12},{24,0},{28,4},{1,25},{... | collective-permute-start | bytes 442376 | tf_op jit(solution)/shard_map/ppermute | solution.py:19
  12.3 100.8 %collective-permute-start.10 = (bf16[96,768]{0,1:T(8,128)(2,1)S(1)}, bf16[96,768]{0,1:T(8,128)(2,1)S(1)}, u32[]{:S(2)}, u32[]{:S(2)}) collective-permute-start(bf16[96,768]{0,1:T(8,128)(2,1)S(1)} %pad_maximum_fusion.39), channel_id=1, source_target_pairs={{0,4},{4,0},{8,12},{12,8},{16,20},{20,16},{24,28},{28,24},{1,5},{5... | collective-permute-start | bytes 442376 | tf_op jit(solution)/shard_map/ppermute | solution.py:19
  15.0 187.9 %all-to-all-start.2 = ((bf16[8,98,768]{2,1,0:T(8,128)(2,1)}), bf16[8,98,768]{2,1,0:T(8,128)(2,1)}, u32[]{:S(2)}, u32[]{:S(2)}) async-start(bf16[8,98,768]{2,1,0:T(8,128)(2,1)} %reshape.456), calls=%async_computation.2 | async-start | bytes 2555904 | tf_op jit(solution)/shard_map/all_to_all | solution.py:76
  88.9 26.1 %collective-permute-start.11 = (bf16[96,768]{0,1:T(8,128)(2,1)S(1)}, bf16[96,768]{0,1:T(8,128)(2,1)}, u32[]{:S(2)}, u32[]{:S(2)}) collective-permute-start(bf16[96,768]{0,1:T(8,128)(2,1)S(1)} %pad_maximum_fusion.39), channel_id=1, source_target_pairs={{0,8},{4,12},{8,0},{12,4},{16,24},{20,28},{24,16},{28,20},{1,9},{5... | collective-permute-start | bytes 442376 | tf_op jit(solution)/shard_map/ppermute | solution.py:19
  91.4 117.7 %collective-permute-start.13 = (bf16[96,768]{0,1:T(8,128)(2,1)S(1)}, bf16[96,768]{0,1:T(8,128)(2,1)}, u32[]{:S(2)}, u32[]{:S(2)}) collective-permute-start(bf16[96,768]{0,1:T(8,128)(2,1)S(1)} %pad_maximum_fusion.39), channel_id=1, source_target_pairs={{0,16},{4,20},{8,24},{12,28},{16,0},{20,4},{24,8},{28,12},{1,17},{... | collective-permute-start | bytes 442376 | tf_op jit(solution)/shard_map/ppermute | solution.py:19
  95.6 21.2 %collective-permute-start.20 = (bf16[96,768]{1,0:T(8,128)(2,1)}, bf16[96,768]{1,0:T(8,128)(2,1)}, u32[]{:S(2)}, u32[]{:S(2)}) collective-permute-start(bf16[96,768]{1,0:T(8,128)(2,1)} %param.20), channel_id=1, source_target_pairs={{0,4},{4,0},{8,12},{12,8},{16,20},{20,16},{24,28},{28,24},{1,5},{5... | collective-permute-start | bytes 442376 | tf_op jit(solution)/shard_map/ppermute | solution.py:19
  110.3 18.9 %collective-permute-start.8 = (bf16[768,768]{1,0:T(8,128)(2,1)S(1)}, bf16[768,768]{1,0:T(8,128)(2,1)}, u32[]{:S(2)}, u32[]{:S(2)}) collective-permute-start(bf16[768,768]{1,0:T(8,128)(2,1)S(1)} %constant_dynamic-update-slice_fusion.24), channel_id=1, source_target_pairs={{0,2},{1,3},{2,0},{3,1},{4,6},{5,7},{6,4},{7,5},{8,10},{9,11},{10,... | collective-permute-start | bytes 3538952 | tf_op jit(solution)/shard_map/ppermute | solution.py:19
  116.0 15.8 %collective-permute-start.7 = (bf16[768,768]{1,0:T(8,128)(2,1)S(1)}, bf16[768,768]{1,0:T(8,128)(2,1)S(1)}, u32[]{:S(2)}, u32[]{:S(2)}) collective-permute-start(bf16[768,768]{1,0:T(8,128)(2,1)S(1)} %constant_dynamic-update-slice_fusion.24), channel_id=1, source_target_pairs={{0,1},{1,0},{2,3},{3,2},{4,5},{5,4},{6,7},{7,6},{8,9},{9,8},{10,11... | collective-permute-start | bytes 3538952 | tf_op jit(solution)/shard_map/ppermute | solution.py:19
  116.8 97.3 %collective-permute-start.15 = (bf16[96,768]{0,1:T(8,128)(2,1)S(1)}, bf16[96,768]{0,1:T(8,128)(2,1)S(1)}, u32[]{:S(2)}, u32[]{:S(2)}) collective-permute-start(bf16[96,768]{0,1:T(8,128)(2,1)S(1)} %pad_maximum_fusion.39), channel_id=1, source_target_pairs={{0,24},{4,28},{8,16},{12,20},{16,8},{20,12},{24,0},{28,4},{1,25},{... | collective-permute-start | bytes 442376 | tf_op jit(solution)/shard_map/ppermute | solution.py:19
  119.1 116.1 %collective-permute-start.23 = (bf16[96,768]{1,0:T(8,128)(2,1)}, bf16[96,768]{1,0:T(8,128)(2,1)}, u32[]{:S(2)}, u32[]{:S(2)}) collective-permute-start(bf16[96,768]{1,0:T(8,128)(2,1)} %param.20), channel_id=1, source_target_pairs={{0,16},{4,20},{8,24},{12,28},{16,0},{20,4},{24,8},{28,12},{1,17},{... | collective-permute-start | bytes 442376 | tf_op jit(solution)/shard_map/ppermute | solution.py:19
  131.8 69.4 %collective-permute-start.27 = (bf16[96,768]{1,0:T(8,128)(2,1)S(1)}, bf16[96,768]{1,0:T(8,128)(2,1)}, u32[]{:S(2)}, u32[]{:S(2)}) collective-permute-start(bf16[96,768]{1,0:T(8,128)(2,1)S(1)} %bitcast.325), channel_id=1, source_target_pairs={{0,4},{4,0},{8,12},{12,8},{16,20},{20,16},{24,28},{28,24},{1,5},{5... | collective-permute-start | bytes 442376 | tf_op jit(solution)/shard_map/ppermute | solution.py:19
  136.8 77.5 %collective-permute-start.28 = (bf16[96,768]{1,0:T(8,128)(2,1)S(1)}, bf16[96,768]{1,0:T(8,128)(2,1)}, u32[]{:S(2)}, u32[]{:S(2)}) collective-permute-start(bf16[96,768]{1,0:T(8,128)(2,1)S(1)} %bitcast.326), channel_id=1, source_target_pairs={{0,8},{4,12},{8,0},{12,4},{16,24},{20,28},{24,16},{28,20},{1,9},{5... | collective-permute-start | bytes 442376 | tf_op jit(solution)/shard_map/ppermute | solution.py:19
  201.2 16.1 %collective-permute-start.12 = (bf16[96,768]{0,1:T(8,128)(2,1)}, bf16[96,768]{0,1:T(8,128)(2,1)S(1)}, u32[]{:S(2)}, u32[]{:S(2)}) collective-permute-start(bf16[96,768]{0,1:T(8,128)(2,1)} %collective-permute-done.11), channel_id=1, source_target_pairs={{0,4},{4,0},{8,12},{12,8},{16,20},{20,16},{24,28},{28,24},{1,5},{5... | collective-permute-start | bytes 442376 | tf_op jit(solution)/shard_map/ppermute | solution.py:19
  202.9 71.1 %all-to-all-start = ((bf16[8,98,768]{2,1,0:T(8,128)(2,1)}), bf16[8,98,768]{2,1,0:T(8,128)(2,1)S(1)}, u32[]{:S(2)}, u32[]{:S(2)}) async-start(bf16[8,98,768]{2,1,0:T(8,128)(2,1)} %reshape.454), calls=%async_computation | async-start | bytes 2555904 | tf_op jit(solution)/shard_map/all_to_all | solution.py:76
  209.1 28.1 %collective-permute-start.25 = (bf16[96,768]{1,0:T(8,128)(2,1)}, bf16[96,768]{1,0:T(8,128)(2,1)S(1)}, u32[]{:S(2)}, u32[]{:S(2)}) collective-permute-start(bf16[96,768]{1,0:T(8,128)(2,1)} %param.20), channel_id=1, source_target_pairs={{0,24},{4,28},{8,16},{12,20},{16,8},{20,12},{24,0},{28,4},{1,25},{... | collective-permute-start | bytes 442376 | tf_op jit(solution)/shard_map/ppermute | solution.py:19
  214.0 41.4 %collective-permute-start.30 = (bf16[96,768]{1,0:T(8,128)(2,1)S(1)}, bf16[96,768]{1,0:T(8,128)(2,1)S(1)}, u32[]{:S(2)}, u32[]{:S(2)}) collective-permute-start(bf16[96,768]{1,0:T(8,128)(2,1)S(1)} %bitcast.327), channel_id=1, source_target_pairs={{0,16},{4,20},{8,24},{12,28},{16,0},{20,4},{24,8},{28,12},{1,17},{... | collective-permute-start | bytes 442376 | tf_op jit(solution)/shard_map/ppermute | solution.py:19
  214.3 11.6 %collective-permute-start.14 = (bf16[96,768]{0,1:T(8,128)(2,1)}, bf16[96,768]{0,1:T(8,128)(2,1)S(1)}, u32[]{:S(2)}, u32[]{:S(2)}) collective-permute-start(bf16[96,768]{0,1:T(8,128)(2,1)} %collective-permute-done.13), channel_id=1, source_target_pairs={{0,4},{4,0},{8,12},{12,8},{16,20},{20,16},{24,28},{28,24},{1,5},{5... | collective-permute-start | bytes 442376 | tf_op jit(solution)/shard_map/ppermute | solution.py:19
  217.3 16.4 %collective-permute-start.16 = (bf16[96,768]{0,1:T(8,128)(2,1)S(1)}, bf16[96,768]{0,1:T(8,128)(2,1)S(1)}, u32[]{:S(2)}, u32[]{:S(2)}) collective-permute-start(bf16[96,768]{0,1:T(8,128)(2,1)S(1)} %collective-permute-done.15), channel_id=1, source_target_pairs={{0,4},{4,0},{8,12},{12,8},{16,20},{20,16},{24,28},{28,24},{1,5},{5... | collective-permute-start | bytes 442376 | tf_op jit(solution)/shard_map/ppermute | solution.py:19
  225.9 30.4 %collective-permute-start.32 = (bf16[96,768]{1,0:T(8,128)(2,1)S(1)}, bf16[96,768]{1,0:T(8,128)(2,1)S(1)}, u32[]{:S(2)}, u32[]{:S(2)}) collective-permute-start(bf16[96,768]{1,0:T(8,128)(2,1)S(1)} %bitcast.328), channel_id=1, source_target_pairs={{0,24},{4,28},{8,16},{12,20},{16,8},{20,12},{24,0},{28,4},{1,25},{... | collective-permute-start | bytes 442376 | tf_op jit(solution)/shard_map/ppermute | solution.py:19
  233.7 23.7 %collective-permute-start.22 = (bf16[96,768]{1,0:T(8,128)(2,1)S(1)}, bf16[96,768]{1,0:T(8,128)(2,1)S(1)}, u32[]{:S(2)}, u32[]{:S(2)}) collective-permute-start(bf16[96,768]{1,0:T(8,128)(2,1)S(1)} %collective-permute-done.21), channel_id=1, source_target_pairs={{0,4},{4,0},{8,12},{12,8},{16,20},{20,16},{24,28},{28,24},{1,5},{5... | collective-permute-start | bytes 442376 | tf_op jit(solution)/shard_map/ppermute | solution.py:19
  235.2 28.8 %collective-permute-start.29 = (bf16[96,768]{1,0:T(8,128)(2,1)}, bf16[96,768]{1,0:T(8,128)(2,1)S(1)}, u32[]{:S(2)}, u32[]{:S(2)}) collective-permute-start(bf16[96,768]{1,0:T(8,128)(2,1)} %collective-permute-done.28), channel_id=1, source_target_pairs={{0,4},{4,0},{8,12},{12,8},{16,20},{20,16},{24,28},{28,24},{1,5},{5... | collective-permute-start | bytes 442376 | tf_op jit(solution)/shard_map/ppermute | solution.py:19
  237.2 23.3 %collective-permute-start.24 = (bf16[96,768]{1,0:T(8,128)(2,1)}, bf16[96,768]{1,0:T(8,128)(2,1)S(1)}, u32[]{:S(2)}, u32[]{:S(2)}) collective-permute-start(bf16[96,768]{1,0:T(8,128)(2,1)} %collective-permute-done.23), channel_id=1, source_target_pairs={{0,4},{4,0},{8,12},{12,8},{16,20},{20,16},{24,28},{28,24},{1,5},{5... | collective-permute-start | bytes 442376 | tf_op jit(solution)/shard_map/ppermute | solution.py:19
  257.4 9.8 %collective-permute-start.33 = (bf16[96,768]{1,0:T(8,128)(2,1)S(1)}, bf16[96,768]{1,0:T(8,128)(2,1)S(1)}, u32[]{:S(2)}, u32[]{:S(2)}) collective-permute-start(bf16[96,768]{1,0:T(8,128)(2,1)S(1)} %collective-permute-done.32), channel_id=1, source_target_pairs={{0,4},{4,0},{8,12},{12,8},{16,20},{20,16},{24,28},{28,24},{1,5},{5... | collective-permute-start | bytes 442376 | tf_op jit(solution)/shard_map/ppermute | solution.py:19
  260.5 19.8 %collective-permute-start.17 = (bf16[768,768]{1,0:T(8,128)(2,1)}, bf16[768,768]{1,0:T(8,128)(2,1)}, u32[]{:S(2)}, u32[]{:S(2)}) collective-permute-start(bf16[768,768]{1,0:T(8,128)(2,1)} %constant_dynamic-update-slice_fusion.16), channel_id=1, source_target_pairs={{0,1},{1,0},{2,3},{3,2},{4,5},{5,4},{6,7},{7,6},{8,9},{9,8},{10,11... | collective-permute-start | bytes 3538952 | tf_op jit(solution)/shard_map/ppermute | solution.py:19
  261.9 29.2 %collective-permute-start.18 = (bf16[768,768]{1,0:T(8,128)(2,1)}, bf16[768,768]{1,0:T(8,128)(2,1)}, u32[]{:S(2)}, u32[]{:S(2)}) collective-permute-start(bf16[768,768]{1,0:T(8,128)(2,1)} %constant_dynamic-update-slice_fusion.16), channel_id=1, source_target_pairs={{0,2},{1,3},{2,0},{3,1},{4,6},{5,7},{6,4},{7,5},{8,10},{9,11},{10,... | collective-permute-start | bytes 3538952 | tf_op jit(solution)/shard_map/ppermute | solution.py:19
  264.1 52.2 %collective-permute-start.36 = (bf16[768,768]{1,0:T(8,128)(2,1)}, bf16[768,768]{1,0:T(8,128)(2,1)}, u32[]{:S(2)}, u32[]{:S(2)}) collective-permute-start(bf16[768,768]{1,0:T(8,128)(2,1)} %constant_dynamic-update-slice_fusion.8), channel_id=1, source_target_pairs={{0,2},{1,3},{2,0},{3,1},{4,6},{5,7},{6,4},{7,5},{8,10},{9,11},{10,... | collective-permute-start | bytes 3538952 | tf_op jit(solution)/shard_map/ppermute | solution.py:19
  265.9 142.1 %collective-permute-start.34 = (bf16[768,768]{1,0:T(8,128)(2,1)}, bf16[768,768]{1,0:T(8,128)(2,1)}, u32[]{:S(2)}, u32[]{:S(2)}) collective-permute-start(bf16[768,768]{1,0:T(8,128)(2,1)} %constant_dynamic-update-slice_fusion.8), channel_id=1, source_target_pairs={{0,1},{1,0},{2,3},{3,2},{4,5},{5,4},{6,7},{7,6},{8,9},{9,8},{10,11... | collective-permute-start | bytes 3538952 | tf_op jit(solution)/shard_map/ppermute | solution.py:19
  267.9 73.2 %collective-permute-start.37 = (bf16[768,768]{1,0:T(8,128)(2,1)}, bf16[768,768]{1,0:T(8,128)(2,1)}, u32[]{:S(2)}, u32[]{:S(2)}) collective-permute-start(bf16[768,768]{1,0:T(8,128)(2,1)} %constant_dynamic-update-slice_fusion), channel_id=1, source_target_pairs={{0,2},{1,3},{2,0},{3,1},{4,6},{5,7},{6,4},{7,5},{8,10},{9,11},{10,... | collective-permute-start | bytes 3538952 | tf_op jit(solution)/shard_map/ppermute | solution.py:19
  280.3 133.8 %collective-permute-start.35 = (bf16[768,768]{1,0:T(8,128)(2,1)}, bf16[768,768]{1,0:T(8,128)(2,1)}, u32[]{:S(2)}, u32[]{:S(2)}) collective-permute-start(bf16[768,768]{1,0:T(8,128)(2,1)} %constant_dynamic-update-slice_fusion), channel_id=1, source_target_pairs={{0,1},{1,0},{2,3},{3,2},{4,5},{5,4},{6,7},{7,6},{8,9},{9,8},{10,11... | collective-permute-start | bytes 3538952 | tf_op jit(solution)/shard_map/ppermute | solution.py:19
  291.0 58.9 %collective-permute-start.19 = (bf16[768,768]{1,0:T(8,128)(2,1)}, bf16[768,768]{1,0:T(8,128)(2,1)S(1)}, u32[]{:S(2)}, u32[]{:S(2)}) collective-permute-start(bf16[768,768]{1,0:T(8,128)(2,1)} %collective-permute-done.18), channel_id=1, source_target_pairs={{0,1},{1,0},{2,3},{3,2},{4,5},{5,4},{6,7},{7,6},{8,9},{9,8},{10,11... | collective-permute-start | bytes 3538952 | tf_op jit(solution)/shard_map/ppermute | solution.py:19
  316.3 78.8 %collective-permute-start.38 = (bf16[768,768]{1,0:T(8,128)(2,1)}, bf16[768,768]{1,0:T(8,128)(2,1)}, u32[]{:S(2)}, u32[]{:S(2)}) collective-permute-start(bf16[768,768]{1,0:T(8,128)(2,1)} %collective-permute-done.36), channel_id=1, source_target_pairs={{0,1},{1,0},{2,3},{3,2},{4,5},{5,4},{6,7},{7,6},{8,9},{9,8},{10,11... | collective-permute-start | bytes 3538952 | tf_op jit(solution)/shard_map/ppermute | solution.py:19
  341.1 56.9 %collective-permute-start.39 = (bf16[768,768]{1,0:T(8,128)(2,1)}, bf16[768,768]{1,0:T(8,128)(2,1)}, u32[]{:S(2)}, u32[]{:S(2)}) collective-permute-start(bf16[768,768]{1,0:T(8,128)(2,1)} %collective-permute-done.37), channel_id=1, source_target_pairs={{0,1},{1,0},{2,3},{3,2},{4,5},{5,4},{6,7},{7,6},{8,9},{9,8},{10,11... | collective-permute-start | bytes 3538952 | tf_op jit(solution)/shard_map/ppermute | solution.py:19
  531.1 47.1 %collective-permute-start.68 = (bf16[768,768]{1,0:T(8,128)(2,1)}, bf16[768,768]{1,0:T(8,128)(2,1)}, u32[]{:S(2)}, u32[]{:S(2)}) collective-permute-start(bf16[768,768]{1,0:T(8,128)(2,1)} %fusion.70), channel_id=1, source_target_pairs={{0,1},{1,0},{2,3},{3,2},{4,5},{5,4},{6,7},{7,6},{8,9},{9,8},{10,11... | collective-permute-start | bytes 3538952 | tf_op jit(solution)/shard_map/ppermute | solution.py:19
  534.2 169.9 %collective-permute-start.67 = (bf16[768,768]{1,0:T(8,128)(2,1)}, bf16[768,768]{1,0:T(8,128)(2,1)}, u32[]{:S(2)}, u32[]{:S(2)}) collective-permute-start(bf16[768,768]{1,0:T(8,128)(2,1)} %fusion.69), channel_id=1, source_target_pairs={{0,1},{1,0},{2,3},{3,2},{4,5},{5,4},{6,7},{7,6},{8,9},{9,8},{10,11... | collective-permute-start | bytes 3538952 | tf_op jit(solution)/shard_map/ppermute | solution.py:19
  534.2 49.4 %collective-permute-start.61 = (bf16[768,768]{1,0:T(8,128)(2,1)}, bf16[768,768]{1,0:T(8,128)(2,1)}, u32[]{:S(2)}, u32[]{:S(2)}) collective-permute-start(bf16[768,768]{1,0:T(8,128)(2,1)} %convolution_convert_fusion.4), channel_id=1, source_target_pairs={{0,1},{1,0},{2,3},{3,2},{4,5},{5,4},{6,7},{7,6},{8,9},{9,8},{10,11... | collective-permute-start | bytes 3538952 | tf_op jit(solution)/shard_map/ppermute | solution.py:19
  534.7 186.3 %collective-permute-start.60 = (bf16[768,768]{1,0:T(8,128)(2,1)}, bf16[768,768]{1,0:T(8,128)(2,1)}, u32[]{:S(2)}, u32[]{:S(2)}) collective-permute-start(bf16[768,768]{1,0:T(8,128)(2,1)} %convolution_convert_fusion.6), channel_id=1, source_target_pairs={{0,1},{1,0},{2,3},{3,2},{4,5},{5,4},{6,7},{7,6},{8,9},{9,8},{10,11... | collective-permute-start | bytes 3538952 | tf_op jit(solution)/shard_map/ppermute | solution.py:19
  537.3 50.7 %collective-permute-start.54 = (bf16[768,768]{0,1:T(8,128)(2,1)}, bf16[768,768]{0,1:T(8,128)(2,1)}, u32[]{:S(2)}, u32[]{:S(2)}) collective-permute-start(bf16[768,768]{0,1:T(8,128)(2,1)} %pad_maximum_fusion.11), channel_id=1, source_target_pairs={{0,1},{1,0},{2,3},{3,2},{4,5},{5,4},{6,7},{7,6},{8,9},{9,8},{10,11... | collective-permute-start | bytes 3538952 | tf_op jit(solution)/shard_map/ppermute | solution.py:19
  551.9 38.7 %all-to-all-start.3 = ((bf16[8,98,768]{2,1,0:T(8,128)(2,1)}), bf16[8,98,768]{2,1,0:T(8,128)(2,1)}, u32[]{:S(2)}, u32[]{:S(2)}) async-start(bf16[8,98,768]{2,1,0:T(8,128)(2,1)} %reshape.431), calls=%async_computation.3 | async-start | bytes 2555904 | tf_op jit(solution)/shard_map/all_to_all | solution.py:76
  582.1 135.3 %collective-permute-start.69 = (bf16[768,768]{1,0:T(8,128)(2,1)}, bf16[768,768]{1,0:T(8,128)(2,1)}, u32[]{:S(2)}, u32[]{:S(2)}) collective-permute-start(bf16[768,768]{1,0:T(8,128)(2,1)} %fusion.45), channel_id=1, source_target_pairs={{0,2},{1,3},{2,0},{3,1},{4,6},{5,7},{6,4},{7,5},{8,10},{9,11},{10,... | collective-permute-start | bytes 3538952 | tf_op jit(solution)/shard_map/ppermute | solution.py:19
  587.4 133.9 %collective-permute-start.62 = (bf16[768,768]{1,0:T(8,128)(2,1)}, bf16[768,768]{1,0:T(8,128)(2,1)}, u32[]{:S(2)}, u32[]{:S(2)}) collective-permute-start(bf16[768,768]{1,0:T(8,128)(2,1)} %add_convert_fusion.8), channel_id=1, source_target_pairs={{0,2},{1,3},{2,0},{3,1},{4,6},{5,7},{6,4},{7,5},{8,10},{9,11},{10,... | collective-permute-start | bytes 3538952 | tf_op jit(solution)/shard_map/ppermute | solution.py:19
  590.6 119.1 %all-to-all-start.1 = ((bf16[8,98,768]{2,1,0:T(8,128)(2,1)}), bf16[8,98,768]{2,1,0:T(8,128)(2,1)}, u32[]{:S(2)}, u32[]{:S(2)}) async-start(bf16[8,98,768]{2,1,0:T(8,128)(2,1)} %reshape.424), calls=%async_computation.1 | async-start | bytes 2555904 | tf_op jit(solution)/shard_map/all_to_all | solution.py:76
  704.1 9.9 %collective-permute-start.44 = (f32[24,96]{1,0:T(8,128)S(1)}, f32[24,96]{1,0:T(8,128)S(1)}, u32[]{:S(2)}, u32[]{:S(2)}) collective-permute-start(f32[24,96]{1,0:T(8,128)S(1)} %get-tuple-element.167), channel_id=1, source_target_pairs={{0,16},{4,20},{8,24},{12,28},{16,0},{20,4},{24,8},{28,12},{1,17},{... | collective-permute-start | bytes 27656 | tf_op jit(solution)/shard_map/ppermute | solution.py:19
  714.0 11.9 %collective-permute-start.53 = (bf16[768,768]{0,1:T(8,128)(2,1)S(1)}, bf16[768,768]{0,1:T(8,128)(2,1)}, u32[]{:S(2)}, u32[]{:S(2)}) collective-permute-start(bf16[768,768]{0,1:T(8,128)(2,1)S(1)} %copy-done.70), channel_id=1, source_target_pairs={{0,1},{1,0},{2,3},{3,2},{4,5},{5,4},{6,7},{7,6},{8,9},{9,8},{10,11... | collective-permute-start | bytes 3538952 | tf_op jit(solution)/shard_map/ppermute | solution.py:19
  714.0 28.5 %collective-permute-start.55 = (bf16[768,768]{0,1:T(8,128)(2,1)S(1)}, bf16[768,768]{0,1:T(8,128)(2,1)}, u32[]{:S(2)}, u32[]{:S(2)}) collective-permute-start(bf16[768,768]{0,1:T(8,128)(2,1)S(1)} %copy-done.69), channel_id=1, source_target_pairs={{0,2},{1,3},{2,0},{3,1},{4,6},{5,7},{6,4},{7,5},{8,10},{9,11},{10,... | collective-permute-start | bytes 3538952 | tf_op jit(solution)/shard_map/ppermute | solution.py:19
  717.4 29.3 %collective-permute-start.47 = (bf16[768,768]{0,1:T(8,128)(2,1)}, bf16[768,768]{0,1:T(8,128)(2,1)S(1)}, u32[]{:S(2)}, u32[]{:S(2)}) collective-permute-start(bf16[768,768]{0,1:T(8,128)(2,1)} %pad_maximum_fusion.9), channel_id=1, source_target_pairs={{0,1},{1,0},{2,3},{3,2},{4,5},{5,4},{6,7},{7,6},{8,9},{9,8},{10,11... | collective-permute-start | bytes 3538952 | tf_op jit(solution)/shard_map/ppermute | solution.py:19
  721.0 46.3 %collective-permute-start.46 = (bf16[768,768]{0,1:T(8,128)(2,1)}, bf16[768,768]{0,1:T(8,128)(2,1)}, u32[]{:S(2)}, u32[]{:S(2)}) collective-permute-start(bf16[768,768]{0,1:T(8,128)(2,1)} %pad_maximum_fusion.8), channel_id=1, source_target_pairs={{0,1},{1,0},{2,3},{3,2},{4,5},{5,4},{6,7},{7,6},{8,9},{9,8},{10,11... | collective-permute-start | bytes 3538952 | tf_op jit(solution)/shard_map/ppermute | solution.py:19
  721.3 30.3 %collective-permute-start.70 = (bf16[4,96,768]{2,1,0:T(8,128)(2,1)}, bf16[4,96,768]{2,1,0:T(8,128)(2,1)}, u32[]{:S(2)}, u32[]{:S(2)}) collective-permute-start(bf16[4,96,768]{2,1,0:T(8,128)(2,1)} %fusion.114), channel_id=1, source_target_pairs={{0,4},{4,0},{8,12},{12,8},{16,20},{20,16},{24,28},{28,24},{1,5},{5... | collective-permute-start | bytes 1769480 | tf_op jit(solution)/shard_map/ppermute | solution.py:19
  725.9 27.7 %collective-permute-start.63 = (bf16[4,96,768]{2,1,0:T(8,128)(2,1)}, bf16[4,96,768]{2,1,0:T(8,128)(2,1)}, u32[]{:S(2)}, u32[]{:S(2)}) collective-permute-start(bf16[4,96,768]{2,1,0:T(8,128)(2,1)} %fusion.113), channel_id=1, source_target_pairs={{0,4},{4,0},{8,12},{12,8},{16,20},{20,16},{24,28},{28,24},{1,5},{5... | collective-permute-start | bytes 1769480 | tf_op jit(solution)/shard_map/ppermute | solution.py:19
  748.4 27.5 %collective-permute-start.48 = (bf16[768,768]{0,1:T(8,128)(2,1)S(1)}, bf16[768,768]{0,1:T(8,128)(2,1)S(1)}, u32[]{:S(2)}, u32[]{:S(2)}) collective-permute-start(bf16[768,768]{0,1:T(8,128)(2,1)S(1)} %add_convert_fusion.10), channel_id=1, source_target_pairs={{0,2},{1,3},{2,0},{3,1},{4,6},{5,7},{6,4},{7,5},{8,10},{9,11},{10,... | collective-permute-start | bytes 3538952 | tf_op jit(solution)/shard_map/ppermute | solution.py:19
  750.0 14.6 %collective-permute-start.56 = (bf16[4,96,768]{2,1,0:T(8,128)(2,1)S(1)}, bf16[4,96,768]{2,1,0:T(8,128)(2,1)S(1)}, u32[]{:S(2)}, u32[]{:S(2)}) collective-permute-start(bf16[4,96,768]{2,1,0:T(8,128)(2,1)S(1)} %fusion.112), channel_id=1, source_target_pairs={{0,4},{4,0},{8,12},{12,8},{16,20},{20,16},{24,28},{28,24},{1,5},{5... | collective-permute-start | bytes 1769480 | tf_op jit(solution)/shard_map/ppermute | solution.py:19
  753.6 27.5 %collective-permute-start.71 = (bf16[96,768]{1,0:T(8,128)(2,1)}, bf16[96,768]{1,0:T(8,128)(2,1)}, u32[]{:S(2)}, u32[]{:S(2)}) collective-permute-start(bf16[96,768]{1,0:T(8,128)(2,1)} %get-tuple-element.139), channel_id=1, source_target_pairs={{0,8},{4,12},{8,0},{12,4},{16,24},{20,28},{24,16},{28,20},{1,9},{5... | collective-permute-start | bytes 442376 | tf_op jit(solution)/shard_map/ppermute | solution.py:19
  753.9 29.3 %collective-permute-start.72 = (bf16[96,768]{1,0:T(8,128)(2,1)}, bf16[96,768]{1,0:T(8,128)(2,1)}, u32[]{:S(2)}, u32[]{:S(2)}) collective-permute-start(bf16[96,768]{1,0:T(8,128)(2,1)} %get-tuple-element.141), channel_id=1, source_target_pairs={{0,16},{4,20},{8,24},{12,28},{16,0},{20,4},{24,8},{28,12},{1,17},{... | collective-permute-start | bytes 442376 | tf_op jit(solution)/shard_map/ppermute | solution.py:19
  764.6 20.0 %collective-permute-start.73 = (bf16[96,768]{1,0:T(8,128)(2,1)}, bf16[96,768]{1,0:T(8,128)(2,1)}, u32[]{:S(2)}, u32[]{:S(2)}) collective-permute-start(bf16[96,768]{1,0:T(8,128)(2,1)} %get-tuple-element.140), channel_id=1, source_target_pairs={{0,24},{4,28},{8,16},{12,20},{16,8},{20,12},{24,0},{28,4},{1,25},{... | collective-permute-start | bytes 442376 | tf_op jit(solution)/shard_map/ppermute | solution.py:19
  767.3 20.8 %collective-permute-start.64 = (bf16[96,768]{1,0:T(8,128)(2,1)}, bf16[96,768]{1,0:T(8,128)(2,1)}, u32[]{:S(2)}, u32[]{:S(2)}) collective-permute-start(bf16[96,768]{1,0:T(8,128)(2,1)} %get-tuple-element.142), channel_id=1, source_target_pairs={{0,8},{4,12},{8,0},{12,4},{16,24},{20,28},{24,16},{28,20},{1,9},{5... | collective-permute-start | bytes 442376 | tf_op jit(solution)/shard_map/ppermute | solution.py:19
  775.9 13.0 %collective-permute-start.65 = (bf16[96,768]{1,0:T(8,128)(2,1)}, bf16[96,768]{1,0:T(8,128)(2,1)}, u32[]{:S(2)}, u32[]{:S(2)}) collective-permute-start(bf16[96,768]{1,0:T(8,128)(2,1)} %get-tuple-element.144), channel_id=1, source_target_pairs={{0,16},{4,20},{8,24},{12,28},{16,0},{20,4},{24,8},{28,12},{1,17},{... | collective-permute-start | bytes 442376 | tf_op jit(solution)/shard_map/ppermute | solution.py:19
  781.1 9.9 %collective-permute-start.66 = (bf16[96,768]{1,0:T(8,128)(2,1)}, bf16[96,768]{1,0:T(8,128)(2,1)S(1)}, u32[]{:S(2)}, u32[]{:S(2)}) collective-permute-start(bf16[96,768]{1,0:T(8,128)(2,1)} %get-tuple-element.143), channel_id=1, source_target_pairs={{0,24},{4,28},{8,16},{12,20},{16,8},{20,12},{24,0},{28,4},{1,25},{... | collective-permute-start | bytes 442376 | tf_op jit(solution)/shard_map/ppermute | solution.py:19
  784.6 16.4 %collective-permute-start.49 = (bf16[4,96,768]{2,1,0:T(8,128)(2,1)S(1)}, bf16[4,96,768]{2,1,0:T(8,128)(2,1)S(1)}, u32[]{:S(2)}, u32[]{:S(2)}) collective-permute-start(bf16[4,96,768]{2,1,0:T(8,128)(2,1)S(1)} %fusion.111), channel_id=1, source_target_pairs={{0,4},{4,0},{8,12},{12,8},{16,20},{20,16},{24,28},{28,24},{1,5},{5... | collective-permute-start | bytes 1769480 | tf_op jit(solution)/shard_map/ppermute | solution.py:19
  788.1 12.9 %collective-permute-start.58 = (bf16[96,768]{1,0:T(8,128)(2,1)S(1)}, bf16[96,768]{1,0:T(8,128)(2,1)S(1)}, u32[]{:S(2)}, u32[]{:S(2)}) collective-permute-start(bf16[96,768]{1,0:T(8,128)(2,1)S(1)} %copy-done.105), channel_id=1, source_target_pairs={{0,16},{4,20},{8,24},{12,28},{16,0},{20,4},{24,8},{28,12},{1,17},{... | collective-permute-start | bytes 442376 | tf_op jit(solution)/shard_map/ppermute | solution.py:19
  789.0 12.0 %collective-permute-start.59 = (bf16[96,768]{1,0:T(8,128)(2,1)S(1)}, bf16[96,768]{1,0:T(8,128)(2,1)S(1)}, u32[]{:S(2)}, u32[]{:S(2)}) collective-permute-start(bf16[96,768]{1,0:T(8,128)(2,1)S(1)} %copy-done.104), channel_id=1, source_target_pairs={{0,24},{4,28},{8,16},{12,20},{16,8},{20,12},{24,0},{28,4},{1,25},{... | collective-permute-start | bytes 442376 | tf_op jit(solution)/shard_map/ppermute | solution.py:19
  804.0 13.3 %collective-permute-start.51 = (bf16[96,768]{1,0:T(8,128)(2,1)S(1)}, bf16[96,768]{1,0:T(8,128)(2,1)S(1)}, u32[]{:S(2)}, u32[]{:S(2)}) collective-permute-start(bf16[96,768]{1,0:T(8,128)(2,1)S(1)} %get-tuple-element.150), channel_id=1, source_target_pairs={{0,16},{4,20},{8,24},{12,28},{16,0},{20,4},{24,8},{28,12},{1,17},{... | collective-permute-start | bytes 442376 | tf_op jit(solution)/shard_map/ppermute | solution.py:19
  804.7 12.6 %collective-permute-start.52 = (bf16[96,768]{1,0:T(8,128)(2,1)S(1)}, bf16[96,768]{1,0:T(8,128)(2,1)S(1)}, u32[]{:S(2)}, u32[]{:S(2)}) collective-permute-start(bf16[96,768]{1,0:T(8,128)(2,1)S(1)} %get-tuple-element.149), channel_id=1, source_target_pairs={{0,24},{4,28},{8,16},{12,20},{16,8},{20,12},{24,0},{28,4},{1,25},{... | collective-permute-start | bytes 442376 | tf_op jit(solution)/shard_map/ppermute | solution.py:19
  (159 other events, 1087.9 us)

commit v2 on v1

v2 whole, which is shorter than its diff:
```python
import jax
import jax.numpy as jnp
from jax import lax
from jax.experimental import pallas as pl
from jax.experimental.pallas import tpu as pltpu
from jax.sharding import PartitionSpec as P


HEAD_DIM = 64
PATCHES = 196
FRAMES = 16
FRAME_RUN = 2
EPSILON = 1e-06
RUNS = FRAMES // FRAME_RUN

BF = jnp.bfloat16
F32 = jnp.float32

SCALE = HEAD_DIM**-0.5
GROUP = 8
VMEM = pltpu.VMEM
LIMIT = 62 * 1024 * 1024


def cost(time_us):
    return pl.CostEstimate(flops=int(time_us * 1e9), bytes_accessed=0, transcendentals=0)


def norm_parts(rows):
    center = rows - jnp.mean(rows, axis=-1, keepdims=True)
    scale = lax.rsqrt(jnp.mean(center * center, axis=-1, keepdims=True) + EPSILON)
    return center * scale, scale


def norm(rows, gain, shift):
    hat, _ = norm_parts(rows)
    return (hat * gain + shift).astype(BF)


def norm_back(rows, gain, grad):
    hat, scale = norm_parts(rows)
    back = grad * gain
    inner = jnp.mean(back * hat, axis=-1, keepdims=True)
    result = scale * (back - jnp.mean(back, axis=-1, keepdims=True) - hat * inner)
    gain_sum = jnp.sum(grad * hat, axis=0, keepdims=True)
    return result, gain_sum, jnp.sum(grad, axis=0, keepdims=True)


def dot(left, right, dims=((1,), (0,))):
    return lax.dot_general(left, right, (dims, ((), ())), preferred_element_type=F32)


NT = ((1,), (1,))
TN = ((0,), (0,))


def softmax(scores, mask):
    if mask is not None:
        scores = jnp.where(mask, scores, -1e30)
    powers = jnp.exp(scores - jnp.max(scores, axis=-1, keepdims=True))
    return powers / jnp.sum(powers, axis=-1, keepdims=True)


def head_slices(head, cols):
    return [slice(which * cols + head * HEAD_DIM, which * cols + (head + 1) * HEAD_DIM) for which in range(4)]


def attend(block, cols, mask):
    results = []
    for head in range(cols // HEAD_DIM):
        q_at, k_at, v_at, _ = head_slices(head, cols)
        scores = dot(block[:, q_at], block[:, k_at], NT) * SCALE
        weights = softmax(scores, mask).astype(BF)
        results.append(dot(weights, block[:, v_at]).astype(BF))
    return results


def attend_back(block, grad_out, cols, mask, store):
    for head in range(cols // HEAD_DIM):
        q_at, k_at, v_at, _ = head_slices(head, cols)
        queries, key_rows, value_rows = block[:, q_at], block[:, k_at], block[:, v_at]
        grad = grad_out[:, head * HEAD_DIM : (head + 1) * HEAD_DIM]
        weights = softmax(dot(queries, key_rows, NT) * SCALE, mask)
        grad_w = dot(grad, value_rows, NT)
        inner = jnp.sum(weights * grad_w, axis=-1, keepdims=True)
        grad_s = (weights * (grad_w - inner)).astype(BF)
        store(q_at, (dot(grad_s, key_rows) * SCALE).astype(BF))
        store(k_at, (dot(grad_s, queries, TN) * SCALE).astype(BF))
        store(v_at, dot(weights.astype(BF), grad, TN).astype(BF))


def only_out(block, cut, skip):
    last = block[:, cut:]
    place = lax.broadcasted_iota(jnp.int32, last.shape, 1)
    return jnp.where(place < skip, jnp.zeros_like(last), last)


def fetch(sources, target, sem):
    copies = [
        pltpu.make_async_copy(item, target.at[r], sem.at[r]) for r, item in enumerate(sources)
    ]
    for copy in copies:
        copy.start()
    for copy in copies:
        copy.wait()


def cut_of(cols):
    cut = 3 * cols // 256 * 256
    return cut, 3 * cols - cut


def spatial_forward(rows, vecs, bias, packs, micro, share):
    frames, patches, width = rows.shape
    full = packs[0].shape[1]
    cols = full // 4
    cut, skip = cut_of(cols)
    padded = -(-share // GROUP) * GROUP
    pieces = patches // share

    def kernel(tok, vec, bia, w0, w1, w2, w3, a_out, x_out, h_out, wbuf, acc, sem):
        @pl.when(pl.program_id(0) == 0)
        def _():
            fetch((w0, w1, w2, w3), wbuf, sem)

        source = tok[0].astype(F32)
        normed = norm(source, vec[0:1], vec[1:2])
        a_out[0] = normed
        acc[...] = source + vec[2:3]

        def body(r, carry):
            x_out[0, r] = (dot(normed, wbuf[r]) + bia[r]).astype(BF)
            heads = attend(x_out[0, r], cols, None)
            for head, item in enumerate(heads):
                x_out[0, r, :, head_slices(head, cols)[3]] = item
            acc[...] += dot(only_out(x_out[0, r], cut, skip), wbuf[r, :, cut:], NT)
            return carry

        lax.fori_loop(0, 4, body, 0)
        h_out[...] = jnp.zeros_like(h_out)
        for piece in range(pieces):
            h_out[0, piece, 0, :share] = acc[piece * share : (piece + 1) * share].astype(BF)

    whole = pl.BlockSpec(memory_space=pl.ANY)
    return pl.pallas_call(
        kernel,
        name="spatial_forward",
        grid=(frames,),
        in_specs=[
            pl.BlockSpec((1, patches, width), lambda i: (i, 0, 0)),
            pl.BlockSpec(vecs.shape, lambda i: (0, 0)),
            pl.BlockSpec(bias.shape, lambda i: (0, 0, 0)),
            whole,
            whole,
            whole,
            whole,
        ],
        out_specs=[
            pl.BlockSpec((1, patches, width), lambda i: (i, 0, 0)),
            pl.BlockSpec((1, 4, patches, full), lambda i: (i, 0, 0, 0)),
            pl.BlockSpec(
                (1, pieces, 1, padded, width),
                lambda i: (i // FRAME_RUN, 0, i % FRAME_RUN, 0, 0),
            ),
        ],
        out_shape=[
            jax.ShapeDtypeStruct((frames, patches, width), BF),
            jax.ShapeDtypeStruct((frames, 4, patches, full), BF),
            jax.ShapeDtypeStruct((micro, pieces, FRAME_RUN, padded, width), BF),
        ],
        scratch_shapes=[
            VMEM((4, width, full), BF),
            VMEM((patches, width), F32),
            pltpu.SemaphoreType.DMA((4,)),
        ],
        cost_estimate=cost(30),
        compiler_params=pltpu.CompilerParams(vmem_limit_bytes=LIMIT),
    )(rows, vecs, bias, *packs)


def spatial_backward(rows, normed, kept, grad, vecs, packs, share):
    frames, patches, width = rows.shape
    full = packs[0].shape[1]
    cols = full // 4
    cut, skip = cut_of(cols)
    _, pieces, _, padded, _ = grad.shape

    def kernel(tok, nrm, x_in, g_in, vec, w0, w1, w2, w3, t_out, s_out, sums, b_out, wbuf, side, gbuf, acc, tot, sem):
        step = pl.program_id(0)

        @pl.when(step == 0)
        def _():
            fetch((w0, w1, w2, w3), wbuf, sem)
            tot[...] = jnp.zeros_like(tot)
            sums[...] = jnp.zeros_like(sums)
            b_out[...] = jnp.zeros_like(b_out)
            side[...] = jnp.zeros_like(side)

        for piece in range(pieces):
            gbuf[piece * share : (piece + 1) * share] = g_in[0, piece, 0, :share].astype(F32)
        grad_b = gbuf[...].astype(BF)
        acc[...] = jnp.zeros_like(acc)

        def body(r, carry):
            grad_o = dot(grad_b, wbuf[r, :, cut:])[:, skip:].astype(BF)

            def store(at, value):
                side[:, at] = value

            attend_back(x_in[0, r], grad_o, cols, None, store)
            acc[...] += dot(side[...], wbuf[r], NT)
            b_out[r] += jnp.sum(side[...].astype(F32), axis=0, keepdims=True)
            tot[r] += dot(nrm[0], side[...], TN)
            tot[r, :, cut:] += dot(grad_b, only_out(x_in[0, r], cut, skip), TN)
            return carry

        lax.fori_loop(0, 4, body, 0)
        back, gain_sum, shift_sum = norm_back(tok[0].astype(F32), vec[0:1], acc[...])
        t_out[0] = gbuf[...] + back
        sums[0:1] += gain_sum
        sums[1:2] += shift_sum

        @pl.when(step == frames - 1)
        def _():
            def last(r, carry):
                s_out[r] = tot[r].astype(BF)
                return carry

            lax.fori_loop(0, 4, last, 0)

    whole = pl.BlockSpec(memory_space=pl.ANY)
    frame = pl.BlockSpec((1, patches, width), lambda i: (i, 0, 0))
    return pl.pallas_call(
        kernel,
        name="spatial_backward",
        grid=(frames,),
        in_specs=[
            frame,
            frame,
            pl.BlockSpec((1, 4, patches, full), lambda i: (i, 0, 0, 0)),
            pl.BlockSpec(
                (1, pieces, 1, padded, width),
                lambda i: (i // FRAME_RUN, 0, i % FRAME_RUN, 0, 0),
            ),
            pl.BlockSpec(vecs.shape, lambda i: (0, 0)),
            whole,
            whole,
            whole,
            whole,
        ],
        out_specs=[
            frame,
            pl.BlockSpec((4, width, full), lambda i: (0, 0, 0)),
            pl.BlockSpec((8, width), lambda i: (0, 0)),
            pl.BlockSpec((4, 1, full), lambda i: (0, 0, 0)),
        ],
        out_shape=[
            jax.ShapeDtypeStruct((frames, patches, width), F32),
            jax.ShapeDtypeStruct((4, width, full), BF),
            jax.ShapeDtypeStruct((8, width), F32),
            jax.ShapeDtypeStruct((4, 1, full), F32),
        ],
        scratch_shapes=[
            VMEM((4, width, full), BF),
            VMEM((patches, full), BF),
            VMEM((patches, width), F32),
            VMEM((patches, width), F32),
            VMEM((4, width, full), F32),
            pltpu.SemaphoreType.DMA((4,)),
        ],
        cost_estimate=cost(50),
        compiler_params=pltpu.CompilerParams(vmem_limit_bytes=LIMIT),
    )(rows, normed, kept, grad, vecs, *packs)


def same_position(span):
    first = lax.broadcasted_iota(jnp.int32, (span, span), 0)
    second = lax.broadcasted_iota(jnp.int32, (span, span), 1)
    return first % GROUP == second % GROUP


def into_groups(source, target, groups):
    span = FRAMES * GROUP
    for at in range(groups):
        part = source[:, at * GROUP : (at + 1) * GROUP, :]
        target[at * span : (at + 1) * span] = part.reshape(span, part.shape[2])


def out_of_groups(source, stage, groups):
    span = FRAMES * GROUP
    for at in range(groups):
        part = source[at * span : (at + 1) * span]
        stage[:, at * GROUP : (at + 1) * GROUP, :] = part.reshape(FRAMES, GROUP, part.shape[1])


def whole_call(kernel, outs, scratch, *args):
    spaces = [pl.BlockSpec(memory_space=pltpu.VMEM if keep else pl.ANY) for keep, _ in args]
    return pl.pallas_call(
        kernel,
        in_specs=spaces,
        out_specs=[pl.BlockSpec(memory_space=pltpu.VMEM) for _ in outs],
        out_shape=[jax.ShapeDtypeStruct(shape, dtype) for shape, dtype in outs],
        scratch_shapes=scratch,
        cost_estimate=cost(45),
        compiler_params=pltpu.CompilerParams(vmem_limit_bytes=LIMIT),
    )(*[item for _, item in args])


def temporal_forward(block, vecs, bias, packs):
    frames, padded, width = block.shape
    full = packs[0].shape[1]
    cols = full // 4
    cut, skip = cut_of(cols)
    groups = padded // GROUP
    span = frames * GROUP
    rows = frames * padded

    def kernel(h_in, vec, bia, w0, w1, w2, w3, a_out, x_out, h_out, r_out, wbuf, stage, sem):
        fetch((w0, w1, w2, w3), wbuf, sem)
        stage[...] = h_in[...].astype(F32)
        into_groups(stage, h_out, groups)
        r_out[...] = h_out[...].astype(BF)
        a_out[...] = norm(h_out[...], vec[0:1], vec[1:2])
        h_out[...] += vec[2:3]
        mask = same_position(span)

        def body(r, carry):
            x_out[r] = (dot(a_out[...], wbuf[r]) + bia[r]).astype(BF)

            def inner(at, carry):
                here = pl.ds(pl.multiple_of(at * span, span), span)
                for head, item in enumerate(attend(x_out[r, here], cols, mask)):
                    x_out[r, here, head_slices(head, cols)[3]] = item
                return carry

            lax.fori_loop(0, groups, inner, 0)
            h_out[...] += dot(only_out(x_out[r], cut, skip), wbuf[r, :, cut:], NT)
            return carry

        lax.fori_loop(0, 4, body, 0)

    return whole_call(
        kernel,
        [((rows, width), BF), ((4, rows, full), BF), ((rows, width), F32), ((rows, width), BF)],
        [
            VMEM((4, width, full), BF),
            VMEM((frames, padded, width), F32),
            pltpu.SemaphoreType.DMA((4,)),
        ],
        (True, block),
        (True, vecs),
        (True, bias),
        *[(False, item) for item in packs],
    )


def feed_forward(h2, grad, vecs, up_bias, ups, downs):
    frames, padded, width = grad.shape
    rows = h2.shape[0]
    hidden = ups[0].shape[1]
    groups = padded // GROUP
    step = rows // 4

    def kernel(
        h_in, g_in, vec, bia, u0, u1, u2, u3, d0, d1, d2, d3,
        m_out, r_out, su_out, sd_out, sums, f_out,
        ubuf, dbuf, stage, dyb, am, act, pre, mix, dam, usem, dsem,
    ):
        fetch((u0, u1, u2, u3), ubuf, usem)
        fetch((d0, d1, d2, d3), dbuf, dsem)
        stage[...] = g_in[...].astype(F32)
        into_groups(stage, r_out, groups)
        dyb[...] = r_out[...].astype(BF)
        sums[...] = jnp.zeros_like(sums)
        sums[3:4] = jnp.sum(r_out[...], axis=0, keepdims=True)
        am[...] = norm(h_in[...], vec[0:1], vec[1:2])
        mix[...] = h_in[...] + vec[2:3]
        dam[...] = jnp.zeros_like(dam)

        def body(r, carry):
            def inner(at, total):
                here = pl.ds(pl.multiple_of(at * step, step), step)
                value = dot(am[here], ubuf[r]) + bia[r]
                half = 0.5 * (1.0 + lax.erf(value * 0.5**0.5))
                gate = (value * half).astype(BF)
                slope = half + value * jnp.exp(-0.5 * value * value) * 0.3989422804014327
                act[here] = gate
                mix[here] += dot(gate, dbuf[r], NT)
                grad_pre = (dot(dyb[here], dbuf[r]) * slope).astype(BF)
                pre[here] = grad_pre
                dam[here] += dot(grad_pre, ubuf[r], NT)
                return total + jnp.sum(grad_pre.astype(F32), axis=0, keepdims=True)

            f_out[r] = lax.fori_loop(0, 4, inner, jnp.zeros((1, hidden), F32))
            sd_out[r] = dot(dyb[...], act[...], TN).astype(BF)
            su_out[r] = dot(am[...], pre[...], TN).astype(BF)
            return carry

        lax.fori_loop(0, 4, body, 0)
        out_of_groups(mix, stage, groups)
        m_out[...] = stage[...].astype(BF)
        back, gain_sum, shift_sum = norm_back(h_in[...], vec[0:1], dam[...])
        r_out[...] += back
        sums[0:1] = gain_sum
        sums[1:2] = shift_sum
        sums[2:3] = jnp.sum(r_out[...], axis=0, keepdims=True)

    return whole_call(
        kernel,
        [
            ((frames, padded, width), BF),
            ((rows, width), F32),
            ((4, width, hidden), BF),
            ((4, width, hidden), BF),
            ((8, width), F32),
            ((4, 1, hidden), F32),
        ],
        [
            VMEM((4, width, hidden), BF),
            VMEM((4, width, hidden), BF),
            VMEM((frames, padded, width), F32),
            VMEM((rows, width), BF),
            VMEM((rows, width), BF),
            VMEM((rows, hidden), BF),
            VMEM((rows, hidden), BF),
            VMEM((rows, width), F32),
            VMEM((rows, width), F32),
            pltpu.SemaphoreType.DMA((4,)),
            pltpu.SemaphoreType.DMA((4,)),
        ],
        (True, h2),
        (True, grad),
        (True, vecs),
        (True, up_bias),
        *[(False, item) for item in ups],
        *[(False, item) for item in downs],
    )


def temporal_backward(grad, h1, normed, kept, vecs, packs, padded):
    rows, width = grad.shape
    full = packs[0].shape[1]
    cols = full // 4
    cut, skip = cut_of(cols)
    groups = padded // GROUP
    span = FRAMES * GROUP

    def kernel(g_in, h_in, nrm, x_in, vec, w0, w1, w2, w3, t_out, s_out, sums, b_out, wbuf, side, grad_b, grad_o, acc, stage, sem):
        fetch((w0, w1, w2, w3), wbuf, sem)
        grad_b[...] = g_in[...].astype(BF)
        acc[...] = jnp.zeros_like(acc)
        side[...] = jnp.zeros_like(side)
        sums[...] = jnp.zeros_like(sums)
        mask = same_position(span)

        def body(r, carry):
            grad_o[...] = dot(grad_b[...], wbuf[r, :, cut:]).astype(BF)

            def inner(at, carry):
                here = pl.ds(pl.multiple_of(at * span, span), span)

                def store(cols_at, value):
                    side[here, cols_at] = value

                attend_back(x_in[r, here], grad_o[here][:, skip:], cols, mask, store)
                return carry

            lax.fori_loop(0, groups, inner, 0)
            acc[...] += dot(side[...], wbuf[r], NT)
            b_out[r] = jnp.sum(side[...].astype(F32), axis=0, keepdims=True)
            first = dot(nrm[...], side[...], TN)
            second = dot(grad_b[...], only_out(x_in[r], cut, skip), TN)
            s_out[r, :, :cut] = first[:, :cut].astype(BF)
            s_out[r, :, cut:] = (first[:, cut:] + second).astype(BF)
            return carry

        lax.fori_loop(0, 4, body, 0)
        back, gain_sum, shift_sum = norm_back(h_in[...].astype(F32), vec[0:1], acc[...])
        acc[...] = g_in[...] + back
        sums[0:1] = gain_sum
        sums[1:2] = shift_sum
        sums[2:3] = jnp.sum(acc[...], axis=0, keepdims=True)
        out_of_groups(acc, stage, groups)
        t_out[...] = stage[...].astype(BF)

    return whole_call(
        kernel,
        [
            ((FRAMES, padded, width), BF),
            ((4, width, full), BF),
            ((8, width), F32),
            ((4, 1, full), F32),
        ],
        [
            VMEM((4, width, full), BF),
            VMEM((rows, full), BF),
            VMEM((rows, width), BF),
            VMEM((rows, full - cut), BF),
            VMEM((rows, width), F32),
            VMEM((FRAMES, padded, width), F32),
            pltpu.SemaphoreType.DMA((4,)),
        ],
        (True, grad),
        (True, h1),
        (True, normed),
        (True, kept),
        (True, vecs),
        *[(False, item) for item in packs],
    )


def assemble(pieces, me, rows):
    count = len(pieces)
    width = pieces[0].shape[1]
    rest = pieces[0].shape[0] - rows

    def kernel(me_ref, *refs):
        ins, outs = refs[:count], refs[count:]
        for bits in range(count):
            at = me_ref[0] ^ bits
            outs[0][pl.ds(pl.multiple_of(at * rows, rows), rows)] = ins[bits][:rows]
            if rest:
                outs[1][at] = ins[bits][rows:]

    shapes = [jax.ShapeDtypeStruct((count * rows, width), pieces[0].dtype)]
    if rest:
        shapes.append(jax.ShapeDtypeStruct((count, rest, width), pieces[0].dtype))
    spec = pl.BlockSpec(memory_space=pltpu.VMEM)
    return pl.pallas_call(
        kernel,
        name="assemble",
        in_specs=[pl.BlockSpec(memory_space=pltpu.SMEM)] + [spec] * count,
        out_specs=[spec] * len(shapes),
        out_shape=shapes,
    )(me.reshape(1), *pieces)


def swap(block, axis, bits):
    size = lax.axis_size(axis)
    return lax.ppermute(block, axis, [(i, i ^ bits) for i in range(size)])


def gather_wide(shard, rows):
    count = lax.axis_size("wide")
    if count != 8:
        whole = lax.all_gather(shard, "wide", axis=0)
        return whole[:, :rows].reshape(count * rows, -1), whole[:, rows:]
    pieces = {0: shard, 1: swap(shard, "wide", 1)}
    for bits in (6, 4, 2):
        pieces[bits] = swap(shard, "wide", bits)
    for bits in (6, 4, 2):
        pieces[bits ^ 1] = swap(pieces[bits], "wide", 1)
    result = assemble([pieces[bits] for bits in range(count)], lax.axis_index("wide"), rows)
    return result[0], result[1] if len(result) > 1 else None


def gather_tensor(block):
    far = swap(block, "tensor", 2)
    near = swap(block, "tensor", 1)
    return [block, near, far, swap(far, "tensor", 1)]


def reduce_all(parts):
    near = parts[0].astype(F32) + swap(parts[1], "tensor", 1).astype(F32)
    far = parts[2].astype(F32) + swap(parts[3], "tensor", 1).astype(F32)
    total = near + swap(far.astype(BF), "tensor", 2).astype(F32)
    return reduce_wide(total, BF)


def reduce_wide(total, link):
    count = lax.axis_size("wide")
    if count != 8:
        return lax.psum_scatter(total, "wide", scatter_dimension=0, tiled=True)
    me = lax.axis_index("wide")
    grid = total.reshape(4, 2, total.shape[0] // 8, total.shape[1])
    mine = lax.dynamic_index_in_dim(grid, me & 1, 1, keepdims=False)
    other = lax.dynamic_index_in_dim(grid, 1 - (me & 1), 1, keepdims=False)
    half = mine + swap(other.astype(link), "wide", 1).astype(F32)
    place = me >> 1
    result = lax.dynamic_index_in_dim(half, place, 0, keepdims=False)
    for bits in (1, 2, 3):
        piece = lax.dynamic_index_in_dim(half, place ^ bits, 0, keepdims=False)
        result = result + swap(piece.astype(link), "wide", bits * 2).astype(F32)
    return result


def exchange(block):
    count = lax.axis_size("wide")
    stride = count // RUNS
    groups = [[run * stride + clip for run in range(RUNS)] for clip in range(stride)]
    return lax.all_to_all(
        block, "wide", split_axis=0, concat_axis=0, tiled=True, axis_index_groups=groups
    )


def layer(
    tokens, cotangent, ln_gain, biases, fc1_bias, w_qkv_s, w_out_s, w_qkv_t, w_out_t, w_up, w_down
):
    micro, row_count, width = tokens.shape
    wide_count = lax.axis_size("wide")
    me_t = lax.axis_index("tensor")
    cols = w_qkv_s.shape[2]
    hidden = w_up.shape[1]
    slim = ln_gain.shape[1]
    share = micro * PATCHES // RUNS
    cut = PATCHES // share
    padded = -(-share // GROUP) * GROUP
    assert row_count == FRAME_RUN * PATCHES and lax.axis_size("tensor") == 4
    assert wide_count % RUNS == 0 and share * cut == PATCHES

    def pack(w_qkv, w_out):
        return jnp.concatenate([w_qkv[0], w_qkv[1], w_qkv[2], w_out.T], axis=1)

    small = jnp.concatenate([ln_gain, biases, fc1_bias.reshape(-1, slim)], axis=0)
    extra = small.shape[0]
    below = -(-small.size // (8 * 4 * cols)) * 8
    small = jnp.pad(small.reshape(-1), (0, below * 4 * cols - small.size))
    first = jnp.concatenate([pack(w_qkv_s, w_out_s), small.reshape(below, 4 * cols)], axis=0)
    whole_s, small = gather_wide(first, w_qkv_s.shape[1])
    pack_s = gather_tensor(whole_s)
    pack_t, pack_u, pack_d = [
        gather_tensor(gather_wide(shard, shard.shape[0])[0])
        for shard in (pack(w_qkv_t, w_out_t), w_up, w_down.T)
    ]

    small = small.reshape(wide_count, -1)[:, : extra * slim]
    small = small.reshape(wide_count, extra, slim).astype(F32)
    vectors = small[:, :13].swapaxes(0, 1).reshape(13, width)
    perm = me_t ^ jnp.arange(4)
    up_bias = small[:, 13:].reshape(4, 1, hidden)[perm]
    cut_cols = jnp.concatenate([vectors[6:8], vectors[9:11]]).reshape(4, 4, cols)[:, perm]
    gap = jnp.zeros((4, cols), F32)
    bias_s, bias_t = [
        jnp.concatenate([cut_cols[i], gap, cut_cols[i + 1], gap], axis=1)[:, None]
        for i in (0, 2)
    ]

    def vecs(*rows):
        return jnp.stack([vectors[i] for i in rows])

    frames = tokens.reshape(micro * FRAME_RUN, PATCHES, width)
    dy = cotangent.reshape(micro, FRAME_RUN, cut, share, width).swapaxes(1, 2)
    dy = jnp.pad(dy, ((0, 0), (0, 0), (0, 0), (0, padded - share), (0, 0)))
    dy = exchange(dy.reshape(RUNS, FRAME_RUN, padded, width)).reshape(FRAMES, padded, width)

    a_s, kept_s, h1 = spatial_forward(frames, vecs(0, 3, 8), bias_s, pack_s, micro, share)
    h1 = exchange(h1.reshape(RUNS, FRAME_RUN, padded, width)).reshape(FRAMES, padded, width)
    a_t, kept_t, h2, h1 = temporal_forward(h1, vecs(1, 4, 11), bias_t, pack_t)
    mixed, dh2, part_u, part_d, sums_m, sum_fc1 = feed_forward(
        h2, dy, vecs(2, 5, 12), up_bias, pack_u, pack_d
    )
    mixed = exchange(mixed.reshape(RUNS, FRAME_RUN, padded, width))
    mixed = mixed.reshape(micro, cut, FRAME_RUN, padded, width)[:, :, :, :share].swapaxes(1, 2)
    grad_d = reduce_all(part_d)
    grad_u = reduce_all(part_u)
    dh1, part_t, sums_t, side_t = temporal_backward(
        dh2, h1, a_t, kept_t, vecs(1, 4), pack_t, padded
    )
    dh1 = exchange(dh1.reshape(RUNS, FRAME_RUN, padded, width))
    dh1 = dh1.reshape(micro, cut, FRAME_RUN, padded, width)
    grad_t = reduce_all(part_t)
    grad_tokens, part_s, sums_s, side_s = spatial_backward(
        frames, a_s, kept_s, dh1, vecs(0, 3), pack_s, share
    )
    grad_s = reduce_all(part_s)

    sides = jnp.stack([side_s, side_t]).reshape(2, 4, 4, cols)[:, perm]
    sides = sides.swapaxes(1, 2).reshape(2, 4, width)
    rows = [sums_s[0:1], sums_t[0:1], sums_m[0:1], sums_s[1:2], sums_t[1:2], sums_m[1:2]]
    rows += [sides[0, 0:1], sides[0, 2:3], sums_t[2:3], sides[1, 0:1], sides[1, 2:3]]
    rows += [sums_m[2:3], sums_m[3:4]]
    table = jnp.concatenate(rows).reshape(13, wide_count, slim).swapaxes(0, 1)
    fc1 = sum_fc1[:, 0][perm].reshape(wide_count, extra - 13, slim)
    table = jnp.concatenate(
        [table, fc1, jnp.zeros((wide_count, -extra % 8, slim), F32)], axis=1
    )
    table = table.reshape(-1, slim)
    table = table + swap(table, "tensor", 1)
    table = table + swap(table, "tensor", 2)
    table = reduce_wide(table, F32)

    def unpack(total):
        w_qkv = jnp.stack([total[:, i * cols : (i + 1) * cols] for i in range(3)])
        return w_qkv, total[:, 3 * cols :].T

    qkv_s, out_s = unpack(grad_s)
    qkv_t, out_t = unpack(grad_t)
    return (
        mixed.reshape(tokens.shape),
        grad_tokens.reshape(tokens.shape),
        table[:3],
        table[3:13],
        table[13:extra].reshape(-1),
        qkv_s,
        out_s,
        qkv_t,
        out_t,
        grad_u,
        grad_d.T,
    )


def solution(mesh):
    specs = (
        P(None, ("wide", "tensor"), None),
        P(None, ("wide", "tensor"), None),
        P(None, "wide"),
        P(None, "wide"),
        P("wide"),
        P(None, "wide", "tensor"),
        P("tensor", "wide"),
        P(None, "wide", "tensor"),
        P("tensor", "wide"),
        P("wide", "tensor"),
        P("tensor", "wide"),
    )
    return jax.shard_map(layer, mesh=mesh, in_specs=specs, out_specs=specs, check_vma=False)
```

time: 826 us -> 639 us (0.77)
  Pallas kernels: 0 us -> 267 us
  matrix products: 214 us -> 0 us
  local copies, waits for them, and re-layouts: 206 us -> 48.7 us
  other arithmetic: 90.2 us -> 33.9 us
  blocking collectives: 52.3 us -> 0 us
  waiting for transfers between devices: 150 us -> 171 us
    pallas_call x0 -> x9, Pallas kernels: none -> 267 us  [the longest x3 169 us: whole_call(): pl.pallas_call(kernel, in_specs=spaces, out_specs=[pl.BlockSpec(memory_sp...]
    dot_general x84 -> x0, matrix products: 214 us -> none  [the longest x72 166 us: dot(): lax.dot_general(left, right, (dims, ((), ())), preferred_element_type=F32)]
    all_gather x1 -> x0, blocking collectives: 52.3 us -> none  [per_device(): small = lax.all_gather(small, 'wide', axis=0).astype(F32)]
    convert_element_type x15 -> x1, local copies, waits for them, and re-layouts: 42 us -> 0.09 us  [layer(): small = small.reshape(wide_count, extra, slim).astype(F32)]
    reshape x25 -> x9, local copies, waits for them, and re-layouts: 42.1 us -> 5.81 us  [the longest x1 2.83 us: layer(): grad_tokens.reshape(tokens.shape)]
    convert_element_type x10 -> x1, other arithmetic: 29.4 us -> 0.01 us  [layer(): small = small.reshape(wide_count, extra, slim).astype(F32)]
    slice x33 -> x22, local copies, waits for them, and re-layouts: 30.4 us -> 3.8 us  [the longest x1 0.88 us: layer(): sums_t[2:3]]
    concatenate x24 -> x19, local copies, waits for them, and re-layouts: 28.2 us -> 1.73 us  [the longest x14 0.97 us: layer(): table = jnp.concatenate(rows).reshape(13, wide_count, slim).swapaxes(0, 1)]
  transfers between devices with their start and end apart: 78 -> 78, of which waited for: 17 -> 23; matrix products, arithmetic and copies ran while one was open for 47% -> 11% of each run, Pallas kernels for 0% -> 34%
where the time goes in v2:
time: 639 us; the launch traced here: 631 us
  Pallas kernels  267 us (42%)
  waiting for transfers between devices  171 us (27%)
  starting transfers between devices  109 us (17%)
  local copies, waits for them, and re-layouts  48.7 us (8%)
  other arithmetic  33.9 us (5%)
    ppermute x74, waiting for transfers between devices, swap(): return lax.ppermute(block, axis, [(i, i ^ bits) for i in range(size)])  171 us
    pallas_call x3, Pallas kernels, whole_call(): pl.pallas_call(kernel, in_specs=spaces, out_specs=[pl.BlockSpec(memory_sp...  169 us
    ppermute x74, starting transfers between devices, swap(): return lax.ppermute(block, axis, [(i, i ^ bits) for i in range(size)])  81.9 us
    pallas_call x1, Pallas kernels, spatial_backward(): pl.pallas_call(kernel, name='spatial_backward', grid=(frames,), in_specs=...  55.1 us
    pallas_call x1, Pallas kernels, spatial_forward(): pl.pallas_call(kernel, name='spatial_forward', grid=(frames,), in_specs=[...  33.1 us
    all_to_all x4, starting transfers between devices, exchange(): lax.all_to_all(block, 'wide', split_axis=0, concat_axis=0, tiled=True, ax...  26.8 us
  transfers between devices with their start and end apart: 78, of which 23 were waited for; matrix products, arithmetic and copies ran while one was open for 11% of the time, Pallas kernels for 34%

profile of v2, /device:TPU:0, one launch (start us, length us, event | category | flops | bytes accessed | tf_op | source)
XLA Modules:
  0.0 631.2 jit_solution(5806274417360690491)
XLA Ops:
  4.2 3.1 collective-permute-start.1
  7.3 2.6 collective-permute-start.3
  9.9 1.7 collective-permute-start
  11.6 2.2 collective-permute-done.1.refs_2_
  13.8 1.7 collective-permute-start.2
  15.5 6.5 %collective-permute-done.3.refs_4_ = bf16[104,768]{1,0:T(8,128)(2,1)S(1)} collective-permute-done((bf16[104,768]{1,0:T(8,128)(2,1)S(1)}, bf16[104,768]{1,0:T(8,128)(2,1)S(1)}, u32[]{:S(2)}, u32[]{:S(2)}) %collective-permute-start.3) | collective-permute-done | bytes 159776 | tf_op jit(solution)/shard_map/ppermute | solution.py:540
  24.1 3.2 collective-permute-done.4.refs_5_
  29.7 2.5 assemble.4
  35.2 1.9 collective-permute-start.13
  40.2 14.8 %collective-permute-done.8.w2 = bf16[768,768]{1,0:T(8,128)(2,1)} collective-permute-done((bf16[768,768]{1,0:T(8,128)(2,1)}, bf16[768,768]{1,0:T(8,128)(2,1)}, u32[]{:S(2)}, u32[]{:S(2)}) %collective-permute-start.8) | collective-permute-done | bytes 1179680 | tf_op jit(solution)/shard_map/ppermute | solution.py:540
  62.8 33.1 %spatial_forward.1 = (bf16[4,196,768]{2,1,0:T(8,128)(2,1)}, bf16[4,4,196,768]{3,2,1,0:T(8,128)(2,1)}, bf16[2,4,2,56,768]{4,3,2,1,0:T(8,128)(2,1)}) custom-call(bf16[4,196,768]{2,1,0:T(8,128)(2,1)} %reshape.196.tok, f32[3,768]{1,0:T(4,128)} %pad_maximum_fusion.10.vec, f32[4,1,768]{2,1,0:T(1,128)} %copy.102.bia, bf16[768,768]{1,0:T(8,128)(2,1)} %get-tuple-element.35.w0, ...), custom_call_target="tpu_custom_call" | custom-call | flops 30000001024 | tf_op jit(solution)/shard_map/spatial_forward/pallas_call | solution.py:145
  95.9 7.5 %all-to-all-start = ((bf16[8,2,56,768]{3,2,1,0:T(8,128)(2,1)}), bf16[8,2,56,768]{3,2,1,0:T(8,128)(2,1)S(1)}, u32[]{:S(2)}, u32[]{:S(2)}) async-start(bf16[8,2,56,768]{3,2,1,0:T(8,128)(2,1)} %bitcast.240), calls=%async_computation | async-start | bytes 2752512 | tf_op jit(solution)/shard_map/all_to_all | solution.py:591
  103.4 2.6 assemble.5.w0
  107.5 2.0 collective-permute-start.31
  109.5 2.4 collective-permute-start.33
  111.9 2.0 collective-permute-start.30
  113.9 16.1 %collective-permute-done.31.refs_2_ = bf16[96,768]{1,0:T(8,128)(2,1)S(1)} collective-permute-done((bf16[96,768]{1,0:T(8,128)(2,1)S(1)}, bf16[96,768]{1,0:T(8,128)(2,1)S(1)}, u32[]{:S(2)}, u32[]{:S(2)}) %collective-permute-start.31) | collective-permute-done | bytes 147488 | tf_op jit(solution)/shard_map/ppermute | solution.py:540
  130.0 2.5 collective-permute-start.21
  132.5 14.3 %collective-permute-done.33.refs_4_ = bf16[96,768]{1,0:T(8,128)(2,1)S(1)} collective-permute-done((bf16[96,768]{1,0:T(8,128)(2,1)S(1)}, bf16[96,768]{1,0:T(8,128)(2,1)S(1)}, u32[]{:S(2)}, u32[]{:S(2)}) %collective-permute-start.33) | collective-permute-done | bytes 147488 | tf_op jit(solution)/shard_map/ppermute | solution.py:540
  149.0 10.2 %collective-permute-done.23.refs_4_ = bf16[96,768]{1,0:T(8,128)(2,1)S(1)} collective-permute-done((bf16[96,768]{1,0:T(8,128)(2,1)S(1)}, bf16[96,768]{1,0:T(8,128)(2,1)S(1)}, u32[]{:S(2)}, u32[]{:S(2)}) %collective-permute-start.23) | collective-permute-done | bytes 147488 | tf_op jit(solution)/shard_map/ppermute | solution.py:540
  163.2 2.6 collective-permute-done.36.refs_7_
  166.6 2.4 assemble.7.d0
  169.2 3.1 collective-permute-done.22.refs_3_
  175.4 2.5 assemble.6.u0
  187.5 7.6 %all-to-all-start.1 = ((bf16[8,2,56,768]{3,2,1,0:T(8,128)(2,1)}), bf16[8,2,56,768]{3,2,1,0:T(8,128)(2,1)}, u32[]{:S(2)}, u32[]{:S(2)}) async-start(bf16[8,2,56,768]{3,2,1,0:T(8,128)(2,1)} %bitcast.21), calls=%async_computation.1 | async-start | bytes 2752512 | tf_op jit(solution)/shard_map/all_to_all | solution.py:591
  195.2 6.2 collective-permute-done.38.d2
  201.4 21.7 %collective-permute-done.28.u2 = bf16[768,768]{1,0:T(8,128)(2,1)} collective-permute-done((bf16[768,768]{1,0:T(8,128)(2,1)}, bf16[768,768]{1,0:T(8,128)(2,1)}, u32[]{:S(2)}, u32[]{:S(2)}) %collective-permute-start.28) | collective-permute-done | bytes 1179680 | tf_op jit(solution)/shard_map/ppermute | solution.py:540
  223.1 50.2 %shard_map.194 = (bf16[896,768]{1,0:T(8,128)(2,1)}, bf16[4,896,768]{2,1,0:T(8,128)(2,1)}, f32[896,768]{1,0:T(8,128)}, bf16[896,768]{1,0:T(8,128)(2,1)}) custom-call(bf16[16,56,768]{2,1,0:T(8,128)(2,1)} %bitcast.239, f32[3,768]{1,0:T(4,128)} %pad_maximum_fusion.11.vec, f32[4,1,768]{2,1,0:T(1,128)} %broadcast_in_dim.18.bia, bf16[768,768]{1,0:T(8,128)(2,1)} %assemble.5.w0, ...), custom_call_target="tpu_custom_call" | custom-call | flops 44999999488 | tf_op jit(solution)/shard_map/pallas_call | solution.py:298
  274.4 47.9 %shard_map.195 = (bf16[16,56,768]{2,1,0:T(8,128)(2,1)}, f32[896,768]{1,0:T(8,128)}, bf16[4,768,768]{2,1,0:T(8,128)(2,1)}, bf16[4,768,768]{2,1,0:T(8,128)(2,1)}, f32[8,768]{1,0:T(8,128)}, /*index=5*/f32[4,1,768]{2,1,0:T(1,128)}) custom-call(f32[896,768]{1,0:T(8,128)} %get-tuple-element.37.h_in, bf16[16,56,768]{2,1,0:T(8,128)(2,1)} %bitcast.22.g_in, ...), custom_call_target="tpu_custom_call" | custom-call | flops 44999999488 | tf_op jit(solution)/shard_map/pallas_call | solution.py:298
  322.2 3.4 slice_bitcast_fusion.2
  328.2 70.7 %shard_map.196 = (bf16[16,56,768]{2,1,0:T(8,128)(2,1)}, bf16[4,768,768]{2,1,0:T(8,128)(2,1)}, f32[8,768]{1,0:T(8,128)}, f32[4,1,768]{2,1,0:T(1,128)}) custom-call(f32[896,768]{1,0:T(8,128)} %get-tuple-element.41.g_in, bf16[896,768]{1,0:T(8,128)(2,1)} %get-tuple-element.42.h_in, bf16[896,768]{1,0:T(8,128)(2,1)} %get-tuple-element.43.nrm, ...), custom_call_target="tpu_custom_call" | custom-call | flops 44999999488 | tf_op jit(solution)/shard_map/pallas_call | solution.py:298
  398.9 3.2 slice_bitcast_fusion.6
  402.1 7.0 %all-to-all-start.3 = ((bf16[8,2,56,768]{3,2,1,0:T(8,128)(2,1)}), bf16[8,2,56,768]{3,2,1,0:T(8,128)(2,1)S(1)}, u32[]{:S(2)}, u32[]{:S(2)}) async-start(bf16[8,2,56,768]{3,2,1,0:T(8,128)(2,1)} %bitcast.28), calls=%async_computation.3 | async-start | bytes 2752512 | tf_op jit(solution)/shard_map/all_to_all | solution.py:591
  409.1 2.6 fusion
  413.4 1.9 fusion.2
  419.5 2.9 fusion.4
  423.9 16.9 %collective-permute-done.69 = bf16[768,768]{1,0:T(8,128)(2,1)} collective-permute-done((bf16[768,768]{1,0:T(8,128)(2,1)}, bf16[768,768]{1,0:T(8,128)(2,1)}, u32[]{:S(2)}, u32[]{:S(2)}) %collective-permute-start.69) | collective-permute-done | bytes 1179680 | tf_op jit(solution)/shard_map/ppermute | solution.py:540
  440.9 2.4 fusion.1
  444.2 2.0 collective-permute-start.70
  446.2 19.9 %collective-permute-done.62 = bf16[768,768]{1,0:T(8,128)(2,1)} collective-permute-done((bf16[768,768]{1,0:T(8,128)(2,1)S(1)}, bf16[768,768]{1,0:T(8,128)(2,1)}, u32[]{:S(2)}, u32[]{:S(2)}) %collective-permute-start.62) | collective-permute-done | bytes 1179680 | tf_op jit(solution)/shard_map/ppermute | solution.py:540
  466.2 2.4 fusion.3
  470.1 2.1 collective-permute-start.63
  473.2 4.8 all-to-all-start.2
  478.0 55.1 %spatial_backward.1 = (f32[4,196,768]{2,1,0:T(8,128)}, bf16[4,768,768]{2,1,0:T(8,128)(2,1)}, f32[8,768]{1,0:T(8,128)}, f32[4,1,768]{2,1,0:T(1,128)}) custom-call(bf16[4,196,768]{2,1,0:T(8,128)(2,1)} %reshape.196.tok, bf16[4,196,768]{2,1,0:T(8,128)(2,1)} %get-tuple-element.39.nrm, bf16[4,4,196,768]{3,2,1,0:T(8,128)(2,1)} %get-tuple-element.40.x_in, ...), custom_call_target="tpu_custom_call" | custom-call | flops 49999998976 | tf_op jit(solution)/shard_map/spatial_backward/pallas_call | solution.py:233
  533.2 3.2 slice_bitcast_fusion.8
  539.3 2.4 fusion.5
  544.2 2.3 collective-permute-done.41
  546.6 2.1 collective-permute-start.42
  548.7 2.8 reshape.213
  555.5 2.4 collective-permute-start.44
  558.5 3.1 fusion.6
  561.6 1.7 collective-permute-done.45
  569.0 6.1 collective-permute-done.56
  577.9 2.4 collective-permute-start.57
  582.3 8.0 %collective-permute-done.48 = bf16[768,768]{1,0:T(8,128)(2,1)} collective-permute-done((bf16[768,768]{1,0:T(8,128)(2,1)}, bf16[768,768]{1,0:T(8,128)(2,1)}, u32[]{:S(2)}, u32[]{:S(2)}) %collective-permute-start.48) | collective-permute-done | bytes 1179680 | tf_op jit(solution)/shard_map/ppermute | solution.py:540
  590.3 3.6 collective-permute-start.59
  593.9 2.4 fusion.7
  597.6 1.8 collective-permute-start.49
  602.0 4.6 collective-permute-start.65
  607.6 2.0 fusion.14
  609.5 2.7 collective-permute-done.49
  613.5 2.0 collective-permute-start.50
  615.5 2.1 collective-permute-start.51
  620.4 8.8 %collective-permute-done.51 = bf16[96,768]{1,0:T(8,128)(2,1)S(1)} collective-permute-done((bf16[96,768]{1,0:T(8,128)(2,1)S(1)}, bf16[96,768]{1,0:T(8,128)(2,1)S(1)}, u32[]{:S(2)}, u32[]{:S(2)}) %collective-permute-start.51) | collective-permute-done | bytes 147488 | tf_op jit(solution)/shard_map/ppermute | solution.py:540
  (344 shorter events, 88.6 us)
Async XLA Ops:
  4.2 9.6 %collective-permute-start.1 = (bf16[104,768]{1,0:T(8,128)(2,1)S(1)}, bf16[104,768]{1,0:T(8,128)(2,1)S(1)}, u32[]{:S(2)}, u32[]{:S(2)}) collective-permute-start(bf16[104,768]{1,0:T(8,128)(2,1)S(1)} %pad_maximum_fusion.2.refs_0_), channel_id=1, source_target_pairs={{0,8},{4,12},{8,0},{12,4},{16,24},{20,28},{24,16},{28,20},{1,9},{5... | collective-permute-start | bytes 479240 | tf_op jit(solution)/shard_map/ppermute | solution.py:540
  7.3 14.7 %collective-permute-start.3 = (bf16[104,768]{1,0:T(8,128)(2,1)S(1)}, bf16[104,768]{1,0:T(8,128)(2,1)S(1)}, u32[]{:S(2)}, u32[]{:S(2)}) collective-permute-start(bf16[104,768]{1,0:T(8,128)(2,1)S(1)} %pad_maximum_fusion.2.refs_0_), channel_id=1, source_target_pairs={{0,16},{4,20},{8,24},{12,28},{16,0},{20,4},{24,8},{28,12},{1,17},{... | collective-permute-start | bytes 479240 | tf_op jit(solution)/shard_map/ppermute | solution.py:540
  9.9 13.6 %collective-permute-start.5 = (bf16[104,768]{1,0:T(8,128)(2,1)S(1)}, bf16[104,768]{1,0:T(8,128)(2,1)S(1)}, u32[]{:S(2)}, u32[]{:S(2)}) collective-permute-start(bf16[104,768]{1,0:T(8,128)(2,1)S(1)} %pad_maximum_fusion.2.refs_0_), channel_id=1, source_target_pairs={{0,24},{4,28},{8,16},{12,20},{16,8},{20,12},{24,0},{28,4},{1,25},{... | collective-permute-start | bytes 479240 | tf_op jit(solution)/shard_map/ppermute | solution.py:540
  9.9 14.2 %collective-permute-start = (bf16[104,768]{1,0:T(8,128)(2,1)S(1)}, bf16[104,768]{1,0:T(8,128)(2,1)S(1)}, u32[]{:S(2)}, u32[]{:S(2)}) collective-permute-start(bf16[104,768]{1,0:T(8,128)(2,1)S(1)} %pad_maximum_fusion.2.refs_0_), channel_id=1, source_target_pairs={{0,4},{4,0},{8,12},{12,8},{16,20},{20,16},{24,28},{28,24},{1,5},{5... | collective-permute-start | bytes 479240 | tf_op jit(solution)/shard_map/ppermute | solution.py:540
  13.8 10.3 %collective-permute-start.2 = (bf16[104,768]{1,0:T(8,128)(2,1)S(1)}, bf16[104,768]{1,0:T(8,128)(2,1)S(1)}, u32[]{:S(2)}, u32[]{:S(2)}) collective-permute-start(bf16[104,768]{1,0:T(8,128)(2,1)S(1)} %collective-permute-done.1.refs_2_), channel_id=1, source_target_pairs={{0,4},{4,0},{8,12},{12,8},{16,20},{20,16},{24,28},{28,24},{1,5},{5... | collective-permute-start | bytes 479240 | tf_op jit(solution)/shard_map/ppermute | solution.py:540
  32.2 22.8 %collective-permute-start.8 = (bf16[768,768]{1,0:T(8,128)(2,1)}, bf16[768,768]{1,0:T(8,128)(2,1)}, u32[]{:S(2)}, u32[]{:S(2)}) collective-permute-start(bf16[768,768]{1,0:T(8,128)(2,1)} %get-tuple-element.35.w0), channel_id=1, source_target_pairs={{0,2},{1,3},{2,0},{3,1},{4,6},{5,7},{6,4},{7,5},{8,10},{9,11},{10,... | collective-permute-start | bytes 3538952 | tf_op jit(solution)/shard_map/ppermute | solution.py:540
  34.0 23.6 %collective-permute-start.11 = (bf16[96,768]{1,0:T(8,128)(2,1)S(1)}, bf16[96,768]{1,0:T(8,128)(2,1)S(1)}, u32[]{:S(2)}, u32[]{:S(2)}) collective-permute-start(bf16[96,768]{1,0:T(8,128)(2,1)S(1)} %pad_maximum_fusion.3.refs_0_), channel_id=1, source_target_pairs={{0,8},{4,12},{8,0},{12,4},{16,24},{20,28},{24,16},{28,20},{1,9},{5... | collective-permute-start | bytes 442376 | tf_op jit(solution)/shard_map/ppermute | solution.py:540
  35.2 23.9 %collective-permute-start.13 = (bf16[96,768]{1,0:T(8,128)(2,1)S(1)}, bf16[96,768]{1,0:T(8,128)(2,1)S(1)}, u32[]{:S(2)}, u32[]{:S(2)}) collective-permute-start(bf16[96,768]{1,0:T(8,128)(2,1)S(1)} %pad_maximum_fusion.3.refs_0_), channel_id=1, source_target_pairs={{0,16},{4,20},{8,24},{12,28},{16,0},{20,4},{24,8},{28,12},{1,17},{... | collective-permute-start | bytes 442376 | tf_op jit(solution)/shard_map/ppermute | solution.py:540
  37.1 22.6 %collective-permute-start.15 = (bf16[96,768]{1,0:T(8,128)(2,1)S(1)}, bf16[96,768]{1,0:T(8,128)(2,1)}, u32[]{:S(2)}, u32[]{:S(2)}) collective-permute-start(bf16[96,768]{1,0:T(8,128)(2,1)S(1)} %pad_maximum_fusion.3.refs_0_), channel_id=1, source_target_pairs={{0,24},{4,28},{8,16},{12,20},{16,8},{20,12},{24,0},{28,4},{1,25},{... | collective-permute-start | bytes 442376 | tf_op jit(solution)/shard_map/ppermute | solution.py:540
  40.2 21.0 %collective-permute-start.7 = (bf16[768,768]{1,0:T(8,128)(2,1)S(1)}, bf16[768,768]{1,0:T(8,128)(2,1)S(1)}, u32[]{:S(2)}, u32[]{:S(2)}) collective-permute-start(bf16[768,768]{1,0:T(8,128)(2,1)S(1)} %copy-done.51), channel_id=1, source_target_pairs={{0,1},{1,0},{2,3},{3,2},{4,5},{5,4},{6,7},{7,6},{8,9},{9,8},{10,11... | collective-permute-start | bytes 3538952 | tf_op jit(solution)/shard_map/ppermute | solution.py:540
  57.6 45.8 %collective-permute-start.10 = (bf16[96,768]{1,0:T(8,128)(2,1)S(1)}, bf16[96,768]{1,0:T(8,128)(2,1)}, u32[]{:S(2)}, u32[]{:S(2)}) collective-permute-start(bf16[96,768]{1,0:T(8,128)(2,1)S(1)} %pad_maximum_fusion.3.refs_0_), channel_id=1, source_target_pairs={{0,4},{4,0},{8,12},{12,8},{16,20},{20,16},{24,28},{28,24},{1,5},{5... | collective-permute-start | bytes 442376 | tf_op jit(solution)/shard_map/ppermute | solution.py:540
  59.2 44.2 %collective-permute-start.12 = (bf16[96,768]{1,0:T(8,128)(2,1)S(1)}, bf16[96,768]{1,0:T(8,128)(2,1)}, u32[]{:S(2)}, u32[]{:S(2)}) collective-permute-start(bf16[96,768]{1,0:T(8,128)(2,1)S(1)} %collective-permute-done.11.refs_2_), channel_id=1, source_target_pairs={{0,4},{4,0},{8,12},{12,8},{16,20},{20,16},{24,28},{28,24},{1,5},{5... | collective-permute-start | bytes 442376 | tf_op jit(solution)/shard_map/ppermute | solution.py:540
  59.7 43.7 %collective-permute-start.14 = (bf16[96,768]{1,0:T(8,128)(2,1)S(1)}, bf16[96,768]{1,0:T(8,128)(2,1)}, u32[]{:S(2)}, u32[]{:S(2)}) collective-permute-start(bf16[96,768]{1,0:T(8,128)(2,1)S(1)} %collective-permute-done.13.refs_4_), channel_id=1, source_target_pairs={{0,4},{4,0},{8,12},{12,8},{16,20},{20,16},{24,28},{28,24},{1,5},{5... | collective-permute-start | bytes 442376 | tf_op jit(solution)/shard_map/ppermute | solution.py:540
  62.2 41.1 %collective-permute-start.16 = (bf16[96,768]{1,0:T(8,128)(2,1)}, bf16[96,768]{1,0:T(8,128)(2,1)}, u32[]{:S(2)}, u32[]{:S(2)}) collective-permute-start(bf16[96,768]{1,0:T(8,128)(2,1)} %collective-permute-done.15.refs_6_), channel_id=1, source_target_pairs={{0,4},{4,0},{8,12},{12,8},{16,20},{20,16},{24,28},{28,24},{1,5},{5... | collective-permute-start | bytes 442376 | tf_op jit(solution)/shard_map/ppermute | solution.py:540
  95.9 90.6 %all-to-all-start = ((bf16[8,2,56,768]{3,2,1,0:T(8,128)(2,1)}), bf16[8,2,56,768]{3,2,1,0:T(8,128)(2,1)S(1)}, u32[]{:S(2)}, u32[]{:S(2)}) async-start(bf16[8,2,56,768]{3,2,1,0:T(8,128)(2,1)} %bitcast.240), calls=%async_computation | async-start | bytes 2752512 | tf_op jit(solution)/shard_map/all_to_all | solution.py:591
  106.0 73.4 %collective-permute-start.18 = (bf16[768,768]{1,0:T(8,128)(2,1)}, bf16[768,768]{1,0:T(8,128)(2,1)}, u32[]{:S(2)}, u32[]{:S(2)}) collective-permute-start(bf16[768,768]{1,0:T(8,128)(2,1)} %assemble.5.w0), channel_id=1, source_target_pairs={{0,2},{1,3},{2,0},{3,1},{4,6},{5,7},{6,4},{7,5},{8,10},{9,11},{10,... | collective-permute-start | bytes 3538952 | tf_op jit(solution)/shard_map/ppermute | solution.py:540
  107.5 22.5 %collective-permute-start.31 = (bf16[96,768]{1,0:T(8,128)(2,1)S(1)}, bf16[96,768]{1,0:T(8,128)(2,1)S(1)}, u32[]{:S(2)}, u32[]{:S(2)}) collective-permute-start(bf16[96,768]{1,0:T(8,128)(2,1)S(1)} %bitcast.251), channel_id=1, source_target_pairs={{0,8},{4,12},{8,0},{12,4},{16,24},{20,28},{24,16},{28,20},{1,9},{5... | collective-permute-start | bytes 442376 | tf_op jit(solution)/shard_map/ppermute | solution.py:540
  109.5 37.2 %collective-permute-start.33 = (bf16[96,768]{1,0:T(8,128)(2,1)S(1)}, bf16[96,768]{1,0:T(8,128)(2,1)S(1)}, u32[]{:S(2)}, u32[]{:S(2)}) collective-permute-start(bf16[96,768]{1,0:T(8,128)(2,1)S(1)} %bitcast.252), channel_id=1, source_target_pairs={{0,16},{4,20},{8,24},{12,28},{16,0},{20,4},{24,8},{28,12},{1,17},{... | collective-permute-start | bytes 442376 | tf_op jit(solution)/shard_map/ppermute | solution.py:540
  111.9 34.9 %collective-permute-start.35 = (bf16[96,768]{1,0:T(8,128)(2,1)S(1)}, bf16[96,768]{1,0:T(8,128)(2,1)S(1)}, u32[]{:S(2)}, u32[]{:S(2)}) collective-permute-start(bf16[96,768]{1,0:T(8,128)(2,1)S(1)} %bitcast.253), channel_id=1, source_target_pairs={{0,24},{4,28},{8,16},{12,20},{16,8},{20,12},{24,0},{28,4},{1,25},{... | collective-permute-start | bytes 442376 | tf_op jit(solution)/shard_map/ppermute | solution.py:540
  111.9 34.9 %collective-permute-start.30 = (bf16[96,768]{1,0:T(8,128)(2,1)S(1)}, bf16[96,768]{1,0:T(8,128)(2,1)S(1)}, u32[]{:S(2)}, u32[]{:S(2)}) collective-permute-start(bf16[96,768]{1,0:T(8,128)(2,1)S(1)} %bitcast.254), channel_id=1, source_target_pairs={{0,4},{4,0},{8,12},{12,8},{16,20},{20,16},{24,28},{28,24},{1,5},{5... | collective-permute-start | bytes 442376 | tf_op jit(solution)/shard_map/ppermute | solution.py:540
  130.0 18.3 %collective-permute-start.21 = (bf16[96,768]{1,0:T(8,128)(2,1)S(1)}, bf16[96,768]{1,0:T(8,128)(2,1)S(1)}, u32[]{:S(2)}, u32[]{:S(2)}) collective-permute-start(bf16[96,768]{1,0:T(8,128)(2,1)S(1)} %copy-done.25), channel_id=1, source_target_pairs={{0,8},{4,12},{8,0},{12,4},{16,24},{20,28},{24,16},{28,20},{1,9},{5... | collective-permute-start | bytes 442376 | tf_op jit(solution)/shard_map/ppermute | solution.py:540
  146.7 12.4 %collective-permute-start.23 = (bf16[96,768]{1,0:T(8,128)(2,1)S(1)}, bf16[96,768]{1,0:T(8,128)(2,1)S(1)}, u32[]{:S(2)}, u32[]{:S(2)}) collective-permute-start(bf16[96,768]{1,0:T(8,128)(2,1)S(1)} %copy-done.25), channel_id=1, source_target_pairs={{0,16},{4,20},{8,24},{12,28},{16,0},{20,4},{24,8},{28,12},{1,17},{... | collective-permute-start | bytes 442376 | tf_op jit(solution)/shard_map/ppermute | solution.py:540
  146.8 13.1 %collective-permute-start.25 = (bf16[96,768]{1,0:T(8,128)(2,1)S(1)}, bf16[96,768]{1,0:T(8,128)(2,1)S(1)}, u32[]{:S(2)}, u32[]{:S(2)}) collective-permute-start(bf16[96,768]{1,0:T(8,128)(2,1)S(1)} %copy-done.25), channel_id=1, source_target_pairs={{0,24},{4,28},{8,16},{12,20},{16,8},{20,12},{24,0},{28,4},{1,25},{... | collective-permute-start | bytes 442376 | tf_op jit(solution)/shard_map/ppermute | solution.py:540
  146.9 14.3 %collective-permute-start.32 = (bf16[96,768]{1,0:T(8,128)(2,1)S(1)}, bf16[96,768]{1,0:T(8,128)(2,1)S(1)}, u32[]{:S(2)}, u32[]{:S(2)}) collective-permute-start(bf16[96,768]{1,0:T(8,128)(2,1)S(1)} %collective-permute-done.31.refs_2_), channel_id=1, source_target_pairs={{0,4},{4,0},{8,12},{12,8},{16,20},{20,16},{24,28},{28,24},{1,5},{5... | collective-permute-start | bytes 442376 | tf_op jit(solution)/shard_map/ppermute | solution.py:540
  148.3 13.6 %collective-permute-start.34 = (bf16[96,768]{1,0:T(8,128)(2,1)S(1)}, bf16[96,768]{1,0:T(8,128)(2,1)S(1)}, u32[]{:S(2)}, u32[]{:S(2)}) collective-permute-start(bf16[96,768]{1,0:T(8,128)(2,1)S(1)} %collective-permute-done.33.refs_4_), channel_id=1, source_target_pairs={{0,4},{4,0},{8,12},{12,8},{16,20},{20,16},{24,28},{28,24},{1,5},{5... | collective-permute-start | bytes 442376 | tf_op jit(solution)/shard_map/ppermute | solution.py:540
  161.2 11.1 %collective-permute-start.22 = (bf16[96,768]{1,0:T(8,128)(2,1)S(1)}, bf16[96,768]{1,0:T(8,128)(2,1)}, u32[]{:S(2)}, u32[]{:S(2)}) collective-permute-start(bf16[96,768]{1,0:T(8,128)(2,1)S(1)} %collective-permute-done.21.refs_2_), channel_id=1, source_target_pairs={{0,4},{4,0},{8,12},{12,8},{16,20},{20,16},{24,28},{28,24},{1,5},{5... | collective-permute-start | bytes 442376 | tf_op jit(solution)/shard_map/ppermute | solution.py:540
  161.9 12.0 %collective-permute-start.24 = (bf16[96,768]{1,0:T(8,128)(2,1)S(1)}, bf16[96,768]{1,0:T(8,128)(2,1)}, u32[]{:S(2)}, u32[]{:S(2)}) collective-permute-start(bf16[96,768]{1,0:T(8,128)(2,1)S(1)} %collective-permute-done.23.refs_4_), channel_id=1, source_target_pairs={{0,4},{4,0},{8,12},{12,8},{16,20},{20,16},{24,28},{28,24},{1,5},{5... | collective-permute-start | bytes 442376 | tf_op jit(solution)/shard_map/ppermute | solution.py:540
  169.1 26.1 %collective-permute-start.17 = (bf16[768,768]{1,0:T(8,128)(2,1)}, bf16[768,768]{1,0:T(8,128)(2,1)}, u32[]{:S(2)}, u32[]{:S(2)}) collective-permute-start(bf16[768,768]{1,0:T(8,128)(2,1)} %assemble.5.w0), channel_id=1, source_target_pairs={{0,1},{1,0},{2,3},{3,2},{4,5},{5,4},{6,7},{7,6},{8,9},{9,8},{10,11... | collective-permute-start | bytes 3538952 | tf_op jit(solution)/shard_map/ppermute | solution.py:540
  172.3 29.2 %collective-permute-start.38 = (bf16[768,768]{1,0:T(8,128)(2,1)}, bf16[768,768]{1,0:T(8,128)(2,1)}, u32[]{:S(2)}, u32[]{:S(2)}) collective-permute-start(bf16[768,768]{1,0:T(8,128)(2,1)} %assemble.7.d0), channel_id=1, source_target_pairs={{0,2},{1,3},{2,0},{3,1},{4,6},{5,7},{6,4},{7,5},{8,10},{9,11},{10,... | collective-permute-start | bytes 3538952 | tf_op jit(solution)/shard_map/ppermute | solution.py:540
  177.9 45.2 %collective-permute-start.28 = (bf16[768,768]{1,0:T(8,128)(2,1)}, bf16[768,768]{1,0:T(8,128)(2,1)}, u32[]{:S(2)}, u32[]{:S(2)}) collective-permute-start(bf16[768,768]{1,0:T(8,128)(2,1)} %assemble.6.u0), channel_id=1, source_target_pairs={{0,2},{1,3},{2,0},{3,1},{4,6},{5,7},{6,4},{7,5},{8,10},{9,11},{10,... | collective-permute-start | bytes 3538952 | tf_op jit(solution)/shard_map/ppermute | solution.py:540
  179.4 43.7 %collective-permute-start.19 = (bf16[768,768]{1,0:T(8,128)(2,1)}, bf16[768,768]{1,0:T(8,128)(2,1)}, u32[]{:S(2)}, u32[]{:S(2)}) collective-permute-start(bf16[768,768]{1,0:T(8,128)(2,1)} %collective-permute-done.18.w2), channel_id=1, source_target_pairs={{0,1},{1,0},{2,3},{3,2},{4,5},{5,4},{6,7},{7,6},{8,9},{9,8},{10,11... | collective-permute-start | bytes 3538952 | tf_op jit(solution)/shard_map/ppermute | solution.py:540
  181.7 91.6 %collective-permute-start.37 = (bf16[768,768]{1,0:T(8,128)(2,1)}, bf16[768,768]{1,0:T(8,128)(2,1)}, u32[]{:S(2)}, u32[]{:S(2)}) collective-permute-start(bf16[768,768]{1,0:T(8,128)(2,1)} %assemble.7.d0), channel_id=1, source_target_pairs={{0,1},{1,0},{2,3},{3,2},{4,5},{5,4},{6,7},{7,6},{8,9},{9,8},{10,11... | collective-permute-start | bytes 3538952 | tf_op jit(solution)/shard_map/ppermute | solution.py:540
  187.5 85.8 %all-to-all-start.1 = ((bf16[8,2,56,768]{3,2,1,0:T(8,128)(2,1)}), bf16[8,2,56,768]{3,2,1,0:T(8,128)(2,1)}, u32[]{:S(2)}, u32[]{:S(2)}) async-start(bf16[8,2,56,768]{3,2,1,0:T(8,128)(2,1)} %bitcast.21), calls=%async_computation.1 | async-start | bytes 2752512 | tf_op jit(solution)/shard_map/all_to_all | solution.py:591
  195.2 78.2 %collective-permute-start.27 = (bf16[768,768]{1,0:T(8,128)(2,1)}, bf16[768,768]{1,0:T(8,128)(2,1)S(1)}, u32[]{:S(2)}, u32[]{:S(2)}) collective-permute-start(bf16[768,768]{1,0:T(8,128)(2,1)} %assemble.6.u0), channel_id=1, source_target_pairs={{0,1},{1,0},{2,3},{3,2},{4,5},{5,4},{6,7},{7,6},{8,9},{9,8},{10,11... | collective-permute-start | bytes 3538952 | tf_op jit(solution)/shard_map/ppermute | solution.py:540
  201.4 71.9 %collective-permute-start.39 = (bf16[768,768]{1,0:T(8,128)(2,1)}, bf16[768,768]{1,0:T(8,128)(2,1)}, u32[]{:S(2)}, u32[]{:S(2)}) collective-permute-start(bf16[768,768]{1,0:T(8,128)(2,1)} %collective-permute-done.38.d2), channel_id=1, source_target_pairs={{0,1},{1,0},{2,3},{3,2},{4,5},{5,4},{6,7},{7,6},{8,9},{9,8},{10,11... | collective-permute-start | bytes 3538952 | tf_op jit(solution)/shard_map/ppermute | solution.py:540
  223.1 50.2 %collective-permute-start.29 = (bf16[768,768]{1,0:T(8,128)(2,1)}, bf16[768,768]{1,0:T(8,128)(2,1)}, u32[]{:S(2)}, u32[]{:S(2)}) collective-permute-start(bf16[768,768]{1,0:T(8,128)(2,1)} %collective-permute-done.28.u2), channel_id=1, source_target_pairs={{0,1},{1,0},{2,3},{3,2},{4,5},{5,4},{6,7},{7,6},{8,9},{9,8},{10,11... | collective-permute-start | bytes 3538952 | tf_op jit(solution)/shard_map/ppermute | solution.py:540
  325.6 83.5 %collective-permute-start.68 = (bf16[768,768]{1,0:T(8,128)(2,1)}, bf16[768,768]{1,0:T(8,128)(2,1)S(1)}, u32[]{:S(2)}, u32[]{:S(2)}) collective-permute-start(bf16[768,768]{1,0:T(8,128)(2,1)} %get-tuple-element.122), channel_id=1, source_target_pairs={{0,1},{1,0},{2,3},{3,2},{4,5},{5,4},{6,7},{7,6},{8,9},{9,8},{10,11... | collective-permute-start | bytes 3538952 | tf_op jit(solution)/shard_map/ppermute | solution.py:540
  326.1 96.3 %collective-permute-start.67 = (bf16[768,768]{1,0:T(8,128)(2,1)}, bf16[768,768]{1,0:T(8,128)(2,1)}, u32[]{:S(2)}, u32[]{:S(2)}) collective-permute-start(bf16[768,768]{1,0:T(8,128)(2,1)} %get-tuple-element.121), channel_id=1, source_target_pairs={{0,1},{1,0},{2,3},{3,2},{4,5},{5,4},{6,7},{7,6},{8,9},{9,8},{10,11... | collective-permute-start | bytes 3538952 | tf_op jit(solution)/shard_map/ppermute | solution.py:540
  327.7 85.6 %collective-permute-start.61 = (bf16[768,768]{1,0:T(8,128)(2,1)}, bf16[768,768]{1,0:T(8,128)(2,1)}, u32[]{:S(2)}, u32[]{:S(2)}) collective-permute-start(bf16[768,768]{1,0:T(8,128)(2,1)} %get-tuple-element.124), channel_id=1, source_target_pairs={{0,1},{1,0},{2,3},{3,2},{4,5},{5,4},{6,7},{7,6},{8,9},{9,8},{10,11... | collective-permute-start | bytes 3538952 | tf_op jit(solution)/shard_map/ppermute | solution.py:540
  402.1 17.1 %collective-permute-start.54 = (bf16[768,768]{1,0:T(8,128)(2,1)}, bf16[768,768]{1,0:T(8,128)(2,1)}, u32[]{:S(2)}, u32[]{:S(2)}) collective-permute-start(bf16[768,768]{1,0:T(8,128)(2,1)} %get-tuple-element.126), channel_id=1, source_target_pairs={{0,1},{1,0},{2,3},{3,2},{4,5},{5,4},{6,7},{7,6},{8,9},{9,8},{10,11... | collective-permute-start | bytes 3538952 | tf_op jit(solution)/shard_map/ppermute | solution.py:540
  402.1 70.0 %all-to-all-start.3 = ((bf16[8,2,56,768]{3,2,1,0:T(8,128)(2,1)}), bf16[8,2,56,768]{3,2,1,0:T(8,128)(2,1)S(1)}, u32[]{:S(2)}, u32[]{:S(2)}) async-start(bf16[8,2,56,768]{3,2,1,0:T(8,128)(2,1)} %bitcast.28), calls=%async_computation.3 | async-start | bytes 2752512 | tf_op jit(solution)/shard_map/all_to_all | solution.py:591
  411.7 29.2 %collective-permute-start.69 = (bf16[768,768]{1,0:T(8,128)(2,1)}, bf16[768,768]{1,0:T(8,128)(2,1)}, u32[]{:S(2)}, u32[]{:S(2)}) collective-permute-start(bf16[768,768]{1,0:T(8,128)(2,1)} %fusion), channel_id=1, source_target_pairs={{0,2},{1,3},{2,0},{3,1},{4,6},{5,7},{6,4},{7,5},{8,10},{9,11},{10,... | collective-permute-start | bytes 3538952 | tf_op jit(solution)/shard_map/ppermute | solution.py:540
  413.3 33.0 %collective-permute-start.60 = (bf16[768,768]{1,0:T(8,128)(2,1)}, bf16[768,768]{1,0:T(8,128)(2,1)}, u32[]{:S(2)}, u32[]{:S(2)}) collective-permute-start(bf16[768,768]{1,0:T(8,128)(2,1)} %get-tuple-element.123), channel_id=1, source_target_pairs={{0,1},{1,0},{2,3},{3,2},{4,5},{5,4},{6,7},{7,6},{8,9},{9,8},{10,11... | collective-permute-start | bytes 3538952 | tf_op jit(solution)/shard_map/ppermute | solution.py:540
  415.3 50.9 %collective-permute-start.62 = (bf16[768,768]{1,0:T(8,128)(2,1)S(1)}, bf16[768,768]{1,0:T(8,128)(2,1)}, u32[]{:S(2)}, u32[]{:S(2)}) collective-permute-start(bf16[768,768]{1,0:T(8,128)(2,1)S(1)} %fusion.2), channel_id=1, source_target_pairs={{0,2},{1,3},{2,0},{3,1},{4,6},{5,7},{6,4},{7,5},{8,10},{9,11},{10,... | collective-permute-start | bytes 3538952 | tf_op jit(solution)/shard_map/ppermute | solution.py:540
  419.2 119.5 %collective-permute-start.53 = (bf16[768,768]{1,0:T(8,128)(2,1)}, bf16[768,768]{1,0:T(8,128)(2,1)}, u32[]{:S(2)}, u32[]{:S(2)}) collective-permute-start(bf16[768,768]{1,0:T(8,128)(2,1)} %get-tuple-element.125), channel_id=1, source_target_pairs={{0,1},{1,0},{2,3},{3,2},{4,5},{5,4},{6,7},{7,6},{8,9},{9,8},{10,11... | collective-permute-start | bytes 3538952 | tf_op jit(solution)/shard_map/ppermute | solution.py:540
  422.4 116.9 %collective-permute-start.55 = (bf16[768,768]{1,0:T(8,128)(2,1)}, bf16[768,768]{1,0:T(8,128)(2,1)}, u32[]{:S(2)}, u32[]{:S(2)}) collective-permute-start(bf16[768,768]{1,0:T(8,128)(2,1)} %fusion.4), channel_id=1, source_target_pairs={{0,2},{1,3},{2,0},{3,1},{4,6},{5,7},{6,4},{7,5},{8,10},{9,11},{10,... | collective-permute-start | bytes 3538952 | tf_op jit(solution)/shard_map/ppermute | solution.py:540
  444.2 122.5 %collective-permute-start.70 = (bf16[4,96,768]{2,1,0:T(8,128)(2,1)}, bf16[4,96,768]{2,1,0:T(8,128)(2,1)}, u32[]{:S(2)}, u32[]{:S(2)}) collective-permute-start(bf16[4,96,768]{2,1,0:T(8,128)(2,1)} %fusion.11), channel_id=1, source_target_pairs={{0,4},{4,0},{8,12},{12,8},{16,20},{20,16},{24,28},{28,24},{1,5},{5... | collective-permute-start | bytes 1769480 | tf_op jit(solution)/shard_map/ppermute | solution.py:540
  470.1 107.8 %collective-permute-start.63 = (bf16[4,96,768]{2,1,0:T(8,128)(2,1)S(1)}, bf16[4,96,768]{2,1,0:T(8,128)(2,1)}, u32[]{:S(2)}, u32[]{:S(2)}) collective-permute-start(bf16[4,96,768]{2,1,0:T(8,128)(2,1)S(1)} %fusion.10), channel_id=1, source_target_pairs={{0,4},{4,0},{8,12},{12,8},{16,20},{20,16},{24,28},{28,24},{1,5},{5... | collective-permute-start | bytes 1769480 | tf_op jit(solution)/shard_map/ppermute | solution.py:540
  473.2 75.4 %all-to-all-start.2 = ((bf16[8,2,56,768]{3,2,1,0:T(8,128)(2,1)}), bf16[8,2,56,768]{3,2,1,0:T(8,128)(2,1)S(1)}, u32[]{:S(2)}, u32[]{:S(2)}) async-start(bf16[8,2,56,768]{3,2,1,0:T(8,128)(2,1)} %bitcast.24), calls=%async_computation.2 | async-start | bytes 2752512 | tf_op jit(solution)/shard_map/all_to_all | solution.py:591
  536.4 21.5 %collective-permute-start.47 = (bf16[768,768]{1,0:T(8,128)(2,1)}, bf16[768,768]{1,0:T(8,128)(2,1)}, u32[]{:S(2)}, u32[]{:S(2)}) collective-permute-start(bf16[768,768]{1,0:T(8,128)(2,1)} %get-tuple-element.128), channel_id=1, source_target_pairs={{0,1},{1,0},{2,3},{3,2},{4,5},{5,4},{6,7},{7,6},{8,9},{9,8},{10,11... | collective-permute-start | bytes 3538952 | tf_op jit(solution)/shard_map/ppermute | solution.py:540
  561.6 13.6 %collective-permute-start.56 = (bf16[4,96,768]{2,1,0:T(8,128)(2,1)}, bf16[4,96,768]{2,1,0:T(8,128)(2,1)}, u32[]{:S(2)}, u32[]{:S(2)}) collective-permute-start(bf16[4,96,768]{2,1,0:T(8,128)(2,1)} %fusion.9), channel_id=1, source_target_pairs={{0,4},{4,0},{8,12},{12,8},{16,20},{20,16},{24,28},{28,24},{1,5},{5... | collective-permute-start | bytes 1769480 | tf_op jit(solution)/shard_map/ppermute | solution.py:540
  561.6 20.6 %collective-permute-start.46 = (bf16[768,768]{1,0:T(8,128)(2,1)}, bf16[768,768]{1,0:T(8,128)(2,1)}, u32[]{:S(2)}, u32[]{:S(2)}) collective-permute-start(bf16[768,768]{1,0:T(8,128)(2,1)} %get-tuple-element.127), channel_id=1, source_target_pairs={{0,1},{1,0},{2,3},{3,2},{4,5},{5,4},{6,7},{7,6},{8,9},{9,8},{10,11... | collective-permute-start | bytes 3538952 | tf_op jit(solution)/shard_map/ppermute | solution.py:540
  563.4 27.0 %collective-permute-start.48 = (bf16[768,768]{1,0:T(8,128)(2,1)}, bf16[768,768]{1,0:T(8,128)(2,1)}, u32[]{:S(2)}, u32[]{:S(2)}) collective-permute-start(bf16[768,768]{1,0:T(8,128)(2,1)} %fusion.6), channel_id=1, source_target_pairs={{0,2},{1,3},{2,0},{3,1},{4,6},{5,7},{6,4},{7,5},{8,10},{9,11},{10,... | collective-permute-start | bytes 3538952 | tf_op jit(solution)/shard_map/ppermute | solution.py:540
  569.0 33.0 %collective-permute-start.71 = (bf16[96,768]{1,0:T(8,128)(2,1)}, bf16[96,768]{1,0:T(8,128)(2,1)}, u32[]{:S(2)}, u32[]{:S(2)}) collective-permute-start(bf16[96,768]{1,0:T(8,128)(2,1)} %get-tuple-element.129), channel_id=1, source_target_pairs={{0,8},{4,12},{8,0},{12,4},{16,24},{20,28},{24,16},{28,20},{1,9},{5... | collective-permute-start | bytes 442376 | tf_op jit(solution)/shard_map/ppermute | solution.py:540
  575.1 31.4 %collective-permute-start.72 = (bf16[96,768]{1,0:T(8,128)(2,1)}, bf16[96,768]{1,0:T(8,128)(2,1)}, u32[]{:S(2)}, u32[]{:S(2)}) collective-permute-start(bf16[96,768]{1,0:T(8,128)(2,1)} %get-tuple-element.131), channel_id=1, source_target_pairs={{0,16},{4,20},{8,24},{12,28},{16,0},{20,4},{24,8},{28,12},{1,17},{... | collective-permute-start | bytes 442376 | tf_op jit(solution)/shard_map/ppermute | solution.py:540
  577.9 19.3 %collective-permute-start.57 = (bf16[96,768]{1,0:T(8,128)(2,1)S(1)}, bf16[96,768]{1,0:T(8,128)(2,1)S(1)}, u32[]{:S(2)}, u32[]{:S(2)}) collective-permute-start(bf16[96,768]{1,0:T(8,128)(2,1)S(1)} %get-tuple-element.135), channel_id=1, source_target_pairs={{0,8},{4,12},{8,0},{12,4},{16,24},{20,28},{24,16},{28,20},{1,9},{5... | collective-permute-start | bytes 442376 | tf_op jit(solution)/shard_map/ppermute | solution.py:540
  582.3 15.2 %collective-permute-start.58 = (bf16[96,768]{1,0:T(8,128)(2,1)S(1)}, bf16[96,768]{1,0:T(8,128)(2,1)S(1)}, u32[]{:S(2)}, u32[]{:S(2)}) collective-permute-start(bf16[96,768]{1,0:T(8,128)(2,1)S(1)} %get-tuple-element.137), channel_id=1, source_target_pairs={{0,16},{4,20},{8,24},{12,28},{16,0},{20,4},{24,8},{28,12},{1,17},{... | collective-permute-start | bytes 442376 | tf_op jit(solution)/shard_map/ppermute | solution.py:540
  597.2 10.4 %collective-permute-start.73 = (bf16[96,768]{1,0:T(8,128)(2,1)}, bf16[96,768]{1,0:T(8,128)(2,1)}, u32[]{:S(2)}, u32[]{:S(2)}) collective-permute-start(bf16[96,768]{1,0:T(8,128)(2,1)} %get-tuple-element.130), channel_id=1, source_target_pairs={{0,24},{4,28},{8,16},{12,20},{16,8},{20,12},{24,0},{28,4},{1,25},{... | collective-permute-start | bytes 442376 | tf_op jit(solution)/shard_map/ppermute | solution.py:540
  597.4 20.1 %collective-permute-start.64 = (bf16[96,768]{1,0:T(8,128)(2,1)}, bf16[96,768]{1,0:T(8,128)(2,1)}, u32[]{:S(2)}, u32[]{:S(2)}) collective-permute-start(bf16[96,768]{1,0:T(8,128)(2,1)} %get-tuple-element.132), channel_id=1, source_target_pairs={{0,8},{4,12},{8,0},{12,4},{16,24},{20,28},{24,16},{28,20},{1,9},{5... | collective-permute-start | bytes 442376 | tf_op jit(solution)/shard_map/ppermute | solution.py:540
  597.6 14.6 %collective-permute-start.49 = (bf16[4,96,768]{2,1,0:T(8,128)(2,1)}, bf16[4,96,768]{2,1,0:T(8,128)(2,1)}, u32[]{:S(2)}, u32[]{:S(2)}) collective-permute-start(bf16[4,96,768]{2,1,0:T(8,128)(2,1)} %fusion.8), channel_id=1, source_target_pairs={{0,4},{4,0},{8,12},{12,8},{16,20},{20,16},{24,28},{28,24},{1,5},{5... | collective-permute-start | bytes 1769480 | tf_op jit(solution)/shard_map/ppermute | solution.py:540
  602.0 16.7 %collective-permute-start.65 = (bf16[96,768]{1,0:T(8,128)(2,1)}, bf16[96,768]{1,0:T(8,128)(2,1)S(1)}, u32[]{:S(2)}, u32[]{:S(2)}) collective-permute-start(bf16[96,768]{1,0:T(8,128)(2,1)} %get-tuple-element.134), channel_id=1, source_target_pairs={{0,16},{4,20},{8,24},{12,28},{16,0},{20,4},{24,8},{28,12},{1,17},{... | collective-permute-start | bytes 442376 | tf_op jit(solution)/shard_map/ppermute | solution.py:540
  606.5 12.2 %collective-permute-start.66 = (bf16[96,768]{1,0:T(8,128)(2,1)}, bf16[96,768]{1,0:T(8,128)(2,1)S(1)}, u32[]{:S(2)}, u32[]{:S(2)}) collective-permute-start(bf16[96,768]{1,0:T(8,128)(2,1)} %get-tuple-element.133), channel_id=1, source_target_pairs={{0,24},{4,28},{8,16},{12,20},{16,8},{20,12},{24,0},{28,4},{1,25},{... | collective-permute-start | bytes 442376 | tf_op jit(solution)/shard_map/ppermute | solution.py:540
  615.5 13.7 %collective-permute-start.51 = (bf16[96,768]{1,0:T(8,128)(2,1)S(1)}, bf16[96,768]{1,0:T(8,128)(2,1)S(1)}, u32[]{:S(2)}, u32[]{:S(2)}) collective-permute-start(bf16[96,768]{1,0:T(8,128)(2,1)S(1)} %get-tuple-element.140), channel_id=1, source_target_pairs={{0,16},{4,20},{8,24},{12,28},{16,0},{20,4},{24,8},{28,12},{1,17},{... | collective-permute-start | bytes 442376 | tf_op jit(solution)/shard_map/ppermute | solution.py:540
  617.6 11.6 %collective-permute-start.52 = (bf16[96,768]{1,0:T(8,128)(2,1)S(1)}, bf16[96,768]{1,0:T(8,128)(2,1)S(1)}, u32[]{:S(2)}, u32[]{:S(2)}) collective-permute-start(bf16[96,768]{1,0:T(8,128)(2,1)S(1)} %get-tuple-element.139), channel_id=1, source_target_pairs={{0,24},{4,28},{8,16},{12,20},{16,8},{20,12},{24,0},{28,4},{1,25},{... | collective-permute-start | bytes 442376 | tf_op jit(solution)/shard_map/ppermute | solution.py:540
  (68 other events, 663.7 us)

commit v3 on v2

--- a/solution.py
+++ b/solution.py
@@ -57,36 +57,41 @@
 def softmax(scores, mask):
     if mask is not None:
         scores = jnp.where(mask, scores, -1e30)
-    powers = jnp.exp(scores - jnp.max(scores, axis=-1, keepdims=True))
-    return powers / jnp.sum(powers, axis=-1, keepdims=True)
+    powers = jnp.exp(scores - jnp.max(scores, axis=0, keepdims=True))
+    return powers * (1.0 / jnp.sum(powers, axis=0, keepdims=True))
 
 
 def head_slices(head, cols):
     return [slice(which * cols + head * HEAD_DIM, which * cols + (head + 1) * HEAD_DIM) for which in range(4)]
 
 
-def attend(block, cols, mask):
-    results = []
-    for head in range(cols // HEAD_DIM):
-        q_at, k_at, v_at, _ = head_slices(head, cols)
-        scores = dot(block[:, q_at], block[:, k_at], NT) * SCALE
-        weights = softmax(scores, mask).astype(BF)
-        results.append(dot(weights, block[:, v_at]).astype(BF))
-    return results
-
-
-def attend_back(block, grad_out, cols, mask, store):
-    for head in range(cols // HEAD_DIM):
-        q_at, k_at, v_at, _ = head_slices(head, cols)
-        queries, key_rows, value_rows = block[:, q_at], block[:, k_at], block[:, v_at]
-        grad = grad_out[:, head * HEAD_DIM : (head + 1) * HEAD_DIM]
-        weights = softmax(dot(queries, key_rows, NT) * SCALE, mask)
-        grad_w = dot(grad, value_rows, NT)
-        inner = jnp.sum(weights * grad_w, axis=-1, keepdims=True)
-        grad_s = (weights * (grad_w - inner)).astype(BF)
-        store(q_at, (dot(grad_s, key_rows) * SCALE).astype(BF))
-        store(k_at, (dot(grad_s, queries, TN) * SCALE).astype(BF))
-        store(v_at, dot(weights.astype(BF), grad, TN).astype(BF))
+def attend(load, cols, spans, mask, scores, weights, store):
+    units = [(span, *head_slices(head, cols)) for head in range(cols // HEAD_DIM) for span in spans]
+    for at, (span, q_at, k_at, _, _) in enumerate(units):
+        scores[at] = dot(load(span, k_at), load(span, q_at), NT)
+    for at in range(len(units)):
+        weights[at] = softmax(scores[at] * SCALE, mask).astype(BF)
+    for at, (span, _, _, v_at, o_at) in enumerate(units):
+        store(span, o_at, dot(weights[at], load(span, v_at), TN).astype(BF))
+
+
+def attend_back(load, load_grad, cols, spans, mask, scores, grads, weights, turned, store):
+    units = [
+        (span, head, *head_slices(head, cols)) for head in range(cols // HEAD_DIM) for span in spans
+    ]
+    for at, (span, head, q_at, k_at, v_at, _) in enumerate(units):
+        scores[at] = dot(load(span, k_at), load(span, q_at), NT)
+        grads[at] = dot(load(span, v_at), load_grad(span, head), NT)
+    for at in range(len(units)):
+        soft = softmax(scores[at] * SCALE, mask)
+        inner = jnp.sum(soft * grads[at], axis=0, keepdims=True)
+        weights[at] = soft.astype(BF)
+        turned[at] = (soft * (grads[at] - inner)).astype(BF)
+    for at, (span, head, q_at, k_at, v_at, _) in enumerate(units):
+        grad_s = turned[at]
+        store(span, q_at, (dot(grad_s, load(span, k_at), TN) * SCALE).astype(BF))
+        store(span, k_at, (dot(grad_s, load(span, q_at)) * SCALE).astype(BF))
+        store(span, v_at, dot(weights[at], load_grad(span, head)).astype(BF))
 
 
 def only_out(block, cut, skip):
@@ -118,7 +123,7 @@
     padded = -(-share // GROUP) * GROUP
     pieces = patches // share
 
-    def kernel(tok, vec, bia, w0, w1, w2, w3, a_out, x_out, h_out, wbuf, acc, sem):
+    def kernel(tok, vec, bia, w0, w1, w2, w3, a_out, x_out, h_out, wbuf, acc, sbuf, pbuf, sem):
         @pl.when(pl.program_id(0) == 0)
         def _():
             fetch((w0, w1, w2, w3), wbuf, sem)
@@ -130,9 +135,14 @@
 
         def body(r, carry):
             x_out[0, r] = (dot(normed, wbuf[r]) + bia[r]).astype(BF)
-            heads = attend(x_out[0, r], cols, None)
-            for head, item in enumerate(heads):
-                x_out[0, r, :, head_slices(head, cols)[3]] = item
+
+            def load(span, at):
+                return x_out[0, r, span, at]
+
+            def store(span, at, value):
+                x_out[0, r, span, at] = value
+
+            attend(load, cols, [slice(0, patches)], None, sbuf, pbuf, store)
             acc[...] += dot(only_out(x_out[0, r], cut, skip), wbuf[r, :, cut:], NT)
             return carry
 
@@ -171,6 +181,8 @@
         scratch_shapes=[
             VMEM((4, width, full), BF),
             VMEM((patches, width), F32),
+            VMEM((cols // HEAD_DIM, patches, patches), F32),
+            VMEM((cols // HEAD_DIM, patches, patches), BF),
             pltpu.SemaphoreType.DMA((4,)),
         ],
         cost_estimate=cost(30),
@@ -185,7 +197,7 @@
     cut, skip = cut_of(cols)
     _, pieces, _, padded, _ = grad.shape
 
-    def kernel(tok, nrm, x_in, g_in, vec, w0, w1, w2, w3, t_out, s_out, sums, b_out, wbuf, side, gbuf, acc, tot, sem):
+    def kernel(tok, nrm, x_in, g_in, vec, w0, w1, w2, w3, t_out, s_out, sums, b_out, wbuf, side, gbuf, acc, tot, grad_o, sbuf, dbuf, pbuf, tbuf, sem):
         step = pl.program_id(0)
 
         @pl.when(step == 0)
@@ -202,12 +214,20 @@
         acc[...] = jnp.zeros_like(acc)
 
         def body(r, carry):
-            grad_o = dot(grad_b, wbuf[r, :, cut:])[:, skip:].astype(BF)
-
-            def store(at, value):
-                side[:, at] = value
-
-            attend_back(x_in[0, r], grad_o, cols, None, store)
+            grad_o[...] = dot(grad_b, wbuf[r, :, cut:]).astype(BF)
+
+            def load(span, at):
+                return x_in[0, r, span, at]
+
+            def load_grad(span, head):
+                return grad_o[span, skip + head * HEAD_DIM : skip + (head + 1) * HEAD_DIM]
+
+            def store(span, at, value):
+                side[span, at] = value
+
+            attend_back(
+                load, load_grad, cols, [slice(0, patches)], None, sbuf, dbuf, pbuf, tbuf, store
+            )
             acc[...] += dot(side[...], wbuf[r], NT)
             b_out[r] += jnp.sum(side[...].astype(F32), axis=0, keepdims=True)
             tot[r] += dot(nrm[0], side[...], TN)
@@ -266,6 +286,11 @@
             VMEM((patches, width), F32),
             VMEM((patches, width), F32),
             VMEM((4, width, full), F32),
+            VMEM((patches, full - cut), BF),
+            VMEM((cols // HEAD_DIM, patches, patches), F32),
+            VMEM((cols // HEAD_DIM, patches, patches), F32),
+            VMEM((cols // HEAD_DIM, patches, patches), BF),
+            VMEM((cols // HEAD_DIM, patches, patches), BF),
             pltpu.SemaphoreType.DMA((4,)),
         ],
         cost_estimate=cost(50),
@@ -314,8 +339,10 @@
     groups = padded // GROUP
     span = frames * GROUP
     rows = frames * padded
-
-    def kernel(h_in, vec, bia, w0, w1, w2, w3, a_out, x_out, h_out, r_out, wbuf, stage, sem):
+    spans = [slice(at * span, (at + 1) * span) for at in range(groups)]
+    units = groups * cols // HEAD_DIM
+
+    def kernel(h_in, vec, bia, w0, w1, w2, w3, a_out, x_out, h_out, r_out, wbuf, stage, sbuf, pbuf, sem):
         fetch((w0, w1, w2, w3), wbuf, sem)
         stage[...] = h_in[...].astype(F32)
         into_groups(stage, h_out, groups)
@@ -327,13 +354,13 @@
         def body(r, carry):
             x_out[r] = (dot(a_out[...], wbuf[r]) + bia[r]).astype(BF)
 
-            def inner(at, carry):
-                here = pl.ds(pl.multiple_of(at * span, span), span)
-                for head, item in enumerate(attend(x_out[r, here], cols, mask)):
-                    x_out[r, here, head_slices(head, cols)[3]] = item
-                return carry
-
-            lax.fori_loop(0, groups, inner, 0)
+            def load(here, at):
+                return x_out[r, here, at]
+
+            def store(here, at, value):
+                x_out[r, here, at] = value
+
+            attend(load, cols, spans, mask, sbuf, pbuf, store)
             h_out[...] += dot(only_out(x_out[r], cut, skip), wbuf[r, :, cut:], NT)
             return carry
 
@@ -345,6 +372,8 @@
         [
             VMEM((4, width, full), BF),
             VMEM((frames, padded, width), F32),
+            VMEM((units, span, span), F32),
+            VMEM((units, span, span), BF),
             pltpu.SemaphoreType.DMA((4,)),
         ],
         (True, block),
@@ -444,8 +473,10 @@
     cut, skip = cut_of(cols)
     groups = padded // GROUP
     span = FRAMES * GROUP
-
-    def kernel(g_in, h_in, nrm, x_in, vec, w0, w1, w2, w3, t_out, s_out, sums, b_out, wbuf, side, grad_b, grad_o, acc, stage, sem):
+    spans = [slice(at * span, (at + 1) * span) for at in range(groups)]
+    units = groups * cols // HEAD_DIM
+
+    def kernel(g_in, h_in, nrm, x_in, vec, w0, w1, w2, w3, t_out, s_out, sums, b_out, wbuf, side, grad_b, grad_o, acc, stage, sbuf, dbuf, pbuf, tbuf, sem):
         fetch((w0, w1, w2, w3), wbuf, sem)
         grad_b[...] = g_in[...].astype(BF)
         acc[...] = jnp.zeros_like(acc)
@@ -456,16 +487,16 @@
         def body(r, carry):
             grad_o[...] = dot(grad_b[...], wbuf[r, :, cut:]).astype(BF)
 
-            def inner(at, carry):
-                here = pl.ds(pl.multiple_of(at * span, span), span)
-
-                def store(cols_at, value):
-                    side[here, cols_at] = value
-
-                attend_back(x_in[r, here], grad_o[here][:, skip:], cols, mask, store)
-                return carry
-
-            lax.fori_loop(0, groups, inner, 0)
+            def load(here, at):
+                return x_in[r, here, at]
+
+            def load_grad(here, head):
+                return grad_o[here, skip + head * HEAD_DIM : skip + (head + 1) * HEAD_DIM]
+
+            def store(here, at, value):
+                side[here, at] = value
+
+            attend_back(load, load_grad, cols, spans, mask, sbuf, dbuf, pbuf, tbuf, store)
             acc[...] += dot(side[...], wbuf[r], NT)
             b_out[r] = jnp.sum(side[...].astype(F32), axis=0, keepdims=True)
             first = dot(nrm[...], side[...], TN)
@@ -498,6 +529,10 @@
             VMEM((rows, full - cut), BF),
             VMEM((rows, width), F32),
             VMEM((FRAMES, padded, width), F32),
+            VMEM((units, span, span), F32),
+            VMEM((units, span, span), F32),
+            VMEM((units, span, span), BF),
+            VMEM((units, span, span), BF),
             pltpu.SemaphoreType.DMA((4,)),
         ],
         (True, grad),
@@ -649,14 +684,15 @@
     mixed, dh2, part_u, part_d, sums_m, sum_fc1 = feed_forward(
         h2, dy, vecs(2, 5, 12), up_bias, pack_u, pack_d
     )
-    mixed = exchange(mixed.reshape(RUNS, FRAME_RUN, padded, width))
-    mixed = mixed.reshape(micro, cut, FRAME_RUN, padded, width)[:, :, :, :share].swapaxes(1, 2)
     grad_d = reduce_all(part_d)
     grad_u = reduce_all(part_u)
     dh1, part_t, sums_t, side_t = temporal_backward(
         dh2, h1, a_t, kept_t, vecs(1, 4), pack_t, padded
     )
     dh1 = exchange(dh1.reshape(RUNS, FRAME_RUN, padded, width))
+    mixed, dh1 = lax.optimization_barrier((mixed, dh1))
+    mixed = exchange(mixed.reshape(RUNS, FRAME_RUN, padded, width))
+    mixed = mixed.reshape(micro, cut, FRAME_RUN, padded, width)[:, :, :, :share].swapaxes(1, 2)
     dh1 = dh1.reshape(micro, cut, FRAME_RUN, padded, width)
     grad_t = reduce_all(part_t)
     grad_tokens, part_s, sums_s, side_s = spatial_backward(

time: 639 us -> 574 us (0.90)
  Pallas kernels: 267 us -> 185 us
  waiting for transfers between devices: 171 us -> 183 us
    pallas_call x3, Pallas kernels: 169 us -> 101 us  [whole_call(): pl.pallas_call(kernel, in_specs=spaces, out_specs=[pl.BlockSpec(memory_sp...]
    ppermute x74, waiting for transfers between devices: 171 us -> 183 us  [swap(): return lax.ppermute(block, axis, [(i, i ^ bits) for i in range(size)])]
    pallas_call x1, Pallas kernels: 55.1 us -> 43.9 us  [spatial_backward(): pl.pallas_call(kernel, name='spatial_backward', grid=(frames,), in_specs=...]
    unnamed x117 -> x113, local copies, waits for them, and re-layouts: 12.6 us -> 13.2 us
  transfers between devices with their start and end apart: 78 -> 78, of which waited for: 23 -> 23; matrix products, arithmetic and copies ran while one was open for 11% -> 12% of each run, Pallas kernels for 34% -> 18%
where the time goes in v3:
time: 574 us; the launch traced here: 566 us
  Pallas kernels  185 us (32%)
  waiting for transfers between devices  183 us (32%)
  starting transfers between devices  111 us (19%)
  local copies, waits for them, and re-layouts  51.3 us (9%)
  other arithmetic  34.8 us (6%)
    ppermute x74, waiting for transfers between devices, swap(): return lax.ppermute(block, axis, [(i, i ^ bits) for i in range(size)])  183 us
    pallas_call x3, Pallas kernels, whole_call(): pl.pallas_call(kernel, in_specs=spaces, out_specs=[pl.BlockSpec(memory_sp...  101 us
    ppermute x74, starting transfers between devices, swap(): return lax.ppermute(block, axis, [(i, i ^ bits) for i in range(size)])  82.3 us
    pallas_call x1, Pallas kernels, spatial_backward(): pl.pallas_call(kernel, name='spatial_backward', grid=(frames,), in_specs=...  43.9 us
    pallas_call x1, Pallas kernels, spatial_forward(): pl.pallas_call(kernel, name='spatial_forward', grid=(frames,), in_specs=[...  29.6 us
    all_to_all x4, starting transfers between devices, exchange(): lax.all_to_all(block, 'wide', split_axis=0, concat_axis=0, tiled=True, ax...  28.3 us
    unnamed x113, local copies, waits for them, and re-layouts  13.2 us
  transfers between devices with their start and end apart: 78, of which 23 were waited for; matrix products, arithmetic and copies ran while one was open for 12% of the time, Pallas kernels for 18%

profile of v3, /device:TPU:0, one launch (start us, length us, event | category | flops | bytes accessed | tf_op | source)
XLA Modules:
  0.0 566.4 jit_solution(1831336818525229503)
XLA Ops:
  4.2 3.1 collective-permute-start.1
  7.3 2.6 collective-permute-start.3
  9.9 1.7 collective-permute-start
  11.6 2.2 collective-permute-done.1.refs_2_
  13.8 1.7 collective-permute-start.2
  15.5 6.5 %collective-permute-done.3.refs_4_ = bf16[104,768]{1,0:T(8,128)(2,1)S(1)} collective-permute-done((bf16[104,768]{1,0:T(8,128)(2,1)S(1)}, bf16[104,768]{1,0:T(8,128)(2,1)S(1)}, u32[]{:S(2)}, u32[]{:S(2)}) %collective-permute-start.3) | collective-permute-done | bytes 159776 | tf_op jit(solution)/shard_map/ppermute | solution.py:575
  24.1 3.2 collective-permute-done.4.refs_5_
  27.3 1.7 collective-permute-done.6.refs_7_
  29.7 2.5 assemble.4
  35.2 1.9 collective-permute-start.13
  40.2 14.8 %collective-permute-done.8.w2 = bf16[768,768]{1,0:T(8,128)(2,1)} collective-permute-done((bf16[768,768]{1,0:T(8,128)(2,1)}, bf16[768,768]{1,0:T(8,128)(2,1)}, u32[]{:S(2)}, u32[]{:S(2)}) %collective-permute-start.8) | collective-permute-done | bytes 1179680 | tf_op jit(solution)/shard_map/ppermute | solution.py:575
  62.8 29.6 %spatial_forward.1 = (bf16[4,196,768]{2,1,0:T(8,128)(2,1)}, bf16[4,4,196,768]{3,2,1,0:T(8,128)(2,1)}, bf16[2,4,2,56,768]{4,3,2,1,0:T(8,128)(2,1)}) custom-call(bf16[4,196,768]{2,1,0:T(8,128)(2,1)} %reshape.196.tok, f32[3,768]{1,0:T(4,128)} %pad_maximum_fusion.10.vec, f32[4,1,768]{2,1,0:T(1,128)} %copy.102.bia, bf16[768,768]{1,0:T(8,128)(2,1)} %get-tuple-element.37.w0, ...), custom_call_target="tpu_custom_call" | custom-call | flops 30000001024 | tf_op jit(solution)/shard_map/spatial_forward/pallas_call | solution.py:155
  92.4 7.4 %all-to-all-start = ((bf16[8,2,56,768]{3,2,1,0:T(8,128)(2,1)}), bf16[8,2,56,768]{3,2,1,0:T(8,128)(2,1)S(1)}, u32[]{:S(2)}, u32[]{:S(2)}) async-start(bf16[8,2,56,768]{3,2,1,0:T(8,128)(2,1)} %bitcast.240), calls=%async_computation | async-start | bytes 2752512 | tf_op jit(solution)/shard_map/all_to_all | solution.py:626
  99.9 2.5 assemble.5.w0
  104.0 2.0 collective-permute-start.31
  106.0 2.4 collective-permute-start.33
  108.3 2.0 collective-permute-start.30
  110.3 16.2 %collective-permute-done.31.refs_2_ = bf16[96,768]{1,0:T(8,128)(2,1)S(1)} collective-permute-done((bf16[96,768]{1,0:T(8,128)(2,1)S(1)}, bf16[96,768]{1,0:T(8,128)(2,1)S(1)}, u32[]{:S(2)}, u32[]{:S(2)}) %collective-permute-start.31) | collective-permute-done | bytes 147488 | tf_op jit(solution)/shard_map/ppermute | solution.py:575
  126.5 2.5 collective-permute-start.21
  129.0 14.3 %collective-permute-done.33.refs_4_ = bf16[96,768]{1,0:T(8,128)(2,1)S(1)} collective-permute-done((bf16[96,768]{1,0:T(8,128)(2,1)S(1)}, bf16[96,768]{1,0:T(8,128)(2,1)S(1)}, u32[]{:S(2)}, u32[]{:S(2)}) %collective-permute-start.33) | collective-permute-done | bytes 147488 | tf_op jit(solution)/shard_map/ppermute | solution.py:575
  145.5 10.2 %collective-permute-done.23.refs_4_ = bf16[96,768]{1,0:T(8,128)(2,1)S(1)} collective-permute-done((bf16[96,768]{1,0:T(8,128)(2,1)S(1)}, bf16[96,768]{1,0:T(8,128)(2,1)S(1)}, u32[]{:S(2)}, u32[]{:S(2)}) %collective-permute-start.23) | collective-permute-done | bytes 147488 | tf_op jit(solution)/shard_map/ppermute | solution.py:575
  159.8 2.6 collective-permute-done.36.refs_7_
  163.1 2.5 assemble.7.d0
  165.8 3.1 collective-permute-done.22.refs_3_
  172.0 2.4 assemble.6.u0
  184.0 7.4 %all-to-all-start.1 = ((bf16[8,2,56,768]{3,2,1,0:T(8,128)(2,1)}), bf16[8,2,56,768]{3,2,1,0:T(8,128)(2,1)}, u32[]{:S(2)}, u32[]{:S(2)}) async-start(bf16[8,2,56,768]{3,2,1,0:T(8,128)(2,1)} %bitcast.21), calls=%async_computation.1 | async-start | bytes 2752512 | tf_op jit(solution)/shard_map/all_to_all | solution.py:626
  191.6 6.4 %collective-permute-done.38.d2 = bf16[768,768]{1,0:T(8,128)(2,1)} collective-permute-done((bf16[768,768]{1,0:T(8,128)(2,1)}, bf16[768,768]{1,0:T(8,128)(2,1)}, u32[]{:S(2)}, u32[]{:S(2)}) %collective-permute-start.38) | collective-permute-done | bytes 1179680 | tf_op jit(solution)/shard_map/ppermute | solution.py:575
  198.0 21.7 %collective-permute-done.28.u2 = bf16[768,768]{1,0:T(8,128)(2,1)} collective-permute-done((bf16[768,768]{1,0:T(8,128)(2,1)}, bf16[768,768]{1,0:T(8,128)(2,1)}, u32[]{:S(2)}, u32[]{:S(2)}) %collective-permute-start.28) | collective-permute-done | bytes 1179680 | tf_op jit(solution)/shard_map/ppermute | solution.py:575
  219.7 20.1 %shard_map.194 = (bf16[896,768]{1,0:T(8,128)(2,1)}, bf16[4,896,768]{2,1,0:T(8,128)(2,1)}, f32[896,768]{1,0:T(8,128)}, bf16[896,768]{1,0:T(8,128)(2,1)}) custom-call(bf16[16,56,768]{2,1,0:T(8,128)(2,1)} %bitcast.239, f32[3,768]{1,0:T(4,128)} %pad_maximum_fusion.11.vec, f32[4,1,768]{2,1,0:T(1,128)} %broadcast_in_dim.18.bia, bf16[768,768]{1,0:T(8,128)(2,1)} %assemble.5.w0, ...), custom_call_target="tpu_custom_call" | custom-call | flops 44999999488 | tf_op jit(solution)/shard_map/pallas_call | solution.py:323
  240.9 47.9 %shard_map.195 = (bf16[16,56,768]{2,1,0:T(8,128)(2,1)}, f32[896,768]{1,0:T(8,128)}, bf16[4,768,768]{2,1,0:T(8,128)(2,1)}, bf16[4,768,768]{2,1,0:T(8,128)(2,1)}, f32[8,768]{1,0:T(8,128)}, /*index=5*/f32[4,1,768]{2,1,0:T(1,128)}) custom-call(f32[896,768]{1,0:T(8,128)} %get-tuple-element.39.h_in, bf16[16,56,768]{2,1,0:T(8,128)(2,1)} %bitcast.22.g_in, ...), custom_call_target="tpu_custom_call" | custom-call | flops 44999999488 | tf_op jit(solution)/shard_map/pallas_call | solution.py:323
  288.7 33.2 %shard_map.196 = (bf16[16,56,768]{2,1,0:T(8,128)(2,1)}, bf16[4,768,768]{2,1,0:T(8,128)(2,1)}, f32[8,768]{1,0:T(8,128)}, f32[4,1,768]{2,1,0:T(1,128)}) custom-call(f32[896,768]{1,0:T(8,128)} %get-tuple-element.41.g_in, bf16[896,768]{1,0:T(8,128)(2,1)} %get-tuple-element.42.h_in, bf16[896,768]{1,0:T(8,128)(2,1)} %get-tuple-element.43.nrm, ...), custom_call_target="tpu_custom_call" | custom-call | flops 44999999488 | tf_op jit(solution)/shard_map/pallas_call | solution.py:323
  321.9 3.4 slice_bitcast_fusion.6
  327.5 7.2 %all-to-all-start.2 = ((bf16[8,2,56,768]{3,2,1,0:T(8,128)(2,1)}), bf16[8,2,56,768]{3,2,1,0:T(8,128)(2,1)S(1)}, u32[]{:S(2)}, u32[]{:S(2)}) async-start(bf16[8,2,56,768]{3,2,1,0:T(8,128)(2,1)} %bitcast.24), calls=%async_computation.2 | async-start | bytes 2752512 | tf_op jit(solution)/shard_map/all_to_all | solution.py:626
  334.6 3.2 slice_bitcast_fusion.4
  338.3 2.6 fusion.4
  342.6 1.9 fusion
  348.2 2.9 fusion.2
  352.6 17.5 %collective-permute-done.55 = bf16[768,768]{1,0:T(8,128)(2,1)} collective-permute-done((bf16[768,768]{1,0:T(8,128)(2,1)}, bf16[768,768]{1,0:T(8,128)(2,1)}, u32[]{:S(2)}, u32[]{:S(2)}) %collective-permute-start.55) | collective-permute-done | bytes 1179680 | tf_op jit(solution)/shard_map/ppermute | solution.py:575
  370.1 2.4 fusion.5
  374.7 2.0 collective-permute-start.56
  376.8 18.6 %collective-permute-done.69 = bf16[768,768]{1,0:T(8,128)(2,1)} collective-permute-done((bf16[768,768]{1,0:T(8,128)(2,1)S(1)}, bf16[768,768]{1,0:T(8,128)(2,1)}, u32[]{:S(2)}, u32[]{:S(2)}) %collective-permute-start.69) | collective-permute-done | bytes 1179680 | tf_op jit(solution)/shard_map/ppermute | solution.py:575
  395.4 3.8 fusion.1
  400.3 43.9 %spatial_backward.1 = (f32[4,196,768]{2,1,0:T(8,128)}, bf16[4,768,768]{2,1,0:T(8,128)(2,1)}, f32[8,768]{1,0:T(8,128)}, f32[4,1,768]{2,1,0:T(1,128)}) custom-call(bf16[4,196,768]{2,1,0:T(8,128)(2,1)} %reshape.196.tok, bf16[4,196,768]{2,1,0:T(8,128)(2,1)} %get-tuple-element.47.nrm, bf16[4,4,196,768]{3,2,1,0:T(8,128)(2,1)} %get-tuple-element.48.x_in, ...), custom_call_target="tpu_custom_call" | custom-call | flops 49999998976 | tf_op jit(solution)/shard_map/spatial_backward/pallas_call | solution.py:253
  447.3 3.2 slice_bitcast_fusion.8
  452.6 2.4 fusion.3
  455.8 2.1 collective-permute-start.42
  461.2 2.0 collective-permute-start.43
  463.2 2.4 collective-permute-start.44
  466.5 2.8 reshape.213
  469.3 6.2 %all-to-all-start.3 = ((bf16[8,2,56,768]{3,2,1,0:T(8,128)(2,1)}), bf16[8,2,56,768]{3,2,1,0:T(8,128)(2,1)}, u32[]{:S(2)}, u32[]{:S(2)}) async-start(bf16[8,2,56,768]{3,2,1,0:T(8,128)(2,1)} %bitcast.238), calls=%async_computation.3 | async-start | bytes 2752512 | tf_op jit(solution)/shard_map/all_to_all | solution.py:626
  475.6 2.1 collective-permute-start.70
  480.4 1.7 fusion.6
  484.9 2.0 collective-permute-start.57
  486.9 18.6 %collective-permute-done.70 = bf16[4,96,768]{2,1,0:T(8,128)(2,1)} collective-permute-done((bf16[4,96,768]{2,1,0:T(8,128)(2,1)}, bf16[4,96,768]{2,1,0:T(8,128)(2,1)}, u32[]{:S(2)}, u32[]{:S(2)}) %collective-permute-start.70) | collective-permute-done | bytes 589856 | tf_op jit(solution)/shard_map/ppermute | solution.py:575
  505.5 1.7 collective-permute-start.58
  508.5 6.9 %collective-permute-done.63 = bf16[4,96,768]{2,1,0:T(8,128)(2,1)} collective-permute-done((bf16[4,96,768]{2,1,0:T(8,128)(2,1)}, bf16[4,96,768]{2,1,0:T(8,128)(2,1)}, u32[]{:S(2)}, u32[]{:S(2)}) %collective-permute-start.63) | collective-permute-done | bytes 589856 | tf_op jit(solution)/shard_map/ppermute | solution.py:575
  515.3 3.3 collective-permute-start.59
  523.7 3.5 collective-permute-start.73
  527.4 2.2 fusion.7
  534.4 2.8 collective-permute-start.66
  537.2 2.0 fusion.14
  539.2 7.6 %collective-permute-done.65 = bf16[96,768]{1,0:T(8,128)(2,1)S(1)} collective-permute-done((bf16[96,768]{1,0:T(8,128)(2,1)}, bf16[96,768]{1,0:T(8,128)(2,1)S(1)}, u32[]{:S(2)}, u32[]{:S(2)}) %collective-permute-start.65) | collective-permute-done | bytes 147488 | tf_op jit(solution)/shard_map/ppermute | solution.py:575
  549.7 2.2 collective-permute-start.50
  558.2 6.2 %collective-permute-done.51 = bf16[96,768]{1,0:T(8,128)(2,1)S(1)} collective-permute-done((bf16[96,768]{1,0:T(8,128)(2,1)S(1)}, bf16[96,768]{1,0:T(8,128)(2,1)S(1)}, u32[]{:S(2)}, u32[]{:S(2)}) %collective-permute-start.51) | collective-permute-done | bytes 147488 | tf_op jit(solution)/shard_map/ppermute | solution.py:575
  (340 shorter events, 93.3 us)
Async XLA Ops:
  7.3 14.7 %collective-permute-start.3 = (bf16[104,768]{1,0:T(8,128)(2,1)S(1)}, bf16[104,768]{1,0:T(8,128)(2,1)S(1)}, u32[]{:S(2)}, u32[]{:S(2)}) collective-permute-start(bf16[104,768]{1,0:T(8,128)(2,1)S(1)} %pad_maximum_fusion.2.refs_0_), channel_id=1, source_target_pairs={{0,16},{4,20},{8,24},{12,28},{16,0},{20,4},{24,8},{28,12},{1,17},{... | collective-permute-start | bytes 479240 | tf_op jit(solution)/shard_map/ppermute | solution.py:575
  9.9 13.6 %collective-permute-start.5 = (bf16[104,768]{1,0:T(8,128)(2,1)S(1)}, bf16[104,768]{1,0:T(8,128)(2,1)S(1)}, u32[]{:S(2)}, u32[]{:S(2)}) collective-permute-start(bf16[104,768]{1,0:T(8,128)(2,1)S(1)} %pad_maximum_fusion.2.refs_0_), channel_id=1, source_target_pairs={{0,24},{4,28},{8,16},{12,20},{16,8},{20,12},{24,0},{28,4},{1,25},{... | collective-permute-start | bytes 479240 | tf_op jit(solution)/shard_map/ppermute | solution.py:575
  9.9 14.2 %collective-permute-start = (bf16[104,768]{1,0:T(8,128)(2,1)S(1)}, bf16[104,768]{1,0:T(8,128)(2,1)S(1)}, u32[]{:S(2)}, u32[]{:S(2)}) collective-permute-start(bf16[104,768]{1,0:T(8,128)(2,1)S(1)} %pad_maximum_fusion.2.refs_0_), channel_id=1, source_target_pairs={{0,4},{4,0},{8,12},{12,8},{16,20},{20,16},{24,28},{28,24},{1,5},{5... | collective-permute-start | bytes 479240 | tf_op jit(solution)/shard_map/ppermute | solution.py:575
  32.2 22.8 %collective-permute-start.8 = (bf16[768,768]{1,0:T(8,128)(2,1)}, bf16[768,768]{1,0:T(8,128)(2,1)}, u32[]{:S(2)}, u32[]{:S(2)}) collective-permute-start(bf16[768,768]{1,0:T(8,128)(2,1)} %get-tuple-element.37.w0), channel_id=1, source_target_pairs={{0,2},{1,3},{2,0},{3,1},{4,6},{5,7},{6,4},{7,5},{8,10},{9,11},{10,... | collective-permute-start | bytes 3538952 | tf_op jit(solution)/shard_map/ppermute | solution.py:575
  34.0 23.6 %collective-permute-start.11 = (bf16[96,768]{1,0:T(8,128)(2,1)S(1)}, bf16[96,768]{1,0:T(8,128)(2,1)S(1)}, u32[]{:S(2)}, u32[]{:S(2)}) collective-permute-start(bf16[96,768]{1,0:T(8,128)(2,1)S(1)} %pad_maximum_fusion.3.refs_0_), channel_id=1, source_target_pairs={{0,8},{4,12},{8,0},{12,4},{16,24},{20,28},{24,16},{28,20},{1,9},{5... | collective-permute-start | bytes 442376 | tf_op jit(solution)/shard_map/ppermute | solution.py:575
  35.2 23.9 %collective-permute-start.13 = (bf16[96,768]{1,0:T(8,128)(2,1)S(1)}, bf16[96,768]{1,0:T(8,128)(2,1)S(1)}, u32[]{:S(2)}, u32[]{:S(2)}) collective-permute-start(bf16[96,768]{1,0:T(8,128)(2,1)S(1)} %pad_maximum_fusion.3.refs_0_), channel_id=1, source_target_pairs={{0,16},{4,20},{8,24},{12,28},{16,0},{20,4},{24,8},{28,12},{1,17},{... | collective-permute-start | bytes 442376 | tf_op jit(solution)/shard_map/ppermute | solution.py:575
  37.1 22.6 %collective-permute-start.15 = (bf16[96,768]{1,0:T(8,128)(2,1)S(1)}, bf16[96,768]{1,0:T(8,128)(2,1)}, u32[]{:S(2)}, u32[]{:S(2)}) collective-permute-start(bf16[96,768]{1,0:T(8,128)(2,1)S(1)} %pad_maximum_fusion.3.refs_0_), channel_id=1, source_target_pairs={{0,24},{4,28},{8,16},{12,20},{16,8},{20,12},{24,0},{28,4},{1,25},{... | collective-permute-start | bytes 442376 | tf_op jit(solution)/shard_map/ppermute | solution.py:575
  40.2 21.0 %collective-permute-start.7 = (bf16[768,768]{1,0:T(8,128)(2,1)S(1)}, bf16[768,768]{1,0:T(8,128)(2,1)S(1)}, u32[]{:S(2)}, u32[]{:S(2)}) collective-permute-start(bf16[768,768]{1,0:T(8,128)(2,1)S(1)} %copy-done.49), channel_id=1, source_target_pairs={{0,1},{1,0},{2,3},{3,2},{4,5},{5,4},{6,7},{7,6},{8,9},{9,8},{10,11... | collective-permute-start | bytes 3538952 | tf_op jit(solution)/shard_map/ppermute | solution.py:575
  57.6 42.3 %collective-permute-start.10 = (bf16[96,768]{1,0:T(8,128)(2,1)S(1)}, bf16[96,768]{1,0:T(8,128)(2,1)}, u32[]{:S(2)}, u32[]{:S(2)}) collective-permute-start(bf16[96,768]{1,0:T(8,128)(2,1)S(1)} %pad_maximum_fusion.3.refs_0_), channel_id=1, source_target_pairs={{0,4},{4,0},{8,12},{12,8},{16,20},{20,16},{24,28},{28,24},{1,5},{5... | collective-permute-start | bytes 442376 | tf_op jit(solution)/shard_map/ppermute | solution.py:575
  59.2 40.7 %collective-permute-start.12 = (bf16[96,768]{1,0:T(8,128)(2,1)S(1)}, bf16[96,768]{1,0:T(8,128)(2,1)}, u32[]{:S(2)}, u32[]{:S(2)}) collective-permute-start(bf16[96,768]{1,0:T(8,128)(2,1)S(1)} %collective-permute-done.11.refs_2_), channel_id=1, source_target_pairs={{0,4},{4,0},{8,12},{12,8},{16,20},{20,16},{24,28},{28,24},{1,5},{5... | collective-permute-start | bytes 442376 | tf_op jit(solution)/shard_map/ppermute | solution.py:575
  59.7 40.2 %collective-permute-start.14 = (bf16[96,768]{1,0:T(8,128)(2,1)S(1)}, bf16[96,768]{1,0:T(8,128)(2,1)}, u32[]{:S(2)}, u32[]{:S(2)}) collective-permute-start(bf16[96,768]{1,0:T(8,128)(2,1)S(1)} %collective-permute-done.13.refs_4_), channel_id=1, source_target_pairs={{0,4},{4,0},{8,12},{12,8},{16,20},{20,16},{24,28},{28,24},{1,5},{5... | collective-permute-start | bytes 442376 | tf_op jit(solution)/shard_map/ppermute | solution.py:575
  62.2 37.7 %collective-permute-start.16 = (bf16[96,768]{1,0:T(8,128)(2,1)}, bf16[96,768]{1,0:T(8,128)(2,1)}, u32[]{:S(2)}, u32[]{:S(2)}) collective-permute-start(bf16[96,768]{1,0:T(8,128)(2,1)} %collective-permute-done.15.refs_6_), channel_id=1, source_target_pairs={{0,4},{4,0},{8,12},{12,8},{16,20},{20,16},{24,28},{28,24},{1,5},{5... | collective-permute-start | bytes 442376 | tf_op jit(solution)/shard_map/ppermute | solution.py:575
  92.4 90.5 %all-to-all-start = ((bf16[8,2,56,768]{3,2,1,0:T(8,128)(2,1)}), bf16[8,2,56,768]{3,2,1,0:T(8,128)(2,1)S(1)}, u32[]{:S(2)}, u32[]{:S(2)}) async-start(bf16[8,2,56,768]{3,2,1,0:T(8,128)(2,1)} %bitcast.240), calls=%async_computation | async-start | bytes 2752512 | tf_op jit(solution)/shard_map/all_to_all | solution.py:626
  102.4 73.5 %collective-permute-start.18 = (bf16[768,768]{1,0:T(8,128)(2,1)}, bf16[768,768]{1,0:T(8,128)(2,1)}, u32[]{:S(2)}, u32[]{:S(2)}) collective-permute-start(bf16[768,768]{1,0:T(8,128)(2,1)} %assemble.5.w0), channel_id=1, source_target_pairs={{0,2},{1,3},{2,0},{3,1},{4,6},{5,7},{6,4},{7,5},{8,10},{9,11},{10,... | collective-permute-start | bytes 3538952 | tf_op jit(solution)/shard_map/ppermute | solution.py:575
  104.0 22.6 %collective-permute-start.31 = (bf16[96,768]{1,0:T(8,128)(2,1)S(1)}, bf16[96,768]{1,0:T(8,128)(2,1)S(1)}, u32[]{:S(2)}, u32[]{:S(2)}) collective-permute-start(bf16[96,768]{1,0:T(8,128)(2,1)S(1)} %bitcast.251), channel_id=1, source_target_pairs={{0,8},{4,12},{8,0},{12,4},{16,24},{20,28},{24,16},{28,20},{1,9},{5... | collective-permute-start | bytes 442376 | tf_op jit(solution)/shard_map/ppermute | solution.py:575
  106.0 37.3 %collective-permute-start.33 = (bf16[96,768]{1,0:T(8,128)(2,1)S(1)}, bf16[96,768]{1,0:T(8,128)(2,1)S(1)}, u32[]{:S(2)}, u32[]{:S(2)}) collective-permute-start(bf16[96,768]{1,0:T(8,128)(2,1)S(1)} %bitcast.252), channel_id=1, source_target_pairs={{0,16},{4,20},{8,24},{12,28},{16,0},{20,4},{24,8},{28,12},{1,17},{... | collective-permute-start | bytes 442376 | tf_op jit(solution)/shard_map/ppermute | solution.py:575
  108.3 35.0 %collective-permute-start.35 = (bf16[96,768]{1,0:T(8,128)(2,1)S(1)}, bf16[96,768]{1,0:T(8,128)(2,1)S(1)}, u32[]{:S(2)}, u32[]{:S(2)}) collective-permute-start(bf16[96,768]{1,0:T(8,128)(2,1)S(1)} %bitcast.253), channel_id=1, source_target_pairs={{0,24},{4,28},{8,16},{12,20},{16,8},{20,12},{24,0},{28,4},{1,25},{... | collective-permute-start | bytes 442376 | tf_op jit(solution)/shard_map/ppermute | solution.py:575
  108.3 35.0 %collective-permute-start.30 = (bf16[96,768]{1,0:T(8,128)(2,1)S(1)}, bf16[96,768]{1,0:T(8,128)(2,1)S(1)}, u32[]{:S(2)}, u32[]{:S(2)}) collective-permute-start(bf16[96,768]{1,0:T(8,128)(2,1)S(1)} %bitcast.254), channel_id=1, source_target_pairs={{0,4},{4,0},{8,12},{12,8},{16,20},{20,16},{24,28},{28,24},{1,5},{5... | collective-permute-start | bytes 442376 | tf_op jit(solution)/shard_map/ppermute | solution.py:575
  126.5 18.3 %collective-permute-start.21 = (bf16[96,768]{1,0:T(8,128)(2,1)S(1)}, bf16[96,768]{1,0:T(8,128)(2,1)S(1)}, u32[]{:S(2)}, u32[]{:S(2)}) collective-permute-start(bf16[96,768]{1,0:T(8,128)(2,1)S(1)} %copy-done.25), channel_id=1, source_target_pairs={{0,8},{4,12},{8,0},{12,4},{16,24},{20,28},{24,16},{28,20},{1,9},{5... | collective-permute-start | bytes 442376 | tf_op jit(solution)/shard_map/ppermute | solution.py:575
  143.3 12.4 %collective-permute-start.23 = (bf16[96,768]{1,0:T(8,128)(2,1)S(1)}, bf16[96,768]{1,0:T(8,128)(2,1)S(1)}, u32[]{:S(2)}, u32[]{:S(2)}) collective-permute-start(bf16[96,768]{1,0:T(8,128)(2,1)S(1)} %copy-done.25), channel_id=1, source_target_pairs={{0,16},{4,20},{8,24},{12,28},{16,0},{20,4},{24,8},{28,12},{1,17},{... | collective-permute-start | bytes 442376 | tf_op jit(solution)/shard_map/ppermute | solution.py:575
  143.3 13.1 %collective-permute-start.25 = (bf16[96,768]{1,0:T(8,128)(2,1)S(1)}, bf16[96,768]{1,0:T(8,128)(2,1)S(1)}, u32[]{:S(2)}, u32[]{:S(2)}) collective-permute-start(bf16[96,768]{1,0:T(8,128)(2,1)S(1)} %copy-done.25), channel_id=1, source_target_pairs={{0,24},{4,28},{8,16},{12,20},{16,8},{20,12},{24,0},{28,4},{1,25},{... | collective-permute-start | bytes 442376 | tf_op jit(solution)/shard_map/ppermute | solution.py:575
  143.4 14.3 %collective-permute-start.32 = (bf16[96,768]{1,0:T(8,128)(2,1)S(1)}, bf16[96,768]{1,0:T(8,128)(2,1)S(1)}, u32[]{:S(2)}, u32[]{:S(2)}) collective-permute-start(bf16[96,768]{1,0:T(8,128)(2,1)S(1)} %collective-permute-done.31.refs_2_), channel_id=1, source_target_pairs={{0,4},{4,0},{8,12},{12,8},{16,20},{20,16},{24,28},{28,24},{1,5},{5... | collective-permute-start | bytes 442376 | tf_op jit(solution)/shard_map/ppermute | solution.py:575
  144.8 13.6 %collective-permute-start.34 = (bf16[96,768]{1,0:T(8,128)(2,1)S(1)}, bf16[96,768]{1,0:T(8,128)(2,1)S(1)}, u32[]{:S(2)}, u32[]{:S(2)}) collective-permute-start(bf16[96,768]{1,0:T(8,128)(2,1)S(1)} %collective-permute-done.33.refs_4_), channel_id=1, source_target_pairs={{0,4},{4,0},{8,12},{12,8},{16,20},{20,16},{24,28},{28,24},{1,5},{5... | collective-permute-start | bytes 442376 | tf_op jit(solution)/shard_map/ppermute | solution.py:575
  157.7 11.1 %collective-permute-start.22 = (bf16[96,768]{1,0:T(8,128)(2,1)S(1)}, bf16[96,768]{1,0:T(8,128)(2,1)}, u32[]{:S(2)}, u32[]{:S(2)}) collective-permute-start(bf16[96,768]{1,0:T(8,128)(2,1)S(1)} %collective-permute-done.21.refs_2_), channel_id=1, source_target_pairs={{0,4},{4,0},{8,12},{12,8},{16,20},{20,16},{24,28},{28,24},{1,5},{5... | collective-permute-start | bytes 442376 | tf_op jit(solution)/shard_map/ppermute | solution.py:575
  158.4 12.0 %collective-permute-start.24 = (bf16[96,768]{1,0:T(8,128)(2,1)S(1)}, bf16[96,768]{1,0:T(8,128)(2,1)}, u32[]{:S(2)}, u32[]{:S(2)}) collective-permute-start(bf16[96,768]{1,0:T(8,128)(2,1)S(1)} %collective-permute-done.23.refs_4_), channel_id=1, source_target_pairs={{0,4},{4,0},{8,12},{12,8},{16,20},{20,16},{24,28},{28,24},{1,5},{5... | collective-permute-start | bytes 442376 | tf_op jit(solution)/shard_map/ppermute | solution.py:575
  165.7 25.8 %collective-permute-start.17 = (bf16[768,768]{1,0:T(8,128)(2,1)}, bf16[768,768]{1,0:T(8,128)(2,1)}, u32[]{:S(2)}, u32[]{:S(2)}) collective-permute-start(bf16[768,768]{1,0:T(8,128)(2,1)} %assemble.5.w0), channel_id=1, source_target_pairs={{0,1},{1,0},{2,3},{3,2},{4,5},{5,4},{6,7},{7,6},{8,9},{9,8},{10,11... | collective-permute-start | bytes 3538952 | tf_op jit(solution)/shard_map/ppermute | solution.py:575
  168.8 29.2 %collective-permute-start.38 = (bf16[768,768]{1,0:T(8,128)(2,1)}, bf16[768,768]{1,0:T(8,128)(2,1)}, u32[]{:S(2)}, u32[]{:S(2)}) collective-permute-start(bf16[768,768]{1,0:T(8,128)(2,1)} %assemble.7.d0), channel_id=1, source_target_pairs={{0,2},{1,3},{2,0},{3,1},{4,6},{5,7},{6,4},{7,5},{8,10},{9,11},{10,... | collective-permute-start | bytes 3538952 | tf_op jit(solution)/shard_map/ppermute | solution.py:575
  174.4 45.3 %collective-permute-start.28 = (bf16[768,768]{1,0:T(8,128)(2,1)}, bf16[768,768]{1,0:T(8,128)(2,1)}, u32[]{:S(2)}, u32[]{:S(2)}) collective-permute-start(bf16[768,768]{1,0:T(8,128)(2,1)} %assemble.6.u0), channel_id=1, source_target_pairs={{0,2},{1,3},{2,0},{3,1},{4,6},{5,7},{6,4},{7,5},{8,10},{9,11},{10,... | collective-permute-start | bytes 3538952 | tf_op jit(solution)/shard_map/ppermute | solution.py:575
  175.9 43.8 %collective-permute-start.19 = (bf16[768,768]{1,0:T(8,128)(2,1)}, bf16[768,768]{1,0:T(8,128)(2,1)}, u32[]{:S(2)}, u32[]{:S(2)}) collective-permute-start(bf16[768,768]{1,0:T(8,128)(2,1)} %collective-permute-done.18.w2), channel_id=1, source_target_pairs={{0,1},{1,0},{2,3},{3,2},{4,5},{5,4},{6,7},{7,6},{8,9},{9,8},{10,11... | collective-permute-start | bytes 3538952 | tf_op jit(solution)/shard_map/ppermute | solution.py:575
  178.2 61.6 %collective-permute-start.37 = (bf16[768,768]{1,0:T(8,128)(2,1)}, bf16[768,768]{1,0:T(8,128)(2,1)}, u32[]{:S(2)}, u32[]{:S(2)}) collective-permute-start(bf16[768,768]{1,0:T(8,128)(2,1)} %assemble.7.d0), channel_id=1, source_target_pairs={{0,1},{1,0},{2,3},{3,2},{4,5},{5,4},{6,7},{7,6},{8,9},{9,8},{10,11... | collective-permute-start | bytes 3538952 | tf_op jit(solution)/shard_map/ppermute | solution.py:575
  184.0 55.8 %all-to-all-start.1 = ((bf16[8,2,56,768]{3,2,1,0:T(8,128)(2,1)}), bf16[8,2,56,768]{3,2,1,0:T(8,128)(2,1)}, u32[]{:S(2)}, u32[]{:S(2)}) async-start(bf16[8,2,56,768]{3,2,1,0:T(8,128)(2,1)} %bitcast.21), calls=%async_computation.1 | async-start | bytes 2752512 | tf_op jit(solution)/shard_map/all_to_all | solution.py:626
  191.5 48.4 %collective-permute-start.27 = (bf16[768,768]{1,0:T(8,128)(2,1)}, bf16[768,768]{1,0:T(8,128)(2,1)S(1)}, u32[]{:S(2)}, u32[]{:S(2)}) collective-permute-start(bf16[768,768]{1,0:T(8,128)(2,1)} %assemble.6.u0), channel_id=1, source_target_pairs={{0,1},{1,0},{2,3},{3,2},{4,5},{5,4},{6,7},{7,6},{8,9},{9,8},{10,11... | collective-permute-start | bytes 3538952 | tf_op jit(solution)/shard_map/ppermute | solution.py:575
  198.0 41.9 %collective-permute-start.39 = (bf16[768,768]{1,0:T(8,128)(2,1)}, bf16[768,768]{1,0:T(8,128)(2,1)}, u32[]{:S(2)}, u32[]{:S(2)}) collective-permute-start(bf16[768,768]{1,0:T(8,128)(2,1)} %collective-permute-done.38.d2), channel_id=1, source_target_pairs={{0,1},{1,0},{2,3},{3,2},{4,5},{5,4},{6,7},{7,6},{8,9},{9,8},{10,11... | collective-permute-start | bytes 3538952 | tf_op jit(solution)/shard_map/ppermute | solution.py:575
  219.7 20.1 %collective-permute-start.29 = (bf16[768,768]{1,0:T(8,128)(2,1)}, bf16[768,768]{1,0:T(8,128)(2,1)}, u32[]{:S(2)}, u32[]{:S(2)}) collective-permute-start(bf16[768,768]{1,0:T(8,128)(2,1)} %collective-permute-done.28.u2), channel_id=1, source_target_pairs={{0,1},{1,0},{2,3},{3,2},{4,5},{5,4},{6,7},{7,6},{8,9},{9,8},{10,11... | collective-permute-start | bytes 3538952 | tf_op jit(solution)/shard_map/ppermute | solution.py:575
  325.3 13.0 %collective-permute-start.54 = (bf16[768,768]{1,0:T(8,128)(2,1)}, bf16[768,768]{1,0:T(8,128)(2,1)S(1)}, u32[]{:S(2)}, u32[]{:S(2)}) collective-permute-start(bf16[768,768]{1,0:T(8,128)(2,1)} %get-tuple-element.130), channel_id=1, source_target_pairs={{0,1},{1,0},{2,3},{3,2},{4,5},{5,4},{6,7},{7,6},{8,9},{9,8},{10,11... | collective-permute-start | bytes 3538952 | tf_op jit(solution)/shard_map/ppermute | solution.py:575
  327.4 15.2 %collective-permute-start.68 = (bf16[768,768]{1,0:T(8,128)(2,1)}, bf16[768,768]{1,0:T(8,128)(2,1)}, u32[]{:S(2)}, u32[]{:S(2)}) collective-permute-start(bf16[768,768]{1,0:T(8,128)(2,1)} %get-tuple-element.126), channel_id=1, source_target_pairs={{0,1},{1,0},{2,3},{3,2},{4,5},{5,4},{6,7},{7,6},{8,9},{9,8},{10,11... | collective-permute-start | bytes 3538952 | tf_op jit(solution)/shard_map/ppermute | solution.py:575
  327.5 71.7 %all-to-all-start.2 = ((bf16[8,2,56,768]{3,2,1,0:T(8,128)(2,1)}), bf16[8,2,56,768]{3,2,1,0:T(8,128)(2,1)S(1)}, u32[]{:S(2)}, u32[]{:S(2)}) async-start(bf16[8,2,56,768]{3,2,1,0:T(8,128)(2,1)} %bitcast.24), calls=%async_computation.2 | async-start | bytes 2752512 | tf_op jit(solution)/shard_map/all_to_all | solution.py:626
  338.0 13.1 %collective-permute-start.53 = (bf16[768,768]{1,0:T(8,128)(2,1)}, bf16[768,768]{1,0:T(8,128)(2,1)}, u32[]{:S(2)}, u32[]{:S(2)}) collective-permute-start(bf16[768,768]{1,0:T(8,128)(2,1)} %get-tuple-element.129), channel_id=1, source_target_pairs={{0,1},{1,0},{2,3},{3,2},{4,5},{5,4},{6,7},{7,6},{8,9},{9,8},{10,11... | collective-permute-start | bytes 3538952 | tf_op jit(solution)/shard_map/ppermute | solution.py:575
  340.9 29.2 %collective-permute-start.55 = (bf16[768,768]{1,0:T(8,128)(2,1)}, bf16[768,768]{1,0:T(8,128)(2,1)}, u32[]{:S(2)}, u32[]{:S(2)}) collective-permute-start(bf16[768,768]{1,0:T(8,128)(2,1)} %fusion.4), channel_id=1, source_target_pairs={{0,2},{1,3},{2,0},{3,1},{4,6},{5,7},{6,4},{7,5},{8,10},{9,11},{10,... | collective-permute-start | bytes 3538952 | tf_op jit(solution)/shard_map/ppermute | solution.py:575
  342.5 34.3 %collective-permute-start.67 = (bf16[768,768]{1,0:T(8,128)(2,1)}, bf16[768,768]{1,0:T(8,128)(2,1)}, u32[]{:S(2)}, u32[]{:S(2)}) collective-permute-start(bf16[768,768]{1,0:T(8,128)(2,1)} %get-tuple-element.125), channel_id=1, source_target_pairs={{0,1},{1,0},{2,3},{3,2},{4,5},{5,4},{6,7},{7,6},{8,9},{9,8},{10,11... | collective-permute-start | bytes 3538952 | tf_op jit(solution)/shard_map/ppermute | solution.py:575
  344.5 50.9 %collective-permute-start.69 = (bf16[768,768]{1,0:T(8,128)(2,1)S(1)}, bf16[768,768]{1,0:T(8,128)(2,1)}, u32[]{:S(2)}, u32[]{:S(2)}) collective-permute-start(bf16[768,768]{1,0:T(8,128)(2,1)S(1)} %fusion), channel_id=1, source_target_pairs={{0,2},{1,3},{2,0},{3,1},{4,6},{5,7},{6,4},{7,5},{8,10},{9,11},{10,... | collective-permute-start | bytes 3538952 | tf_op jit(solution)/shard_map/ppermute | solution.py:575
  347.9 104.7 %collective-permute-start.60 = (bf16[768,768]{1,0:T(8,128)(2,1)}, bf16[768,768]{1,0:T(8,128)(2,1)}, u32[]{:S(2)}, u32[]{:S(2)}) collective-permute-start(bf16[768,768]{1,0:T(8,128)(2,1)} %get-tuple-element.127), channel_id=1, source_target_pairs={{0,1},{1,0},{2,3},{3,2},{4,5},{5,4},{6,7},{7,6},{8,9},{9,8},{10,11... | collective-permute-start | bytes 3538952 | tf_op jit(solution)/shard_map/ppermute | solution.py:575
  351.1 101.5 %collective-permute-start.62 = (bf16[768,768]{1,0:T(8,128)(2,1)}, bf16[768,768]{1,0:T(8,128)(2,1)}, u32[]{:S(2)}, u32[]{:S(2)}) collective-permute-start(bf16[768,768]{1,0:T(8,128)(2,1)} %fusion.2), channel_id=1, source_target_pairs={{0,2},{1,3},{2,0},{3,1},{4,6},{5,7},{6,4},{7,5},{8,10},{9,11},{10,... | collective-permute-start | bytes 3538952 | tf_op jit(solution)/shard_map/ppermute | solution.py:575
  374.7 108.9 %collective-permute-start.56 = (bf16[4,96,768]{2,1,0:T(8,128)(2,1)}, bf16[4,96,768]{2,1,0:T(8,128)(2,1)}, u32[]{:S(2)}, u32[]{:S(2)}) collective-permute-start(bf16[4,96,768]{2,1,0:T(8,128)(2,1)} %fusion.9), channel_id=1, source_target_pairs={{0,4},{4,0},{8,12},{12,8},{16,20},{20,16},{24,28},{28,24},{1,5},{5... | collective-permute-start | bytes 1769480 | tf_op jit(solution)/shard_map/ppermute | solution.py:575
  450.5 29.9 %collective-permute-start.47 = (bf16[768,768]{1,0:T(8,128)(2,1)}, bf16[768,768]{1,0:T(8,128)(2,1)S(1)}, u32[]{:S(2)}, u32[]{:S(2)}) collective-permute-start(bf16[768,768]{1,0:T(8,128)(2,1)} %get-tuple-element.132), channel_id=1, source_target_pairs={{0,1},{1,0},{2,3},{3,2},{4,5},{5,4},{6,7},{7,6},{8,9},{9,8},{10,11... | collective-permute-start | bytes 3538952 | tf_op jit(solution)/shard_map/ppermute | solution.py:575
  461.2 14.3 %collective-permute-start.43 = (f32[24,96]{1,0:T(8,128)}, f32[24,96]{1,0:T(8,128)}, u32[]{:S(2)}, u32[]{:S(2)}) collective-permute-start(f32[24,96]{1,0:T(8,128)} %get-tuple-element.161), channel_id=1, source_target_pairs={{0,8},{4,12},{8,0},{12,4},{16,24},{20,28},{24,16},{28,20},{1,9},{5... | collective-permute-start | bytes 27656 | tf_op jit(solution)/shard_map/ppermute | solution.py:575
  463.2 14.4 %collective-permute-start.44 = (f32[24,96]{1,0:T(8,128)}, f32[24,96]{1,0:T(8,128)}, u32[]{:S(2)}, u32[]{:S(2)}) collective-permute-start(f32[24,96]{1,0:T(8,128)} %get-tuple-element.163), channel_id=1, source_target_pairs={{0,16},{4,20},{8,24},{12,28},{16,0},{20,4},{24,8},{28,12},{1,17},{... | collective-permute-start | bytes 27656 | tf_op jit(solution)/shard_map/ppermute | solution.py:575
  465.6 12.2 %collective-permute-start.45 = (f32[24,96]{1,0:T(8,128)S(1)}, f32[24,96]{1,0:T(8,128)}, u32[]{:S(2)}, u32[]{:S(2)}) collective-permute-start(f32[24,96]{1,0:T(8,128)S(1)} %get-tuple-element.162), channel_id=1, source_target_pairs={{0,24},{4,28},{8,16},{12,20},{16,8},{20,12},{24,0},{28,4},{1,25},{... | collective-permute-start | bytes 27656 | tf_op jit(solution)/shard_map/ppermute | solution.py:575
  469.3 85.0 %all-to-all-start.3 = ((bf16[8,2,56,768]{3,2,1,0:T(8,128)(2,1)}), bf16[8,2,56,768]{3,2,1,0:T(8,128)(2,1)}, u32[]{:S(2)}, u32[]{:S(2)}) async-start(bf16[8,2,56,768]{3,2,1,0:T(8,128)(2,1)} %bitcast.238), calls=%async_computation.3 | async-start | bytes 2752512 | tf_op jit(solution)/shard_map/all_to_all | solution.py:626
  475.6 30.0 %collective-permute-start.70 = (bf16[4,96,768]{2,1,0:T(8,128)(2,1)}, bf16[4,96,768]{2,1,0:T(8,128)(2,1)}, u32[]{:S(2)}, u32[]{:S(2)}) collective-permute-start(bf16[4,96,768]{2,1,0:T(8,128)(2,1)} %fusion.11), channel_id=1, source_target_pairs={{0,4},{4,0},{8,12},{12,8},{16,20},{20,16},{24,28},{28,24},{1,5},{5... | collective-permute-start | bytes 1769480 | tf_op jit(solution)/shard_map/ppermute | solution.py:575
  477.7 37.6 %collective-permute-start.63 = (bf16[4,96,768]{2,1,0:T(8,128)(2,1)}, bf16[4,96,768]{2,1,0:T(8,128)(2,1)}, u32[]{:S(2)}, u32[]{:S(2)}) collective-permute-start(bf16[4,96,768]{2,1,0:T(8,128)(2,1)} %fusion.10), channel_id=1, source_target_pairs={{0,4},{4,0},{8,12},{12,8},{16,20},{20,16},{24,28},{28,24},{1,5},{5... | collective-permute-start | bytes 1769480 | tf_op jit(solution)/shard_map/ppermute | solution.py:575
  477.8 49.5 %collective-permute-start.46 = (bf16[768,768]{1,0:T(8,128)(2,1)}, bf16[768,768]{1,0:T(8,128)(2,1)}, u32[]{:S(2)}, u32[]{:S(2)}) collective-permute-start(bf16[768,768]{1,0:T(8,128)(2,1)} %get-tuple-element.131), channel_id=1, source_target_pairs={{0,1},{1,0},{2,3},{3,2},{4,5},{5,4},{6,7},{7,6},{8,9},{9,8},{10,11... | collective-permute-start | bytes 3538952 | tf_op jit(solution)/shard_map/ppermute | solution.py:575
  482.1 45.3 %collective-permute-start.48 = (bf16[768,768]{1,0:T(8,128)(2,1)S(1)}, bf16[768,768]{1,0:T(8,128)(2,1)S(1)}, u32[]{:S(2)}, u32[]{:S(2)}) collective-permute-start(bf16[768,768]{1,0:T(8,128)(2,1)S(1)} %fusion.6), channel_id=1, source_target_pairs={{0,2},{1,3},{2,0},{3,1},{4,6},{5,7},{6,4},{7,5},{8,10},{9,11},{10,... | collective-permute-start | bytes 3538952 | tf_op jit(solution)/shard_map/ppermute | solution.py:575
  484.9 36.4 %collective-permute-start.57 = (bf16[96,768]{1,0:T(8,128)(2,1)S(1)}, bf16[96,768]{1,0:T(8,128)(2,1)S(1)}, u32[]{:S(2)}, u32[]{:S(2)}) collective-permute-start(bf16[96,768]{1,0:T(8,128)(2,1)S(1)} %get-tuple-element.139), channel_id=1, source_target_pairs={{0,8},{4,12},{8,0},{12,4},{16,24},{20,28},{24,16},{28,20},{1,9},{5... | collective-permute-start | bytes 442376 | tf_op jit(solution)/shard_map/ppermute | solution.py:575
  505.5 15.8 %collective-permute-start.58 = (bf16[96,768]{1,0:T(8,128)(2,1)S(1)}, bf16[96,768]{1,0:T(8,128)(2,1)S(1)}, u32[]{:S(2)}, u32[]{:S(2)}) collective-permute-start(bf16[96,768]{1,0:T(8,128)(2,1)S(1)} %get-tuple-element.141), channel_id=1, source_target_pairs={{0,16},{4,20},{8,24},{12,28},{16,0},{20,4},{24,8},{28,12},{1,17},{... | collective-permute-start | bytes 442376 | tf_op jit(solution)/shard_map/ppermute | solution.py:575
  521.4 13.1 %collective-permute-start.71 = (bf16[96,768]{1,0:T(8,128)(2,1)}, bf16[96,768]{1,0:T(8,128)(2,1)}, u32[]{:S(2)}, u32[]{:S(2)}) collective-permute-start(bf16[96,768]{1,0:T(8,128)(2,1)} %get-tuple-element.133), channel_id=1, source_target_pairs={{0,8},{4,12},{8,0},{12,4},{16,24},{20,28},{24,16},{28,20},{1,9},{5... | collective-permute-start | bytes 442376 | tf_op jit(solution)/shard_map/ppermute | solution.py:575
  521.4 13.1 %collective-permute-start.72 = (bf16[96,768]{1,0:T(8,128)(2,1)}, bf16[96,768]{1,0:T(8,128)(2,1)}, u32[]{:S(2)}, u32[]{:S(2)}) collective-permute-start(bf16[96,768]{1,0:T(8,128)(2,1)} %get-tuple-element.135), channel_id=1, source_target_pairs={{0,16},{4,20},{8,24},{12,28},{16,0},{20,4},{24,8},{28,12},{1,17},{... | collective-permute-start | bytes 442376 | tf_op jit(solution)/shard_map/ppermute | solution.py:575
  523.7 13.5 %collective-permute-start.73 = (bf16[96,768]{1,0:T(8,128)(2,1)}, bf16[96,768]{1,0:T(8,128)(2,1)}, u32[]{:S(2)}, u32[]{:S(2)}) collective-permute-start(bf16[96,768]{1,0:T(8,128)(2,1)} %get-tuple-element.134), channel_id=1, source_target_pairs={{0,24},{4,28},{8,16},{12,20},{16,8},{20,12},{24,0},{28,4},{1,25},{... | collective-permute-start | bytes 442376 | tf_op jit(solution)/shard_map/ppermute | solution.py:575
  527.3 11.9 %collective-permute-start.64 = (bf16[96,768]{1,0:T(8,128)(2,1)}, bf16[96,768]{1,0:T(8,128)(2,1)}, u32[]{:S(2)}, u32[]{:S(2)}) collective-permute-start(bf16[96,768]{1,0:T(8,128)(2,1)} %get-tuple-element.136), channel_id=1, source_target_pairs={{0,8},{4,12},{8,0},{12,4},{16,24},{20,28},{24,16},{28,20},{1,9},{5... | collective-permute-start | bytes 442376 | tf_op jit(solution)/shard_map/ppermute | solution.py:575
  530.4 18.0 %collective-permute-start.49 = (bf16[4,96,768]{2,1,0:T(8,128)(2,1)}, bf16[4,96,768]{2,1,0:T(8,128)(2,1)}, u32[]{:S(2)}, u32[]{:S(2)}) collective-permute-start(bf16[4,96,768]{2,1,0:T(8,128)(2,1)} %fusion.8), channel_id=1, source_target_pairs={{0,4},{4,0},{8,12},{12,8},{16,20},{20,16},{24,28},{28,24},{1,5},{5... | collective-permute-start | bytes 1769480 | tf_op jit(solution)/shard_map/ppermute | solution.py:575
  534.4 12.3 %collective-permute-start.65 = (bf16[96,768]{1,0:T(8,128)(2,1)}, bf16[96,768]{1,0:T(8,128)(2,1)S(1)}, u32[]{:S(2)}, u32[]{:S(2)}) collective-permute-start(bf16[96,768]{1,0:T(8,128)(2,1)} %get-tuple-element.138), channel_id=1, source_target_pairs={{0,16},{4,20},{8,24},{12,28},{16,0},{20,4},{24,8},{28,12},{1,17},{... | collective-permute-start | bytes 442376 | tf_op jit(solution)/shard_map/ppermute | solution.py:575
  534.4 12.3 %collective-permute-start.66 = (bf16[96,768]{1,0:T(8,128)(2,1)}, bf16[96,768]{1,0:T(8,128)(2,1)S(1)}, u32[]{:S(2)}, u32[]{:S(2)}) collective-permute-start(bf16[96,768]{1,0:T(8,128)(2,1)} %get-tuple-element.137), channel_id=1, source_target_pairs={{0,24},{4,28},{8,16},{12,20},{16,8},{20,12},{24,0},{28,4},{1,25},{... | collective-permute-start | bytes 442376 | tf_op jit(solution)/shard_map/ppermute | solution.py:575
  551.9 12.5 %collective-permute-start.51 = (bf16[96,768]{1,0:T(8,128)(2,1)S(1)}, bf16[96,768]{1,0:T(8,128)(2,1)S(1)}, u32[]{:S(2)}, u32[]{:S(2)}) collective-permute-start(bf16[96,768]{1,0:T(8,128)(2,1)S(1)} %get-tuple-element.144), channel_id=1, source_target_pairs={{0,16},{4,20},{8,24},{12,28},{16,0},{20,4},{24,8},{28,12},{1,17},{... | collective-permute-start | bytes 442376 | tf_op jit(solution)/shard_map/ppermute | solution.py:575
  552.8 11.5 %collective-permute-start.52 = (bf16[96,768]{1,0:T(8,128)(2,1)S(1)}, bf16[96,768]{1,0:T(8,128)(2,1)S(1)}, u32[]{:S(2)}, u32[]{:S(2)}) collective-permute-start(bf16[96,768]{1,0:T(8,128)(2,1)S(1)} %get-tuple-element.143), channel_id=1, source_target_pairs={{0,24},{4,28},{8,16},{12,20},{16,8},{20,12},{24,0},{28,4},{1,25},{... | collective-permute-start | bytes 442376 | tf_op jit(solution)/shard_map/ppermute | solution.py:575
  (66 other events, 661.3 us)
